TPU v7x, 32 devices: a whole 2x2x4 slice. The times are simulated.
32 devices in a mesh: dp: 16 (over z, x, core), head: 2 (over y).
Axes of the slice: x: 2, y: 2, z: 4, core: 2. Of those that a mesh axis runs over, the one named last changes fastest.
Arguments:
- tokens: bfloat16 [16384, 768], P('dp'), may hold values from -6 to 6
- boxes: int32 [4, 16384], P(None, 'dp'), may hold values from 0 to 611
- resolution: int32 [32], P('dp'), may hold values from 0 to 3
- w_query: bfloat16 [768, 768], P(None, 'head'), may hold values from -0.21875 to 0.21875
- bias_query: bfloat16 [768], P('head'), may hold values from -3 to 3
- w_key: bfloat16 [768, 768], P(None, 'head'), may hold values from -0.21875 to 0.21875
- w_value: bfloat16 [768, 768], P(None, 'head'), may hold values from -0.21875 to 0.21875
- bias_value: bfloat16 [768], P('head'), may hold values from -3 to 3
- w_box: bfloat16 [768, 768], P(None, 'head'), may hold values from -0.21875 to 0.21875
- w_out: bfloat16 [768, 768], P('head'), may hold values from -1.25 to 1.25
- bias_out: bfloat16 [768], replicated, may hold values from -3 to 3
- norm1_gain: bfloat16 [768], replicated, may hold values from 0.25 to 1.75
- norm1_bias: bfloat16 [768], replicated, may hold values from -2 to 2
- w_in: bfloat16 [768, 3072], P(None, 'head'), may hold values from -0.21875 to 0.21875
- bias_in: bfloat16 [3072], P('head'), may hold values from -3 to 3
- w_back: bfloat16 [3072, 768], P('head'), may hold values from -0.109375 to 0.109375
- bias_back: bfloat16 [768], replicated, may hold values from -3 to 3
- norm2_gain: bfloat16 [768], replicated, may hold values from 0.25 to 1.75
- norm2_bias: bfloat16 [768], replicated, may hold values from -2 to 2
- grad_out: bfloat16 [16384, 768], P('dp'), may hold values from -18 to 18
Outputs:
- output: bfloat16 [16384, 768], P('dp')
- grad_input: float32 [16384, 768], P('dp')
- grad_w_query: float32 [768, 768], P('dp', 'head')
- grad_bias_query: float32 [768], P('head')
- grad_w_key: float32 [768, 768], P('dp', 'head')
- grad_w_value: float32 [768, 768], P('dp', 'head')
- grad_bias_value: float32 [768], P('head')
- grad_w_box: float32 [768, 768], P('dp', 'head')
- grad_w_out: float32 [768, 768], P('head', 'dp')
- grad_bias_out: float32 [768], replicated
- grad_norm1_gain: float32 [768], replicated
- grad_norm1_bias: float32 [768], replicated
- grad_w_in: float32 [768, 3072], P('dp', 'head')
- grad_bias_in: float32 [3072], P('head')
- grad_w_back: float32 [3072, 768], P('head', 'dp')
- grad_bias_back: float32 [768], replicated
- grad_norm2_gain: float32 [768], replicated
- grad_norm2_bias: float32 [768], replicated
All inputs are finite; a program needn't handle non-finite values.
Results may differ from a plain program's by a relative error of at most 0.02.
Values may be sent and summed in bfloat16 or wider, within the bound.
No kernel may reach another device: no remote copies, remote signals or barrier semaphores. Data moves between devices by JAX's collectives and lax.ppermute only.
A program may use at most 192 MiB of HBM per device.

v0:
```python
from functools import partial
import math

import jax
import numpy as np
import jax.numpy as jnp
from jax import lax
from jax.experimental import pallas as pl
from jax.experimental.pallas import tpu as pltpu
from jax.sharding import PartitionSpec as P

HEAD = 64
F32 = jnp.float32
BF16 = jnp.bfloat16
VMEM_LIMIT = 63 * 1024 * 1024


def hbm(shape, dtype):
    return pltpu.HBM(tuple(shape), dtype)


def mm(a, b):
    return jnp.dot(a, b, preferred_element_type=F32)


def mm_nt(a, b):
    return lax.dot_general(a, b, (((1,), (1,)), ((), ())), preferred_element_type=F32)


def params(steps):
    return pltpu.CompilerParams(
        dimension_semantics=("arbitrary",) * steps, vmem_limit_bytes=VMEM_LIMIT
    )


def cost(flops, nbytes, trans=0):
    return pl.CostEstimate(flops=int(flops), bytes_accessed=int(nbytes), transcendentals=int(trans))


def sin_cos(angle):
    turns = jnp.floor(angle * (2.0 / math.pi) + 0.5)
    r = angle - turns * 1.5703125
    r = r - turns * 4.837512969970703125e-4
    r = r - turns * 7.54978995489188216e-8
    r2 = r * r
    s = r + r * r2 * (
        -1.6666654611e-1 + r2 * (8.3321608736e-3 + r2 * -1.9515295891e-4)
    )
    c = 1.0 - 0.5 * r2 + r2 * r2 * (
        4.166664568298827e-2 + r2 * (-1.388731625493765e-3 + r2 * 2.443315711809948e-5)
    )
    quad = turns.astype(jnp.int32)
    odd = (quad & 1) == 1
    sine = jnp.where(odd, c, s)
    cosine = jnp.where(odd, s, c)
    sine = jnp.where((quad & 2) == 2, -sine, sine)
    cosine = jnp.where(((quad + 1) & 2) == 2, -cosine, cosine)
    return sine, cosine


def lane_mask(shape, which):
    lanes = lax.broadcasted_iota(jnp.int32, shape, 1)
    return (lanes < HEAD) if which == 0 else (lanes >= HEAD)


def row_mask(shape, which):
    rows = lax.broadcasted_iota(jnp.int32, shape, 0)
    return (rows < HEAD) if which == 0 else (rows >= HEAD)


def keep(mask, x):
    return jnp.where(mask, x, jnp.zeros_like(x))


def attn_fwd_kernel(
    groups, which_page, pick, res, tok_ref, box_ref, freq_ref, wq_ref, wk_ref, wv_ref, bq_ref, bv_ref, wbt_ref, wo_ref,
    part_ref, p_ref, q_ref, k_ref, v_ref, ctx_ref, s_ref, c_ref, tok_t_ref, codes, mixed, acc, biases,
):
    step = pl.program_id(0)
    half = s_ref.shape[1]

    @pl.when(step == 0)
    def _():
        rows = s_ref.shape[0]
        lanes = lax.broadcasted_iota(jnp.int32, (rows, half), 1)
        level = res[pick[which_page]]
        width = (612 + 204 * level).astype(F32)
        height = (792 + 264 * level).astype(F32)
        corners = box_ref[...]
        centre_x = (corners[0:1] + corners[2:3]).astype(F32) * 500.0 / width
        centre_y = (corners[1:2] + corners[3:4]).astype(F32) * 500.0 / height
        both = jnp.concatenate([centre_x, centre_y, jnp.zeros((6, rows), F32)], axis=0).T
        centre = jnp.where(lanes < half // 2, both[:, 0:1], both[:, 1:2])
        sine, cosine = sin_cos(centre * freq_ref[...])
        s_ref[...] = sine
        c_ref[...] = cosine
        codes[:, :half] = cosine.astype(BF16)
        codes[:, half : 2 * half] = sine.astype(BF16)
        acc[...] = jnp.zeros_like(acc)
        biases[0:1] = bq_ref[...].astype(F32).reshape(1, -1)
        biases[1:2] = bv_ref[...].astype(F32).reshape(1, -1)
        tok_t = split_rows(tok_ref[...].T, groups)
        tok_t_ref[0] = tok_t[:half]
        tok_t_ref[1] = tok_t[half:]

    tok = tok_ref[...]
    rows = tok.shape[0]
    wide = wq_ref.shape[1]
    span = pl.ds(pl.multiple_of(step * wide, wide), wide)
    qkv = mm(tok, jnp.concatenate([wq_ref[...], wk_ref[...], wv_ref[...]], axis=1))
    q2 = (qkv[:, :wide] + biases[0:1, span]).astype(BF16) * BF16(0.125)
    k2 = qkv[:, wide : 2 * wide].astype(BF16)
    v2 = (qkv[:, 2 * wide :] + biases[1:2, span]).astype(BF16)
    q_ref[...] = q2
    k_ref[...] = k2
    v_ref[...] = v2
    codes[:, 2 * half :] = k2
    sine, cosine = s_ref[...], c_ref[...]
    for which in range(2):
        span = slice(which * rows, (which + 1) * rows)
        qm = keep(lane_mask(q2.shape, which), q2)
        off = mm(qm, wbt_ref[...])
        a, b = off[:, :half], off[:, half:]
        mixed[span, :half] = (a * sine + b * cosine).astype(BF16)
        mixed[span, half : 2 * half] = (b * sine - a * cosine).astype(BF16)
        mixed[span, 2 * half :] = qm
    parts = []
    for which in range(2):
        span = slice(which * rows, (which + 1) * rows)
        scores = mm_nt(mixed[span], codes[...])
        top = jnp.max(scores, axis=1, keepdims=True)
        raised = jnp.exp(scores - top)
        total = jnp.sum(raised, axis=1, keepdims=True)
        prob = (raised * (1.0 / total)).astype(BF16)
        p_ref[which] = prob
        parts.append(mm(prob, v2))
    ctx2 = jnp.where(lane_mask(parts[0].shape, 0), parts[0], parts[1]).astype(BF16)
    ctx_ref[...] = ctx2
    acc[...] += mm(ctx2, wo_ref[...])

    @pl.when(step == pl.num_programs(0) - 1)
    def _():
        part_ref[...] = acc[...].astype(BF16)


def attn_fwd(which_page, pick, res, tokens, boxes, freq, wq, wk, wv, bq, bv, wbt, wo, length, groups):
    dim = tokens.shape[1]
    inner = wq.shape[1]
    heads = inner // HEAD
    pairs = heads // 2
    wide = 2 * HEAD
    page = lambda i, pick, res: (pick[which_page], 0)
    fixed = lambda i, pick, res: (0, 0)
    cols = lambda i, pick, res: (0, i)
    rows = lambda i, pick, res: (i, 0)
    flops = 2 * length * (dim * inner * 4 + heads * (HEAD * dim + length * (dim + 2 * HEAD)))
    return pl.pallas_call(
        partial(attn_fwd_kernel, groups, which_page),
        grid_spec=pltpu.PrefetchScalarGridSpec(
            num_scalar_prefetch=2,
            grid=(pairs,),
            in_specs=[
                pl.BlockSpec((length, dim), page),
                pl.BlockSpec((4, length), lambda i, pick, res: (0, pick[which_page])),
                pl.BlockSpec((1, dim // 2), fixed),
                pl.BlockSpec((dim, wide), cols),
                pl.BlockSpec((dim, wide), cols),
                pl.BlockSpec((dim, wide), cols),
                pl.BlockSpec((inner,), lambda i, pick, res: (0,)),
                pl.BlockSpec((inner,), lambda i, pick, res: (0,)),
                pl.BlockSpec((wide, dim), rows),
                pl.BlockSpec((wide, dim), rows),
            ],
            out_specs=[
                pl.BlockSpec((length, dim), fixed),
                pl.BlockSpec((2, length, length), lambda i, pick, res: (i, 0, 0)),
                pl.BlockSpec((length, wide), cols),
                pl.BlockSpec((length, wide), cols),
                pl.BlockSpec((length, wide), cols),
                pl.BlockSpec((length, wide), cols),
                pl.BlockSpec((length, dim // 2), fixed),
                pl.BlockSpec((length, dim // 2), fixed),
                pl.BlockSpec((2, dim // 2, length), lambda i, pick, res: (0, 0, 0)),
            ],
            scratch_shapes=[
                pltpu.VMEM((length, dim + wide), BF16),
                pltpu.VMEM((2 * length, dim + wide), BF16),
                pltpu.VMEM((length, dim), F32),
                pltpu.VMEM((8, inner), F32),
            ],
        ),
        out_shape=[
            hbm((length, dim), BF16),
            hbm((heads, length, length), BF16),
            hbm((length, inner), BF16),
            hbm((length, inner), BF16),
            hbm((length, inner), BF16),
            hbm((length, inner), BF16),
            hbm((length, dim // 2), F32),
            hbm((length, dim // 2), F32),
            hbm((2, dim // 2, length), BF16),
        ],
        compiler_params=params(1),
        cost_estimate=cost(flops, 10e6, heads * length * length),
        name="attn_fwd",
    )(pick, res, tokens, boxes, freq, wq, wk, wv, bq, bv, wbt, wo)


def attn_bwd_kernel(groups, box_groups, first, pick, *refs):
    (df_ref, tok_t_ref, ctx_ref, wo_ref, q_ref, k_ref, v_ref, p_ref, s_ref, c_ref, wbt_ref,
     wq_ref, wk_ref, wv_ref, *refs) = refs
    if first:
        part_ref, small_ref, inp_ref, codes, acc, df_t = refs
    else:
        prev_ref, prev_small_ref, extra_ref, *refs = refs
        sent_ref, kept_ref, small_ref, inp_ref, codes, acc, df_t, grads = refs
    step = pl.program_id(0)
    half = s_ref.shape[1]

    @pl.when(step == 0)
    def _():
        codes[:, :half] = c_ref[...].astype(BF16)
        codes[:, half:] = s_ref[...].astype(BF16)
        acc[...] = jnp.zeros_like(acc)
        turned = split_rows(df_ref[...].T, groups)
        df_t[0] = turned[:half]
        df_t[1] = turned[half:]

    sine, cosine = s_ref[...], c_ref[...]
    q2, k2, v2 = q_ref[...], k_ref[...], v_ref[...]
    dctx = mm_nt(df_ref[...], wo_ref[...]).astype(BF16)
    dctx_t = dctx.T
    q_t = q2.T
    wbt = wbt_ref[...]
    dq = jnp.zeros(q2.shape, F32)
    dk_t, dv_t, dwb = [], [], []
    for which in range(2):
        low, high = which * HEAD, (which + 1) * HEAD
        dm = keep(lane_mask(dctx.shape, which), dctx)
        prob = p_ref[which]
        grad_probs = mm_nt(dm, v2)
        dv_t.append(mm(dctx_t[low:high], prob))
        wide_prob = prob.astype(F32)
        both = wide_prob * grad_probs
        inner = jnp.sum(both, axis=1, keepdims=True)
        ds = (both - wide_prob * inner).astype(BF16)
        dk_t.append(mm(q_t[low:high], ds))
        km = keep(lane_mask(k2.shape, which), k2)
        ga = mm(ds, codes[:, :half]).astype(BF16).astype(F32)
        gb = mm(ds, codes[:, half:]).astype(BF16).astype(F32)
        oa = (ga * sine - gb * cosine).astype(BF16)
        ob = (gb * sine + ga * cosine).astype(BF16)
        wm = keep(row_mask(wbt.shape, which), wbt)
        dq = dq + (mm(ds, km) + mm_nt(oa, wm[:, :half]) + mm_nt(ob, wm[:, half:]))
        dwb.append(jnp.concatenate([mm(q_t[low:high], oa), mm(q_t[low:high], ob)], axis=1))
    dq2 = (dq * 0.125).astype(BF16)
    dk2 = jnp.concatenate(dk_t, axis=0).T.astype(BF16)
    dv2 = jnp.concatenate(dv_t, axis=0).T.astype(BF16)
    sides = jnp.concatenate([dq2, dk2, dv2], axis=1)
    acc[...] += mm_nt(sides, jnp.concatenate([wq_ref[...], wk_ref[...], wv_ref[...]], axis=1))

    box = split_rows(jnp.concatenate(dwb, axis=0).T, box_groups)
    ctx2 = ctx_ref[...]
    zeros = jnp.zeros((1, 3 * q2.shape[1]), F32)
    small = jnp.concatenate(
        [column_sum(dq2.astype(F32)), column_sum(dv2.astype(F32)), zeros], axis=1
    )
    if not first:
        small = small + prev_small_ref[...]
    small_ref[...] = small
    for h in range(2):
        grad = jnp.concatenate(
            [mm(tok_t_ref[h], sides), mm(df_t[h], ctx2), box[h * half : (h + 1) * half]], axis=1
        )
        if first:
            part_ref[h] = grad.astype(BF16)
        else:
            grads[h] = (grad + prev_ref[h].astype(F32)).astype(BF16)
    if not first:
        sent_ref[:half] = grads[pick[3]]
        sent_ref[half:] = wide_tail(small)
        kept_ref[...] = grads[pick[2]]

    @pl.when(step == pl.num_programs(0) - 1)
    def _():
        rows = acc.shape[0]
        inp_ref[:rows] = acc[...].astype(BF16)
        if not first:
            inp_ref[rows:] = extra_ref[...]


def attn_bwd(pick, df, saved, wo, wbt, wq, wk, wv, groups, box_groups, prev=None, extra=None):
    prob, q, k, v, ctx, sine, cosine, tok_t = saved
    length, dim = df.shape
    inner = wq.shape[1]
    heads = inner // HEAD
    pairs = heads // 2
    wide = 2 * HEAD
    first = prev is None
    sent = length if first else 2 * length
    fixed = lambda i, pick: (0, 0)
    cols = lambda i, pick: (0, i)
    rows = lambda i, pick: (i, 0)
    block = lambda i, pick: (0, 0, i)
    flops = 2 * length * (dim * inner * 8 + heads * (3 * HEAD * dim + length * (dim + 4 * HEAD)))
    part = pl.BlockSpec((2, dim // 2, 5 * wide), block)
    small = pl.BlockSpec((1, 5 * wide), cols)
    small_shape = hbm((1, 5 * inner), F32)
    inp = pl.BlockSpec((sent, dim), fixed)
    inp_shape = hbm((sent, dim), BF16)
    scratch = [
        pltpu.VMEM((length, dim), BF16),
        pltpu.VMEM((length, dim), F32),
        pltpu.VMEM((2, dim // 2, length), BF16),
    ]
    if first:
        out_specs = [part, small, inp]
        out_shape = [hbm((2, dim // 2, 5 * inner), BF16), small_shape, inp_shape]
        more_specs, more = [], []
    else:
        out_specs = [
            pl.BlockSpec((dim // 2 + TAIL, 5 * wide), cols), pl.BlockSpec((dim // 2, 5 * wide), cols), small, inp,
        ]
        out_shape = [
            hbm((dim // 2 + TAIL, 5 * inner), BF16), hbm((dim // 2, 5 * inner), BF16), small_shape, inp_shape,
        ]
        more_specs, more = [part, small, pl.BlockSpec((length, dim), fixed)], [*prev, extra]
        scratch.append(pltpu.VMEM((2, dim // 2, 5 * wide), BF16))
    return pl.pallas_call(
        partial(attn_bwd_kernel, groups, box_groups, first),
        grid_spec=pltpu.PrefetchScalarGridSpec(
            num_scalar_prefetch=1,
            grid=(pairs,),
            in_specs=[
                pl.BlockSpec((length, dim), fixed),
                pl.BlockSpec((2, dim // 2, length), lambda i, pick: (0, 0, 0)),
                pl.BlockSpec((length, wide), cols),
                pl.BlockSpec((wide, dim), rows),
                pl.BlockSpec((length, wide), cols),
                pl.BlockSpec((length, wide), cols),
                pl.BlockSpec((length, wide), cols),
                pl.BlockSpec((2, length, length), lambda i, pick: (i, 0, 0)),
                pl.BlockSpec((length, dim // 2), fixed),
                pl.BlockSpec((length, dim // 2), fixed),
                pl.BlockSpec((wide, dim), rows),
                pl.BlockSpec((dim, wide), cols),
                pl.BlockSpec((dim, wide), cols),
                pl.BlockSpec((dim, wide), cols),
            ]
            + more_specs,
            out_specs=out_specs,
            scratch_shapes=scratch,
        ),
        out_shape=out_shape,
        compiler_params=params(1),
        cost_estimate=cost(flops, 14e6),
        name="attn_bwd",
    )(pick, df, tok_t, ctx, wo, q, k, v, prob, sine, cosine, wbt, wq, wk, wv, *more)


def split_rows(x_t, groups):
    return jnp.concatenate([x_t[start : start + count] for start, count in groups], axis=0)


def shard_groups(dim, shards):
    rows = dim // shards
    if not fast_path(dim, shards):
        return [(0, dim)]
    order = [z * 4 + x * 2 + c for c in range(2) for z in range(shards // 4) for x in range(2)]
    return [(block * rows, rows) for block in order]


def fast_path(dim, shards):
    return shards == 16 and (dim // shards) % 16 == 0


def gelu_parts(v):
    e = jnp.exp(v * v * -0.5)
    t = 1.0 / (1.0 + (0.3275911 * math.sqrt(0.5)) * jnp.abs(v))
    poly = t * (
        0.5 * 0.254829592
        + t * (0.5 * -0.284496736 + t * (0.5 * 1.421413741 + t * (0.5 * -1.453152027 + t * (0.5 * 1.061405429))))
    )
    tail = poly * e
    phi = jnp.where(v >= 0, 1.0 - tail, tail)
    return phi, phi + v * (e * (1.0 / math.sqrt(2.0 * math.pi)))


def norm_stats(hidden):
    centred = hidden - jnp.mean(hidden, axis=1, keepdims=True)
    variance = jnp.mean(centred * centred, axis=1, keepdims=True)
    inv = lax.rsqrt(variance + 1e-05)
    return centred * inv, inv


def norm_back(grad, scaled, inv):
    return inv * (
        grad
        - jnp.mean(grad, axis=1, keepdims=True)
        - scaled * jnp.mean(grad * scaled, axis=1, keepdims=True)
    )


def column_sum(x):
    return jnp.sum(x, axis=0, keepdims=True)


def ff_kernel(
    groups, pick, tok_ref, part_ref, got_ref, gout_ref, bo_ref, g1_ref, b1_ref, bb_ref, g2_ref, b2_ref,
    bi_here, bi_there,
    wi_here, wb_here, wi0, wi1, wi2, wi3, wb0, wb1, wb2, wb3,
    out_ref, df_ref, lhs_ref, rhs_ref, small_ref,
    wi, wb, slope, norm_low, grad_low, acc, wide, bi_ref, sems,
):
    blocks, dim, cols = wi.shape
    here = blocks // 2
    piece = cols // 2
    remote = [(wi0, wb0), (wi1, wb1), (wi2, wb2), (wi3, wb3)]
    for p in range(2 * blocks):
        if p < blocks:
            at = (p % 2) * piece
            span = pl.ds(at, piece)
            source = (wi_here.at[:, pl.ds(p * piece, piece)], wb_here.at[pl.ds(p * piece, piece), :])
        else:
            span = pl.ds(pl.multiple_of(((pick[6] ^ p) & 1) * piece, piece), piece)
            source = remote[p - blocks]
            slot = here + ((((pick[8] ^ p) & 3) >> 1) ^ pick[7])
            span_back = pl.ds(pl.multiple_of(((pick[8] ^ p) & 1) * piece, piece), piece)
        pltpu.make_async_copy(source[0], wi.at[p // 2, :, span], sems.at[0, p]).start()
        if p < blocks:
            pltpu.make_async_copy(source[1], wb.at[p // 2, span, :], sems.at[1, p // 2]).start()
        else:
            pltpu.make_async_copy(source[1], wb.at[slot, span_back, :], sems.at[1, slot]).start()

    def vec(ref):
        return ref[...].astype(F32).reshape(1, -1)

    here_at, there_at = pick[0] * here, pick[1] * here
    bias_here, bias_there = vec(bi_here), vec(bi_there)
    for j in range(here):
        bi_ref[pl.ds(here_at + j, 1), :] = bias_here[:, j * cols : (j + 1) * cols]
        bi_ref[pl.ds(there_at + j, 1), :] = bias_there[:, j * cols : (j + 1) * cols]

    def place(j):
        return jnp.where(j < here, here_at + j, there_at + (pick[7] ^ (j - here)))

    bo, g1, b1, bb, g2, b2 = (vec(r) for r in (bo_ref, g1_ref, b1_ref, bb_ref, g2_ref, b2_ref))
    first_sum = (
        tok_ref[...].astype(F32)
        + (part_ref[...].astype(F32) + got_ref[...].astype(F32))
        + bo
    )
    scaled1, inv1 = norm_stats(first_sum)
    normed = scaled1 * g1 + b1
    low = normed.astype(BF16)
    norm_low[...] = low
    wide[...] = normed + bb
    acc[...] = jnp.zeros_like(acc)
    low_t = split_rows(low.T, groups)
    split = low_t.shape[0] // 2
    lhs_ref[0, 0] = low_t[:split]
    lhs_ref[1, 0] = low_t[split:]

    def forward(j, _):
        for p in range(2):
            pltpu.make_async_copy(wi0, wi.at[j, :, pl.ds(0, piece)], sems.at[0, 2 * j + p]).wait()
        pltpu.make_async_copy(wb.at[j], wb.at[j], sems.at[1, j]).wait()
        pre = mm(norm_low[...], wi[j]) + bi_ref[pl.ds(place(j), 1), :]
        phi, step = gelu_parts(pre)
        act = (pre * phi).astype(BF16)
        rhs_ref[1, j] = act
        slope[j] = step
        acc[...] += mm(act, wb[j])
        return 0

    lax.fori_loop(0, blocks, forward, 0)
    scaled2, inv2 = norm_stats(wide[...] + acc[...])
    out_ref[...] = (scaled2 * g2 + b2).astype(BF16)
    gout = gout_ref[...].astype(F32)
    small_gain2 = column_sum(gout * scaled2)
    small_bias2 = column_sum(gout)
    grad_second = norm_back(gout * g2, scaled2, inv2)
    small_back = column_sum(grad_second)
    low2 = grad_second.astype(BF16)
    grad_low[...] = low2
    low2_t = split_rows(low2.T, groups)
    lhs_ref[0, 1] = low2_t[:split]
    lhs_ref[1, 1] = low2_t[split:]
    acc[...] = grad_second

    def backward(j, _):
        grad_act = mm_nt(grad_low[...], wb[j]).astype(BF16).astype(F32)
        grad_pre = (grad_act * slope[j]).astype(BF16)
        rhs_ref[0, j] = grad_pre
        bi_ref[pl.ds(place(j), 1), :] = column_sum(grad_pre.astype(F32))
        acc[...] += mm_nt(grad_pre, wi[j])
        return 0

    lax.fori_loop(0, blocks, backward, 0)
    grad_normed = acc[...]
    first_sum = (
        tok_ref[...].astype(F32)
        + (part_ref[...].astype(F32) + got_ref[...].astype(F32))
        + bo
    )
    scaled1, inv1 = norm_stats(first_sum)
    small_gain1 = column_sum(grad_normed * scaled1)
    small_bias1 = column_sum(grad_normed)
    grad_first = norm_back(grad_normed * g1, scaled1, inv1)
    small_out = column_sum(grad_first)
    df_ref[...] = grad_first.astype(BF16)
    small_ref[...] = jnp.concatenate(
        [
            jnp.concatenate([small_gain2, small_bias2], axis=1),
            jnp.concatenate([small_back, small_gain1], axis=1),
            jnp.concatenate([small_bias1, small_out], axis=1),
            jnp.concatenate([bi_ref[j : j + 1] for j in range(here)], axis=1),
            jnp.concatenate([bi_ref[j : j + 1] for j in range(here, blocks)], axis=1),
            jnp.zeros((3, 2 * dim), F32),
        ],
        axis=0,
    )


def feed_forward(pick, tokens, part, got, grad_out, rows, bias_in, bias_there, wi_here, wb_here, wi_pieces, wb_pieces, groups):
    length, dim = part.shape
    cols = 2 * wi_pieces[0].shape[1]
    blocks = 2 * wi_here.shape[1] // cols
    page = lambda i, pick: (pick[0], 0)
    fixed = lambda i, pick: (0, 0)
    row = pl.BlockSpec((dim,), lambda i, pick: (0,))
    bias_row = pl.BlockSpec(bias_in.shape, lambda i, pick: (0,))
    whole = pl.BlockSpec((length, dim), fixed)
    anywhere = pl.BlockSpec(memory_space=pl.ANY)
    hidden = blocks * cols
    return pl.pallas_call(
        partial(ff_kernel, groups),
        grid_spec=pltpu.PrefetchScalarGridSpec(
            num_scalar_prefetch=1,
            grid=(1,),
            in_specs=[
                pl.BlockSpec((length, dim), page),
                whole,
                whole,
                pl.BlockSpec((length, dim), page),
                row, row, row, row, row, row,
                bias_row, bias_row,
            ]
            + [anywhere] * 10,
            out_specs=[
                whole,
                whole,
                pl.BlockSpec((2, 2, dim // 2, length), lambda i, pick: (0, 0, 0, 0)),
                pl.BlockSpec((2, blocks, length, cols), lambda i, pick: (0, 0, 0, 0)),
                pl.BlockSpec((8, 2 * dim), fixed),
            ],
            scratch_shapes=[
                pltpu.VMEM((blocks, dim, cols), BF16),
                pltpu.VMEM((blocks, cols, dim), BF16),
                pltpu.VMEM((blocks, length, cols), F32),
                pltpu.VMEM((length, dim), BF16),
                pltpu.VMEM((length, dim), BF16),
                pltpu.VMEM((length, dim), F32),
                pltpu.VMEM((length, dim), F32),
                pltpu.VMEM((blocks, cols), F32),
                pltpu.SemaphoreType.DMA((2, 2 * blocks)),
            ],
        ),
        out_shape=[
            hbm((length, dim), BF16),
            hbm((length, dim), BF16),
            hbm((2, 2, dim // 2, length), BF16),
            hbm((2, blocks, length, cols), BF16),
            hbm((8, 2 * dim), F32),
        ],
        compiler_params=params(1),
        cost_estimate=cost(8 * length * dim * hidden, 4 * dim * hidden + 8 * length * hidden, length * hidden),
        name="feed_forward",
    )(pick, tokens, part, got, grad_out, *rows, bias_in, bias_there, wi_here, wb_here, *wi_pieces, *wb_pieces)


TAIL = 16


def split2(x):
    high = x.astype(BF16)
    return high, (x - high.astype(F32)).astype(BF16)


def rounded(x):
    high, low = split2(x)
    return high.astype(F32) + low.astype(F32)


def tall(x):
    return jnp.concatenate([x, jnp.zeros((TAIL - x.shape[0],) + x.shape[1:], x.dtype)], axis=0)


def ff_send_kernel(pick, lhs_ref, rhs_ref, small_ref, out_ref):
    rows = lhs_ref.shape[2]
    for m in range(2):
        out_ref[m, :rows] = mm(lhs_ref[0, m], rhs_ref[m, 0]).astype(BF16)
    for m, term in enumerate(split2(small_ref[...])):
        out_ref[m, rows:] = tall(term)


def ff_keep_kernel(pick, lhs_ref, rhs_ref, got_ref, small_ref, xs_ref, xk_ref, small_out, acc):
    rows = lhs_ref.shape[2]
    shard = acc.shape[0] // 8
    x_index = pick[4]
    for m in range(2):
        acc[...] = mm(lhs_ref[0, m], rhs_ref[m, 0]) + got_ref[m, :rows].astype(F32)
        for z in range(4):
            away = pl.multiple_of((2 * z + 1 - x_index) * shard, 8)
            mine = pl.multiple_of((2 * z + x_index) * shard, 8)
            xs_ref[m, z * shard : (z + 1) * shard] = acc[pl.ds(away, shard), :].astype(BF16)
            xk_ref[m, z * shard : (z + 1) * shard] = acc[pl.ds(mine, shard), :].astype(BF16)
    small = rounded(small_ref[...]) + (got_ref[0, rows : rows + 8].astype(F32) + got_ref[1, rows : rows + 8].astype(F32))
    small_out[...] = small
    for m, term in enumerate(split2(small)):
        xs_ref[m, 4 * shard :] = tall(term)


def ff_grad(pick, lhs, rhs, small, remote, got=None):
    _, mats, rows, length = lhs.shape
    _, blocks, _, cols = rhs.shape
    half = blocks // 2
    base = half if remote else 0
    which = 2 if got is not None else 3
    dest = (lambda j, pick: j ^ pick[7]) if remote else (lambda j, pick: j)
    column = lambda height: pl.BlockSpec((2, height, cols), lambda j, pick: (0, 0, dest(j, pick)))
    small_spec = pl.BlockSpec((8, cols), lambda j, pick: (0, dest(j, pick)))
    in_specs = [
        pl.BlockSpec((1, mats, rows, length), lambda j, pick: (pick[which], 0, 0, 0)),
        pl.BlockSpec((2, 1, length, cols), lambda j, pick: (0, base + j, 0, 0)),
    ]
    wide = half * cols
    estimate = cost(2 * mats * rows * length * wide, 10e6)
    if got is None:
        return pl.pallas_call(
            ff_send_kernel,
            grid_spec=pltpu.PrefetchScalarGridSpec(
                num_scalar_prefetch=1,
                grid=(half,),
                in_specs=in_specs + [small_spec],
                out_specs=column(rows + TAIL),
            ),
            out_shape=hbm((2, rows + TAIL, wide), BF16),
            compiler_params=params(1),
            cost_estimate=estimate,
            name="ff_grad_send",
        )(pick, lhs, rhs, small)
    return pl.pallas_call(
        ff_keep_kernel,
        grid_spec=pltpu.PrefetchScalarGridSpec(
            num_scalar_prefetch=1,
            grid=(half,),
            in_specs=in_specs + [column(rows + TAIL), small_spec],
            out_specs=[column(rows // 2 + TAIL), column(rows // 2), small_spec],
            scratch_shapes=[pltpu.VMEM((rows, cols), F32)],
        ),
        out_shape=[
            hbm((2, rows // 2 + TAIL, wide), BF16),
            hbm((2, rows // 2, wide), BF16),
            hbm((8, wide), F32),
        ],
        compiler_params=params(1),
        cost_estimate=estimate,
        name="ff_grad_keep",
    )(pick, lhs, rhs, got, small)


def wide_tail(vector):
    high, low = split2(vector)
    return tall(jnp.concatenate([high, low], axis=0))


def attn_split_kernel(pick, kept_ref, got_ref, small_ref, xs_ref, xk_ref, small_out, acc):
    rows = kept_ref.shape[0]
    acc[...] = kept_ref[...].astype(F32) + got_ref[:rows].astype(F32)
    x_index = pick[4]
    shard = rows // 8
    for z in range(4):
        away = pl.multiple_of((2 * z + 1 - x_index) * shard, 8)
        mine = pl.multiple_of((2 * z + x_index) * shard, 8)
        xs_ref[0, z * shard : (z + 1) * shard] = acc[pl.ds(away, shard), :].astype(BF16)
        xk_ref[0, z * shard : (z + 1) * shard] = acc[pl.ds(mine, shard), :].astype(BF16)
    small = rounded(small_ref[...]) + (
        got_ref[rows : rows + 1].astype(F32) + got_ref[rows + 1 : rows + 2].astype(F32)
    )
    small_out[...] = jnp.concatenate([small, jnp.zeros((7, small.shape[1]), F32)], axis=0)
    xs_ref[0, 4 * shard :] = wide_tail(small)


def attn_split(pick, kept, got, small):
    rows, cols = kept.shape
    steps = 3
    column = lambda height: pl.BlockSpec((height, cols // steps), lambda i, pick: (0, i))
    deep = lambda height: pl.BlockSpec((1, height, cols // steps), lambda i, pick: (0, 0, i))
    return pl.pallas_call(
        attn_split_kernel,
        grid_spec=pltpu.PrefetchScalarGridSpec(
            num_scalar_prefetch=1,
            grid=(steps,),
            in_specs=[column(rows), column(rows + TAIL), column(1)],
            out_specs=[deep(rows // 2 + TAIL), deep(rows // 2), column(8)],
            scratch_shapes=[pltpu.VMEM((rows, cols // steps), F32)],
        ),
        out_shape=[
            hbm((1, rows // 2 + TAIL, cols), BF16),
            hbm((1, rows // 2, cols), BF16),
            hbm((8, cols), F32),
        ],
        compiler_params=params(1),
        cost_estimate=cost(kept.size, 6 * kept.size),
        name="attn_split",
    )(pick, kept, got, small)


def tail_sum(ref, at):
    if ref.shape[0] == 2:
        return ref[0, at : at + 8].astype(F32) + ref[1, at : at + 8].astype(F32)
    one = ref[0, at : at + 1].astype(F32) + ref[0, at + 1 : at + 2].astype(F32)
    return jnp.concatenate([one, jnp.zeros((7, one.shape[1]), F32)], axis=0)


def put_tail(ref, at, small):
    if ref.shape[0] == 2:
        for m, term in enumerate(split2(small)):
            ref[m, at:] = tall(term)
    else:
        ref[0, at:] = wide_tail(small[0:1])


def add_x_kernel(tailed, pick, keep_ref, got_ref, small_ref, own, s1, s2, s3, *rest):
    shard = own.shape[1]
    z = pick[5]
    if tailed:
        small = rounded(small_ref[...]) + tail_sum(got_ref, 4 * shard)
        rest[0][...] = small
    for d, ref in enumerate((own, s1, s2, s3)):
        at = pl.multiple_of((z ^ d) * shard, 16)
        ref[:, :shard] = (
            keep_ref[:, pl.ds(at, shard), :].astype(F32) + got_ref[:, pl.ds(at, shard), :].astype(F32)
        ).astype(BF16)
        if d and tailed:
            put_tail(ref, shard, small)


def add_x(pick, kept, got, small, tailed):
    mats, rows, cols = kept.shape
    shard = rows // 4
    own = hbm((mats, shard, cols), BF16)
    sent = hbm((mats, shard + (TAIL if tailed else 0), cols), BF16)
    full = lambda s: pl.BlockSpec(s.shape, lambda i, pick: (0,) * len(s.shape))
    extra = [hbm(small.shape, F32)] if tailed else []
    return pl.pallas_call(
        partial(add_x_kernel, tailed),
        grid_spec=pltpu.PrefetchScalarGridSpec(
            num_scalar_prefetch=1,
            grid=(1,),
            in_specs=[full(kept), full(got), full(small)],
            out_specs=[full(own)] + [full(sent)] * 3 + [full(s) for s in extra],
        ),
        out_shape=[own] + [sent] * 3 + extra,
        compiler_params=params(1),
        cost_estimate=cost(kept.size, 6 * kept.size),
        name="add_x",
    )(pick, kept, got, small)


def sum4(own, r1, r2, r3):
    return (own.astype(F32) + r1.astype(F32)) + (r2.astype(F32) + r3.astype(F32))


def small4(small_ref, others, at):
    terms = [tail_sum(r, at) for r in others]
    return (rounded(small_ref[...]) + terms[0]) + (terms[1] + terms[2])


def add_z_kernel(own, r1, r2, r3, small_ref, out, small_out):
    shard = own.shape[1]
    out[:, :shard] = sum4(own[...], r1[:, :shard], r2[:, :shard], r3[:, :shard]).astype(BF16)
    small = small4(small_ref, (r1, r2, r3), shard)
    small_out[...] = small
    put_tail(out, shard, small)


def add_z(blocks, small):
    return pl.pallas_call(
        add_z_kernel,
        out_shape=[
            hbm(blocks[1].shape, BF16),
            hbm(small.shape, F32),
        ],
        compiler_params=pltpu.CompilerParams(vmem_limit_bytes=VMEM_LIMIT),
        cost_estimate=cost(4 * blocks[0].size, 10 * blocks[0].size),
        name="add_z",
    )(*blocks, small)


def ff_last_kernel(pick, own, r1, r2, r3, got, small_ref, in_out, back_out, *vectors):
    small_out = vectors[-1]
    shard = own.shape[1]
    in_out[...] = sum4(own[0], r1[0], r2[0], r3[0]) + got[0, :shard].astype(F32)
    back_out[...] = sum4(own[1], r1[1, :shard], r2[1, :shard], r3[1, :shard]) + got[1, :shard].astype(F32)
    small = rounded(small_ref[...]) + tail_sum(got, shard)
    small_out[...] = small
    dim = small.shape[1] // 2
    for i in range(6):
        vectors[i][...] = small[i // 2 : i // 2 + 1, (i % 2) * dim : (i % 2 + 1) * dim].reshape(dim)
    vectors[6][...] = small_out[pl.ds(3 + pick[0], 1), :].reshape(2 * dim)


def ff_last(pick, blocks, got, small):
    _, rows, cols = blocks[0].shape
    dim = cols // 2
    full = lambda s: pl.BlockSpec(s.shape, lambda i, pick: (0,) * len(s.shape))
    out_shape = (
        [hbm((rows, cols), F32)] * 2
        + [hbm((dim,), F32)] * 6
        + [hbm((cols,), F32)]
    )
    return pl.pallas_call(
        ff_last_kernel,
        grid_spec=pltpu.PrefetchScalarGridSpec(
            num_scalar_prefetch=1,
            grid=(1,),
            in_specs=[full(b) for b in blocks] + [full(got), full(small)],
            out_specs=[full(s) for s in out_shape],
            scratch_shapes=[pltpu.VMEM(small.shape, F32)],
        ),
        out_shape=out_shape,
        compiler_params=params(1),
        cost_estimate=cost(10 * got.size, 20 * got.size),
        name="ff_last",
    )(pick, *blocks, got, small)


def attn_last_kernel(own, r1, r2, r3, small_ref, q_out, k_out, v_out, box_out, wo_out, bq_out, bv_out):
    shard = own.shape[1]
    wide = 2 * HEAD
    pairs = q_out.shape[1] // wide
    small = small4(small_ref, (r1, r2, r3), shard)
    for p in range(pairs):
        at = slice(p * wide, (p + 1) * wide)
        for i, ref in enumerate((q_out, k_out, v_out, wo_out, box_out)):
            span = slice((5 * p + i) * wide, (5 * p + i + 1) * wide)
            ref[:, at] = sum4(own[0, :, span], r1[0, :shard, span], r2[0, :shard, span], r3[0, :shard, span])
    for i, ref in enumerate((bq_out, bv_out)):
        row = [small[0:1, (5 * p + i) * wide : (5 * p + i + 1) * wide] for p in range(pairs)]
        ref[...] = jnp.concatenate(row, axis=1).reshape(pairs * wide)


def attn_last(blocks, small):
    _, rows, cols = blocks[0].shape
    cols = cols // 5
    flat = hbm((rows, cols), F32)
    vector = hbm((cols,), F32)
    return pl.pallas_call(
        attn_last_kernel,
        out_shape=[flat] * 5 + [vector, vector],
        compiler_params=pltpu.CompilerParams(vmem_limit_bytes=VMEM_LIMIT),
        cost_estimate=cost(4 * blocks[0].size, 12 * blocks[0].size),
        name="attn_last",
    )(*blocks, small)


def place_grad_kernel(pick, df_ref, a_ref, b_ref, *refs):
    refs[-1][...] = df_ref[...].astype(F32) + (a_ref[...].astype(F32) + b_ref[...].astype(F32))


def place_grad(which, pick, df, mine, got, pages, into=None):
    length, dim = df.shape
    steps = 2
    part = pl.BlockSpec((length // steps, dim), lambda i, pick: (i, 0))
    args = [df, mine, got] + ([] if into is None else [into])
    return pl.pallas_call(
        place_grad_kernel,
        grid_spec=pltpu.PrefetchScalarGridSpec(
            num_scalar_prefetch=1,
            grid=(steps,),
            in_specs=[part] * 3 + ([] if into is None else [pl.BlockSpec(memory_space=pl.ANY)]),
            out_specs=pl.BlockSpec((length // steps, dim), lambda i, pick: (pick[which] * steps + i, 0)),
        ),
        out_shape=hbm((pages * length, dim), F32),
        input_output_aliases={} if into is None else {4: 0},
        compiler_params=params(1),
        cost_estimate=cost(3 * df.size, 10 * df.size),
        name="place_grad",
    )(pick, *args)


def place_output_kernel(pick, a_ref, b_ref, out_ref):
    length = a_ref.shape[0]
    own = pl.multiple_of(pick[0] * length, length)
    other = pl.multiple_of(pick[1] * length, length)
    out_ref[pl.ds(own, length), :] = a_ref[...]
    out_ref[pl.ds(other, length), :] = b_ref[...]


def place_output(pick, mine, got):
    length, dim = mine.shape
    whole = pl.BlockSpec((length, dim), lambda i, pick: (0, 0))
    return pl.pallas_call(
        place_output_kernel,
        grid_spec=pltpu.PrefetchScalarGridSpec(
            num_scalar_prefetch=1,
            grid=(1,),
            in_specs=[whole, pl.BlockSpec((length, dim), lambda i, pick: (1, 0))],
            out_specs=pl.BlockSpec((2 * length, dim), lambda i, pick: (0, 0)),
        ),
        out_shape=hbm((2 * length, dim), BF16),
        compiler_params=params(1),
        cost_estimate=cost(mine.size, 8 * mine.size),
        name="place_output",
    )(pick, mine, got)


def swap_perm(size, flip):
    return [(i, i ^ flip) for i in range(size)]


def encoding_rows(w_box):
    rows, cols = w_box.shape
    quarters = w_box.reshape(4, rows // 4, cols)
    return jnp.concatenate([quarters[i] for i in (0, 2, 1, 3)], axis=0)


def encoding_groups(groups, dim):
    quarter = dim // 4
    place = (0, 2, 1, 3)
    out = []
    for start, count in groups:
        while count:
            size = min(count, quarter - start % quarter)
            out.append((place[start // quarter] * quarter + start % quarter, size))
            start, count = start + size, count - size
    return out


def shards(
    shards_dp,
    tokens,
    boxes,
    resolution,
    w_query,
    bias_query,
    w_key,
    w_value,
    bias_value,
    w_box,
    w_out,
    bias_out,
    norm1_gain,
    norm1_bias,
    w_in,
    bias_in,
    w_back,
    bias_back,
    norm2_gain,
    norm2_bias,
    grad_out,
):
    dim = tokens.shape[1]
    pages = resolution.shape[0]
    length = tokens.shape[0] // pages
    hidden = w_in.shape[1]
    piece = hidden // 4
    here = lax.axis_index("head").astype(jnp.int32)
    spot = lax.axis_index("dp").astype(jnp.int32)
    core, x_index, z_index, corner = spot % 2, (spot // 2) % 2, spot // 4, spot % 4
    corner_z = (z_index % 2) * 2 + core
    pick = jnp.stack([here, 1 - here, core, 1 - core, x_index, z_index, corner, corner // 2, corner_z])
    groups = shard_groups(dim, shards_dp)
    fast = fast_path(dim, shards_dp)

    def over_head(value):
        return lax.ppermute(value, "head", [(0, 1), (1, 0)])

    def over_dp(value, flip):
        return lax.ppermute(value, "dp", swap_perm(shards_dp, flip))

    def after(value, *others):
        return lax.optimization_barrier((value, others))[0]

    in_first = over_head(lax.dynamic_slice_in_dim(w_in, corner * piece, piece, 1))
    back_first = over_head(lax.dynamic_slice_in_dim(w_back, corner_z * piece, piece, 0))
    bias_there = over_head(bias_in)

    quarter = w_box.shape[0] // 4
    freqs = np.exp(np.arange(quarter, dtype=np.float32) * np.float32(-math.log(10000.0) / quarter))
    freqs = jnp.asarray(np.concatenate([freqs, freqs])[None, :])
    box_t = encoding_rows(w_box).T

    def attend(which, tok):
        return attn_fwd(
            which, pick, resolution, tok, boxes, freqs, w_query, w_key, w_value, bias_query, bias_value,
            box_t, w_out, length, groups,
        )

    part_other, *saved_other = attend(1, tokens)
    got = over_head(part_other)
    in_first, back_first = after((in_first, back_first), part_other)
    in_second, back_second = over_dp(in_first, 2), over_dp(back_first, 4)
    in_near, back_near = over_dp(in_first, 1), over_dp(back_first, 1)
    part_own, *saved_own = attend(0, after(tokens, part_other))
    in_second, back_second = after((in_second, back_second), part_own)
    in_pieces = [in_first, in_near, in_second, over_dp(in_second, 1)]
    back_pieces = [back_first, back_near, back_second, over_dp(back_second, 1)]

    out_own, df_own, lhs, rhs, small = feed_forward(
        pick, tokens, part_own, got, grad_out,
        (bias_out, norm1_gain, norm1_bias, bias_back, norm2_gain, norm2_bias),
        bias_in, bias_there, w_in, w_back, in_pieces, back_pieces, groups,
    )
    df_other = over_head(df_own)
    box_groups = encoding_groups(groups, w_box.shape[0])

    def attend_back(df, saved, prev=None, extra=None, pick=pick):
        return attn_bwd(
            pick, df, saved, w_out, box_t, w_query, w_key, w_value, groups, box_groups, prev, extra
        )

    if fast:
        sent_a = ff_grad(pick, lhs, rhs, small, True)
        got_a = over_dp(sent_a, 1)
        sent_b = ff_grad(pick, lhs, after(rhs, sent_a), small, False)
        got_b = over_dp(sent_b, 1)
        xs_a, xk_a, small_1 = ff_grad(pick, lhs, after(rhs, sent_b), small, True, got_a)
        xg_a = over_dp(xs_a, 2)
        got_b = after(got_b, xs_a)
        xs_b, xk_b, small_b = ff_grad(pick, lhs, after(rhs, xs_a), small, False, got_b)
        df_own = after(df_own, xs_b)
    *part_a, inp_own = attend_back(df_own, saved_own)
    inp_own_got = over_head(inp_own)

    if fast:
        xg_a, df_other, xs_b = after((xg_a, df_other, xs_b), inp_own)
        xg_b = over_dp(xs_b, 2)
        *z_a, small_2 = add_x(pick, xk_a, after(xg_a, df_other), small_1, True)
        zg_a = [z_a[0]] + [over_dp(z_a[d], 4 * d) for d in (1, 2, 3)]
        df_other = after(df_other, z_a[0])

    pick_back = pick if fast else pick.at[2:4].set(jnp.arange(2, dtype=jnp.int32))
    sent, kept, a_small, inp_other = attend_back(df_other, saved_other, part_a, out_own, pick_back)
    inp_other_got = over_head(inp_other)

    if fast:
        xg_b, zg_a, inp_own_got = after((xg_b, zg_a, inp_own_got), inp_other)
        sent, xk_b = after((sent, xk_b), xg_b, zg_a, inp_own_got)
        sent_got = over_dp(sent, 1)
        z_b = add_x(pick, xk_b, xg_b, small_b, False)
        a_sum, small_3 = add_z([after(zg_a[0], z_b[0])] + zg_a[1:], small_2)
        xs, xk, a_small = attn_split(pick, kept, after(sent_got, a_sum), a_small)
        xg = over_dp(xs, 2)
        z_b = after(z_b, xs)
        zg_b = [z_b[0]] + [over_dp(z_b[d], 4 * d) for d in (1, 2, 3)]
        grad_input = place_grad(1, pick, after(df_other, xs), inp_other, inp_own_got, pages)
        *blocks, a_small = add_x(pick, after(xk, grad_input), xg, a_small, True)
        zg_b = after(zg_b, blocks)
        blocks, a_sum, df_own = after((blocks, a_sum, df_own), zg_b)
        blocks = [blocks[0]] + [over_dp(blocks[d], 4 * d) for d in (1, 2, 3)]
        a_sum = over_head(a_sum)
        grad_input = place_grad(0, pick, df_own, inp_own, inp_other_got, pages, grad_input)
        grad_in, grad_back, n2g, n2b, bias_back_sum, n1g, n1b, bias_out_sum, bias_in_sum = ff_last(
            pick, after(zg_b, grad_input), a_sum, small_3
        )
        output = place_output(pick, after(out_own, grad_in), inp_other_got)
        blocks = after(blocks, output)
        grad_q, grad_k, grad_v, grad_box, grad_wo, bq_sum, bv_sum = attn_last(blocks, a_small)
        grad_back, grad_wo = grad_back.T, grad_wo.T
    else:
        scatter = lambda value, axis: lax.psum_scatter(
            value.astype(F32), "dp", scatter_dimension=axis, tiled=True
        )
        cores = [pick.at[3].set(c) for c in (0, 1)]
        halves = [
            scatter(
                jnp.concatenate([ff_grad(p, lhs, rhs, small, remote)[:, : dim // 2] for p in cores], axis=1), 1
            )
            for remote in (True, False)
        ]
        total = halves[1] + over_head(halves[0])
        grad_in, grad_back = total[0], total[1].T
        total = scatter(jnp.concatenate([kept, sent[: dim // 2]], axis=0), 0)
        total = total.reshape(total.shape[0], -1, 5, 2 * HEAD).transpose(2, 0, 1, 3)
        grad_q, grad_k, grad_v, grad_wo, grad_box = total.reshape(5, total.shape[1], -1)
        grad_wo = grad_wo.T
        small = lax.psum(small, ("dp", "head"))
        n2g, n2b, bias_back_sum, n1g, n1b, bias_out_sum = small[:3].reshape(6, dim)
        bias_in_sum = lax.dynamic_index_in_dim(small, 3 + here, 0, keepdims=False)
        bq_sum, bv_sum = lax.psum(a_small, "dp").reshape(-1, 5, 2 * HEAD)[:, :2].transpose(1, 0, 2).reshape(2, -1)
        output = place_output(pick, out_own, inp_other_got)
        grad_input = place_grad(1, pick, df_other, inp_other, inp_own_got, pages)
        grad_input = place_grad(0, pick, df_own, inp_own, inp_other_got, pages, grad_input)
    return (
        output,
        grad_input,
        grad_q,
        bq_sum,
        grad_k,
        grad_v,
        bv_sum,
        grad_box,
        grad_wo,
        bias_out_sum,
        n1g,
        n1b,
        grad_in,
        bias_in_sum,
        grad_back,
        bias_back_sum,
        n2g,
        n2b,
    )


def solution(mesh):
    placed = (
        P("dp", None),
        P(None, "dp"),
        P("dp"),
        P(None, "head"),
        P("head"),
        P(None, "head"),
        P(None, "head"),
        P("head"),
        P(None, "head"),
        P("head", None),
        P(),
        P(),
        P(),
        P(None, "head"),
        P("head"),
        P("head", None),
        P(),
        P(),
        P(),
        P("dp", None),
    )
    return jax.shard_map(
        partial(shards, mesh.shape["dp"]),
        mesh=mesh,
        in_specs=placed,
        out_specs=(
            P("dp", None),
            P("dp", None),
            P("dp", "head"),
            P("head"),
            P("dp", "head"),
            P("dp", "head"),
            P("head"),
            P("dp", "head"),
            P("head", "dp"),
            P(),
            P(),
            P(),
            P("dp", "head"),
            P("head"),
            P("head", "dp"),
            P(),
            P(),
            P(),
        ),
        check_vma=False,
    )
```

profile of v0, /device:TPU:0, one launch (start us, length us, event | category | flops | bytes accessed | tf_op | source)
XLA Modules:
  0.0 239.3 jit_solution(6623224537784932132)
XLA Ops:
  1.9 3.0 %collective-permute-start.3 = (bf16[384,768]{1,0:T(8,128)(2,1)S(1)}, bf16[384,768]{1,0:T(8,128)(2,1)}, u32[]{:S(2)}, u32[]{:S(2)}) collective-permute-start(bf16[384,768]{1,0:T(8,128)(2,1)S(1)} %constant_dynamic-slice_fusion), channel_id=1, source_target_pairs={{0,1},{1,0},{2,3},{3,2},{4,5},{5,4},{6,7},{7,6},{8,9},{9,8},{10,11... | collective-permute-start | bytes 1769480 | tf_op jit(solution)/shard_map/ppermute | solution.py:979
  9.3 17.1 %attn_fwd.2 = (bf16[512,768]{1,0:T(8,128)(2,1)}, bf16[6,512,512]{2,1,0:T(8,128)(2,1)}, bf16[512,384]{1,0:T(8,128)(2,1)}, bf16[512,384]{1,0:T(8,128)(2,1)}, bf16[...) custom-call(s32[9]{0:T(128)} %stack.39.pick, ...), custom_call_target="tpu_custom_call" | custom-call | flops 4328521728 | bytes 10000000 | tf_op jit(solution)/shard_map/attn_fwd/pallas_call | solution.py:157
  26.5 4.5 %collective-permute-done.2.wi0 = bf16[768,384]{1,0:T(8,128)(2,1)} collective-permute-done((bf16[768,384]{1,0:T(8,128)(2,1)}, bf16[768,384]{1,0:T(8,128)(2,1)}, u32[]{:S(2)}, u32[]{:S(2)}) %collective-permute-start.2) | collective-permute-done | bytes 589856 | tf_op jit(solution)/shard_map/ppermute | solution.py:979
  36.3 17.0 %attn_fwd.3 = (bf16[512,768]{1,0:T(8,128)(2,1)}, bf16[6,512,512]{2,1,0:T(8,128)(2,1)}, bf16[512,384]{1,0:T(8,128)(2,1)}, bf16[512,384]{1,0:T(8,128)(2,1)}, bf16[...) custom-call(s32[9]{0:T(128)} %stack.39.pick, ...), custom_call_target="tpu_custom_call" | custom-call | flops 4328521728 | bytes 10000000 | tf_op jit(solution)/shard_map/attn_fwd/pallas_call | solution.py:157
  58.2 24.8 %feed_forward.1 = (bf16[512,768]{1,0:T(8,128)(2,1)}, bf16[512,768]{1,0:T(8,128)(2,1)}, bf16[2,2,384,512]{3,2,1,0:T(8,128)(2,1)}, bf16[2,4,512,768]{3,2,1,0:T(8,128)(2,1)}, f32[8,1536]{1,0:T(8,128)}) custom-call(s32[9]{0:T(128)} %stack.39.pick, bf16[1024,768]{1,0:T(8,128)(2,1)} %tok_ref.4, bf16[512,768]{1,0:T(8,128)(2,1)} %get-tuple-element.141.part_ref, ...), custom_call_target="tpu_custom_call" | custom-call | flops 9663676416 | bytes 22020096 | tf_op jit(solution)/shard_map/feed_forward/pallas_call | solution.py:536
  83.0 5.0 %ff_grad_send.2 = bf16[2,400,1536]{2,1,0:T(8,128)(2,1)} custom-call(s32[9]{0:T(128)} %stack.39.pick, bf16[2,2,384,512]{3,2,1,0:T(8,128)(2,1)} %get-tuple-element.147.lhs_ref, bf16[2,4,512,768]{3,2,1,0:T(8,128)(2,1)} %get-tuple-element.154.rhs_ref, f32[8,1536]{1,0:T(8,128)} %get-tuple-element.149.small_ref), custom_call_target="tpu_custom_call" | custom-call | flops 1207959552 | bytes 10000000 | tf_op jit(solution)/shard_map/ff_grad_send/pallas_call | solution.py:640
  88.2 5.1 %ff_grad_send.3 = bf16[2,400,1536]{2,1,0:T(8,128)(2,1)} custom-call(s32[9]{0:T(128)} %stack.39.pick, bf16[2,2,384,512]{3,2,1,0:T(8,128)(2,1)} %get-tuple-element.147.lhs_ref, bf16[2,4,512,768]{3,2,1,0:T(8,128)(2,1)} %get-tuple-element.154.rhs_ref, f32[8,1536]{1,0:T(8,128)} %get-tuple-element.149.small_ref), custom_call_target="tpu_custom_call" | custom-call | flops 1207959552 | bytes 10000000 | tf_op jit(solution)/shard_map/ff_grad_send/pallas_call | solution.py:640
  93.6 5.6 %ff_grad_keep.2 = (bf16[2,208,1536]{2,1,0:T(8,128)(2,1)}, bf16[2,192,1536]{2,1,0:T(8,128)(2,1)}, f32[8,1536]{1,0:T(8,128)}) custom-call(s32[9]{0:T(128)} %stack.39.pick, bf16[2,2,384,512]{3,2,1,0:T(8,128)(2,1)} %get-tuple-element.147.lhs_ref, bf16[2,4,512,768]{3,2,1,0:T(8,128)(2,1)} %get-tuple-element.154.rhs_ref, ...), custom_call_target="tpu_custom_call" | custom-call | flops 1207959552 | bytes 10000000 | tf_op jit(solution)/shard_map/ff_grad_keep/pallas_call | solution.py:653
  101.3 5.6 %ff_grad_keep.3 = (bf16[2,208,1536]{2,1,0:T(8,128)(2,1)}, bf16[2,192,1536]{2,1,0:T(8,128)(2,1)}, f32[8,1536]{1,0:T(8,128)}) custom-call(s32[9]{0:T(128)} %stack.39.pick, bf16[2,2,384,512]{3,2,1,0:T(8,128)(2,1)} %get-tuple-element.147.lhs_ref, bf16[2,4,512,768]{3,2,1,0:T(8,128)(2,1)} %get-tuple-element.154.rhs_ref, ...), custom_call_target="tpu_custom_call" | custom-call | flops 1207959552 | bytes 10000000 | tf_op jit(solution)/shard_map/ff_grad_keep/pallas_call | solution.py:653
  106.9 20.6 %attn_bwd.2 = (bf16[2,384,1920]{2,1,0:T(8,128)(2,1)}, f32[1,1920]{1,0:T(1,128)}, bf16[512,768]{1,0:T(8,128)(2,1)}) custom-call(s32[9]{0:T(128)} %stack.39.pick, bf16[512,768]{1,0:T(8,128)(2,1)} %get-tuple-element.227.refs_0_.df_ref, bf16[2,384,512]{2,1,0:T(8,128)(2,1)} %get-tuple-element.158.refs_1_, bf16[512,384]{1,0:T(8,128)(2,1)} %get-tuple-element.159.refs_2_, ...), custom_call_target="tpu_custom_call" | custom-call | flops 6543114240 | bytes 14000000 | tf_op jit(solution)/shard_map/attn_bwd/pallas_call | solution.py:329
  131.8 3.6 %add_x.3 = (bf16[2,48,1536]{2,1,0:T(8,128)(2,1)}, bf16[2,64,1536]{2,1,0:T(8,128)(2,1)}, bf16[2,64,1536]{2,1,0:T(8,128)(2,1)}, bf16[2,64,1536]{2,1,0:T(8,128)(2,1)}, f32[8,1536]{1,0:T(8,128)}) custom-call(s32[9]{0:T(128)} %stack.39.pick, bf16[2,192,1536]{2,1,0:T(8,128)(2,1)} %get-tuple-element.168.keep_ref, ...), custom_call_target="tpu_custom_call" | custom-call | flops 589824 | bytes 3538944 | tf_op jit(solution)/shard_map/add_x/pallas_call | solution.py:757
  139.8 21.7 %attn_bwd.3 = (bf16[400,1920]{1,0:T(8,128)(2,1)}, bf16[384,1920]{1,0:T(8,128)(2,1)}, f32[1,1920]{1,0:T(1,128)}, bf16[1024,768]{1,0:T(8,128)(2,1)}) custom-call(s32[9]{0:T(128)} %stack.39.pick, bf16[512,768]{1,0:T(8,128)(2,1)} %collective-permute-done.12.refs_0_.df_ref, bf16[2,384,512]{2,1,0:T(8,128)(2,1)} %get-tuple-element.174.refs_1_, ...), custom_call_target="tpu_custom_call" | custom-call | flops 6543114240 | bytes 14000000 | tf_op jit(solution)/shard_map/attn_bwd/pallas_call | solution.py:329
  161.5 4.5 %collective-permute-done.16.r2 = bf16[2,64,1536]{2,1,0:T(8,128)(2,1)} collective-permute-done((bf16[2,64,1536]{2,1,0:T(8,128)(2,1)}, bf16[2,64,1536]{2,1,0:T(8,128)(2,1)}, u32[]{:S(2)}, u32[]{:S(2)}) %collective-permute-start.16) | collective-permute-done | bytes 393248 | tf_op jit(solution)/shard_map/ppermute | solution.py:982
  166.4 3.4 %add_x.4 = (bf16[2,48,1536]{2,1,0:T(8,128)(2,1)}, bf16[2,48,1536]{2,1,0:T(8,128)(2,1)}, bf16[2,48,1536]{2,1,0:T(8,128)(2,1)}, bf16[2,48,1536]{2,1,0:T(8,128)(2,1)}) custom-call(s32[9]{0:T(128)} %stack.39.pick, bf16[2,192,1536]{2,1,0:T(8,128)(2,1)} %get-tuple-element.197.keep_ref, bf16[2,208,1536]{2,1,0:T(8,128)(2,1)} %collective-permute-done.14.got_ref, ...), custom_call_target="tpu_custom_call" | custom-call | flops 589824 | bytes 3538944 | tf_op jit(solution)/shard_map/add_x/pallas_call | solution.py:757
  172.0 4.7 %attn_split.1 = (bf16[1,208,1920]{2,1,0:T(8,128)(2,1)}, bf16[1,192,1920]{2,1,0:T(8,128)(2,1)}, f32[8,1920]{1,0:T(8,128)}) custom-call(s32[9]{0:T(128)} %stack.39.pick, bf16[384,1920]{1,0:T(8,128)(2,1)} %get-tuple-element.203.kept_ref, bf16[400,1920]{1,0:T(8,128)(2,1)} %collective-permute-done.19.got_ref, f32[1,1920]{1,0:T(1,128)} %get-tuple-element.209.small_ref), custom_call_target="tpu_custom_call" | custom-call | flops 737280 | bytes 4423680 | tf_op jit(solution)/shard_map/attn_split/pallas_call | solution.py:700
  178.4 6.8 %collective-permute-start.20 = (bf16[2,48,1536]{2,1,0:T(8,128)(2,1)}, bf16[2,48,1536]{2,1,0:T(8,128)(2,1)}, u32[]{:S(2)}, u32[]{:S(2)}) collective-permute-start(bf16[2,48,1536]{2,1,0:T(8,128)(2,1)} %get-tuple-element.212), channel_id=1, source_target_pairs={{0,8},{2,10},{4,12},{6,14},{8,0},{10,2},{12,4},{14,6},{16,24},{18,... | collective-permute-start | bytes 884744 | tf_op jit(solution)/shard_map/ppermute | solution.py:982
  188.6 3.3 %place_grad.2.refs_0_ = f32[1024,768]{1,0:T(8,128)} custom-call(s32[9]{0:T(128)} %stack.39.pick, bf16[512,768]{1,0:T(8,128)(2,1)} %collective-permute-done.12.refs_0_.df_ref, bf16[1024,768]{1,0:T(8,128)(2,1)} %get-tuple-element.190.a_ref, bf16[512,768]{1,0:T(8,128)(2,1)} %copy-done.2), custom_call_target="tpu_custom_call" | custom-call | flops 1179648 | bytes 3932160 | tf_op jit(solution)/shard_map/place_grad/pallas_call | solution.py:878
  191.9 4.9 %collective-permute-done.23.got_ref = bf16[1,208,1920]{2,1,0:T(8,128)(2,1)S(1)} collective-permute-done((bf16[1,208,1920]{2,1,0:T(8,128)(2,1)}, bf16[1,208,1920]{2,1,0:T(8,128)(2,1)S(1)}, u32[]{:S(2)}, u32[]{:S(2)}) %collective-permute-start.23) | collective-permute-done | bytes 798752 | tf_op jit(solution)/shard_map/ppermute | solution.py:982
  197.7 3.1 %add_x.5 = (bf16[1,48,1920]{2,1,0:T(8,128)(2,1)}, bf16[1,64,1920]{2,1,0:T(8,128)(2,1)}, bf16[1,64,1920]{2,1,0:T(8,128)(2,1)}, bf16[1,64,1920]{2,1,0:T(8,128)(2,1)}, f32[8,1920]{1,0:T(8,128)}) custom-call(s32[9]{0:T(128)} %stack.39.pick, bf16[1,192,1920]{2,1,0:T(8,128)(2,1)} %get-tuple-element.217.keep_ref, bf16[1,208,1920]{2,1,0:T(8,128)(2,1)} %copy-done, ...), custom_call_target="tpu_custom_call" | custom-call | flops 368640 | bytes 2211840 | tf_op jit(solution)/shard_map/add_x/pallas_call | solution.py:757
  200.7 8.2 %collective-permute-done.21.r2 = bf16[2,48,1536]{2,1,0:T(8,128)(2,1)} collective-permute-done((bf16[2,48,1536]{2,1,0:T(8,128)(2,1)}, bf16[2,48,1536]{2,1,0:T(8,128)(2,1)}, u32[]{:S(2)}, u32[]{:S(2)}) %collective-permute-start.21) | collective-permute-done | bytes 294944 | tf_op jit(solution)/shard_map/ppermute | solution.py:982
  210.5 5.6 %collective-permute-start.26 = (bf16[1,64,1920]{2,1,0:T(8,128)(2,1)}, bf16[1,64,1920]{2,1,0:T(8,128)(2,1)S(1)}, u32[]{:S(2)}, u32[]{:S(2)}) collective-permute-start(bf16[1,64,1920]{2,1,0:T(8,128)(2,1)} %get-tuple-element.237), channel_id=1, source_target_pairs={{0,8},{2,10},{4,12},{6,14},{8,0},{10,2},{12,4},{14,6},{16,24},{18,... | collective-permute-start | bytes 737288 | tf_op jit(solution)/shard_map/ppermute | solution.py:982
  219.5 3.3 %place_grad.3 = f32[1024,768]{1,0:T(8,128)} custom-call(s32[9]{0:T(128)} %stack.39.pick, bf16[512,768]{1,0:T(8,128)(2,1)} %get-tuple-element.227.refs_0_.df_ref, bf16[512,768]{1,0:T(8,128)(2,1)} %get-tuple-element.166.a_ref, bf16[1024,768]{1,0:T(8,128)(2,1)} %collective-permute-done.24.b_ref, ...), custom_call_target="tpu_custom_call", output_to_operand_aliasing={{}: (4, {})} | custom-call | flops 1179648 | bytes 3932160 | tf_op jit(solution)/shard_map/place_grad/pallas_call | solution.py:878
  226.5 3.3 %place_output.1 = bf16[1024,768]{1,0:T(8,128)(2,1)} custom-call(s32[9]{0:T(128)} %stack.39.pick, bf16[512,768]{1,0:T(8,128)(2,1)} %get-tuple-element.235.refs_16_.a_ref, bf16[1024,768]{1,0:T(8,128)(2,1)} %collective-permute-done.24.b_ref), custom_call_target="tpu_custom_call" | custom-call | flops 393216 | bytes 3145728 | tf_op jit(solution)/shard_map/place_output/pallas_call | solution.py:905
  229.8 6.7 %collective-permute-done.27.r2 = bf16[1,64,1920]{2,1,0:T(8,128)(2,1)S(1)} collective-permute-done((bf16[1,64,1920]{2,1,0:T(8,128)(2,1)}, bf16[1,64,1920]{2,1,0:T(8,128)(2,1)S(1)}, u32[]{:S(2)}, u32[]{:S(2)}) %collective-permute-start.27) | collective-permute-done | bytes 245792 | tf_op jit(solution)/shard_map/ppermute | solution.py:982
  (82 shorter events, 47.1 us)
Async XLA Ops:
  1.9 24.6 %collective-permute-start.3 = (bf16[384,768]{1,0:T(8,128)(2,1)S(1)}, bf16[384,768]{1,0:T(8,128)(2,1)}, u32[]{:S(2)}, u32[]{:S(2)}) collective-permute-start(bf16[384,768]{1,0:T(8,128)(2,1)S(1)} %constant_dynamic-slice_fusion), channel_id=1, source_target_pairs={{0,1},{1,0},{2,3},{3,2},{4,5},{5,4},{6,7},{7,6},{8,9},{9,8},{10,11... | collective-permute-start | bytes 1769480 | tf_op jit(solution)/shard_map/ppermute | solution.py:979
  6.8 24.1 %collective-permute-start.2 = (bf16[768,384]{1,0:T(8,128)(2,1)}, bf16[768,384]{1,0:T(8,128)(2,1)}, u32[]{:S(2)}, u32[]{:S(2)}) collective-permute-start(bf16[768,384]{1,0:T(8,128)(2,1)} %constant_dynamic-slice_fusion.1), channel_id=1, source_target_pairs={{0,1},{1,0},{2,3},{3,2},{4,5},{5,4},{6,7},{7,6},{8,9},{9,8},{10,11... | collective-permute-start | bytes 1769480 | tf_op jit(solution)/shard_map/ppermute | solution.py:979
  31.0 22.4 %collective-permute-start.5 = (bf16[768,384]{1,0:T(8,128)(2,1)}, bf16[768,384]{1,0:T(8,128)(2,1)}, u32[]{:S(2)}, u32[]{:S(2)}) collective-permute-start(bf16[768,384]{1,0:T(8,128)(2,1)} %collective-permute-done.2.wi0), channel_id=1, source_target_pairs={{0,4},{2,6},{4,0},{6,2},{8,12},{10,14},{12,8},{14,10},{16,20},{18,... | collective-permute-start | bytes 1769480 | tf_op jit(solution)/shard_map/ppermute | solution.py:982
  32.7 21.2 %collective-permute-start.6 = (bf16[384,768]{1,0:T(8,128)(2,1)}, bf16[384,768]{1,0:T(8,128)(2,1)}, u32[]{:S(2)}, u32[]{:S(2)}) collective-permute-start(bf16[384,768]{1,0:T(8,128)(2,1)} %collective-permute-done.3.wb0), channel_id=1, source_target_pairs={{0,8},{2,10},{4,12},{6,14},{8,0},{10,2},{12,4},{14,6},{16,24},{18,... | collective-permute-start | bytes 1769480 | tf_op jit(solution)/shard_map/ppermute | solution.py:982
  34.3 20.1 %collective-permute-start = (bf16[512,768]{1,0:T(8,128)(2,1)}, bf16[512,768]{1,0:T(8,128)(2,1)S(1)}, u32[]{:S(2)}, u32[]{:S(2)}) collective-permute-start(bf16[512,768]{1,0:T(8,128)(2,1)} %get-tuple-element.139), channel_id=1, source_target_pairs={{0,1},{1,0},{2,3},{3,2},{4,5},{5,4},{6,7},{7,6},{8,9},{9,8},{10,11... | collective-permute-start | bytes 2359304 | tf_op jit(solution)/shard_map/ppermute | solution.py:979
  35.8 18.2 %collective-permute-start.1 = (bf16[1536]{0:T(1024)(128)(2,1)S(1)}, bf16[1536]{0:T(1024)(128)(2,1)S(1)}, u32[]{:S(2)}, u32[]{:S(2)}) collective-permute-start(bf16[1536]{0:T(1024)(128)(2,1)S(1)} %copy-done.8), channel_id=1, source_target_pairs={{0,1},{1,0},{2,3},{3,2},{4,5},{5,4},{6,7},{7,6},{8,9},{9,8},{10,11... | collective-permute-start | bytes 9224 | tf_op jit(solution)/shard_map/ppermute | solution.py:979
  93.2 8.0 %collective-permute-start.13 = (bf16[2,400,1536]{2,1,0:T(8,128)(2,1)}, bf16[2,400,1536]{2,1,0:T(8,128)(2,1)}, u32[]{:S(2)}, u32[]{:S(2)}) collective-permute-start(bf16[2,400,1536]{2,1,0:T(8,128)(2,1)} %ff_grad_send.3), channel_id=1, source_target_pairs={{0,2},{2,0},{4,6},{6,4},{8,10},{10,8},{12,14},{14,12},{16,18},{18,... | collective-permute-start | bytes 7372808 | tf_op jit(solution)/shard_map/ppermute | solution.py:982
  99.3 30.6 %collective-permute-start.11 = (bf16[2,208,1536]{2,1,0:T(8,128)(2,1)}, bf16[2,208,1536]{2,1,0:T(8,128)(2,1)}, u32[]{:S(2)}, u32[]{:S(2)}) collective-permute-start(bf16[2,208,1536]{2,1,0:T(8,128)(2,1)} %get-tuple-element.152), channel_id=1, source_target_pairs={{0,4},{2,6},{4,0},{6,2},{8,12},{10,14},{12,8},{14,10},{16,20},{18,... | collective-permute-start | bytes 3833864 | tf_op jit(solution)/shard_map/ppermute | solution.py:982
  99.7 27.7 %collective-permute-start.12 = (bf16[512,768]{1,0:T(8,128)(2,1)S(1)}, bf16[512,768]{1,0:T(8,128)(2,1)}, u32[]{:S(2)}, u32[]{:S(2)}) collective-permute-start(bf16[512,768]{1,0:T(8,128)(2,1)S(1)} %copy-done.1), channel_id=1, source_target_pairs={{0,1},{1,0},{2,3},{3,2},{4,5},{5,4},{6,7},{7,6},{8,9},{9,8},{10,11... | collective-permute-start | bytes 2359304 | tf_op jit(solution)/shard_map/ppermute | solution.py:979
  129.8 36.1 %collective-permute-start.14 = (bf16[2,208,1536]{2,1,0:T(8,128)(2,1)}, bf16[2,208,1536]{2,1,0:T(8,128)(2,1)}, u32[]{:S(2)}, u32[]{:S(2)}) collective-permute-start(bf16[2,208,1536]{2,1,0:T(8,128)(2,1)} %get-tuple-element.186), channel_id=1, source_target_pairs={{0,4},{2,6},{4,0},{6,2},{8,12},{10,14},{12,8},{14,10},{16,20},{18,... | collective-permute-start | bytes 3833864 | tf_op jit(solution)/shard_map/ppermute | solution.py:982
  130.3 31.1 %collective-permute-start.18 = (bf16[512,768]{1,0:T(8,128)(2,1)}, bf16[512,768]{1,0:T(8,128)(2,1)S(1)}, u32[]{:S(2)}, u32[]{:S(2)}) collective-permute-start(bf16[512,768]{1,0:T(8,128)(2,1)} %get-tuple-element.166.a_ref), channel_id=1, source_target_pairs={{0,1},{1,0},{2,3},{3,2},{4,5},{5,4},{6,7},{7,6},{8,9},{9,8},{10,11... | collective-permute-start | bytes 2359304 | tf_op jit(solution)/shard_map/ppermute | solution.py:979
  135.4 26.1 %collective-permute-start.15 = (bf16[2,64,1536]{2,1,0:T(8,128)(2,1)}, bf16[2,64,1536]{2,1,0:T(8,128)(2,1)}, u32[]{:S(2)}, u32[]{:S(2)}) collective-permute-start(bf16[2,64,1536]{2,1,0:T(8,128)(2,1)} %get-tuple-element.187), channel_id=1, source_target_pairs={{0,8},{2,10},{4,12},{6,14},{8,0},{10,2},{12,4},{14,6},{16,24},{18,... | collective-permute-start | bytes 1179656 | tf_op jit(solution)/shard_map/ppermute | solution.py:982
  135.8 30.1 %collective-permute-start.16 = (bf16[2,64,1536]{2,1,0:T(8,128)(2,1)}, bf16[2,64,1536]{2,1,0:T(8,128)(2,1)}, u32[]{:S(2)}, u32[]{:S(2)}) collective-permute-start(bf16[2,64,1536]{2,1,0:T(8,128)(2,1)} %get-tuple-element.188), channel_id=1, source_target_pairs={{0,16},{2,18},{4,20},{6,22},{8,24},{10,26},{12,28},{14,30},{16,0},... | collective-permute-start | bytes 1179656 | tf_op jit(solution)/shard_map/ppermute | solution.py:982
  138.4 27.5 %collective-permute-start.17 = (bf16[2,64,1536]{2,1,0:T(8,128)(2,1)}, bf16[2,64,1536]{2,1,0:T(8,128)(2,1)}, u32[]{:S(2)}, u32[]{:S(2)}) collective-permute-start(bf16[2,64,1536]{2,1,0:T(8,128)(2,1)} %get-tuple-element.189), channel_id=1, source_target_pairs={{0,24},{2,26},{4,28},{6,30},{8,16},{10,18},{12,20},{14,22},{16,8},... | collective-permute-start | bytes 1179656 | tf_op jit(solution)/shard_map/ppermute | solution.py:982
  166.0 6.1 %collective-permute-start.19 = (bf16[400,1920]{1,0:T(8,128)(2,1)}, bf16[400,1920]{1,0:T(8,128)(2,1)}, u32[]{:S(2)}, u32[]{:S(2)}) collective-permute-start(bf16[400,1920]{1,0:T(8,128)(2,1)} %get-tuple-element.204), channel_id=1, source_target_pairs={{0,2},{2,0},{4,6},{6,4},{8,10},{10,8},{12,14},{14,12},{16,18},{18,... | collective-permute-start | bytes 4608008 | tf_op jit(solution)/shard_map/ppermute | solution.py:982
  166.0 53.5 %collective-permute-start.24 = (bf16[1024,768]{1,0:T(8,128)(2,1)}, bf16[1024,768]{1,0:T(8,128)(2,1)}, u32[]{:S(2)}, u32[]{:S(2)}) collective-permute-start(bf16[1024,768]{1,0:T(8,128)(2,1)} %get-tuple-element.190.a_ref), channel_id=1, source_target_pairs={{0,1},{1,0},{2,3},{3,2},{4,5},{5,4},{6,7},{7,6},{8,9},{9,8},{10,11... | collective-permute-start | bytes 4718600 | tf_op jit(solution)/shard_map/ppermute | solution.py:979
  176.7 20.1 %collective-permute-start.23 = (bf16[1,208,1920]{2,1,0:T(8,128)(2,1)}, bf16[1,208,1920]{2,1,0:T(8,128)(2,1)S(1)}, u32[]{:S(2)}, u32[]{:S(2)}) collective-permute-start(bf16[1,208,1920]{2,1,0:T(8,128)(2,1)} %get-tuple-element.210), channel_id=1, source_target_pairs={{0,4},{2,6},{4,0},{6,2},{8,12},{10,14},{12,8},{14,10},{16,20},{18,... | collective-permute-start | bytes 2396168 | tf_op jit(solution)/shard_map/ppermute | solution.py:982
  178.4 22.3 %collective-permute-start.20 = (bf16[2,48,1536]{2,1,0:T(8,128)(2,1)}, bf16[2,48,1536]{2,1,0:T(8,128)(2,1)}, u32[]{:S(2)}, u32[]{:S(2)}) collective-permute-start(bf16[2,48,1536]{2,1,0:T(8,128)(2,1)} %get-tuple-element.212), channel_id=1, source_target_pairs={{0,8},{2,10},{4,12},{6,14},{8,0},{10,2},{12,4},{14,6},{16,24},{18,... | collective-permute-start | bytes 884744 | tf_op jit(solution)/shard_map/ppermute | solution.py:982
  185.2 23.8 %collective-permute-start.21 = (bf16[2,48,1536]{2,1,0:T(8,128)(2,1)}, bf16[2,48,1536]{2,1,0:T(8,128)(2,1)}, u32[]{:S(2)}, u32[]{:S(2)}) collective-permute-start(bf16[2,48,1536]{2,1,0:T(8,128)(2,1)} %get-tuple-element.213), channel_id=1, source_target_pairs={{0,16},{2,18},{4,20},{6,22},{8,24},{10,26},{12,28},{14,30},{16,0},... | collective-permute-start | bytes 884744 | tf_op jit(solution)/shard_map/ppermute | solution.py:982
  187.1 21.9 %collective-permute-start.22 = (bf16[2,48,1536]{2,1,0:T(8,128)(2,1)}, bf16[2,48,1536]{2,1,0:T(8,128)(2,1)}, u32[]{:S(2)}, u32[]{:S(2)}) collective-permute-start(bf16[2,48,1536]{2,1,0:T(8,128)(2,1)} %get-tuple-element.214), channel_id=1, source_target_pairs={{0,24},{2,26},{4,28},{6,30},{8,16},{10,18},{12,20},{14,22},{16,8},... | collective-permute-start | bytes 884744 | tf_op jit(solution)/shard_map/ppermute | solution.py:982
  209.0 13.8 %collective-permute-start.25 = (bf16[2,64,1536]{2,1,0:T(8,128)(2,1)}, bf16[2,64,1536]{2,1,0:T(8,128)(2,1)S(1)}, u32[]{:S(2)}, u32[]{:S(2)}) collective-permute-start(bf16[2,64,1536]{2,1,0:T(8,128)(2,1)} %get-tuple-element.232), channel_id=1, source_target_pairs={{0,1},{1,0},{2,3},{3,2},{4,5},{5,4},{6,7},{7,6},{8,9},{9,8},{10,11... | collective-permute-start | bytes 1179656 | tf_op jit(solution)/shard_map/ppermute | solution.py:979
  210.5 19.3 %collective-permute-start.26 = (bf16[1,64,1920]{2,1,0:T(8,128)(2,1)}, bf16[1,64,1920]{2,1,0:T(8,128)(2,1)S(1)}, u32[]{:S(2)}, u32[]{:S(2)}) collective-permute-start(bf16[1,64,1920]{2,1,0:T(8,128)(2,1)} %get-tuple-element.237), channel_id=1, source_target_pairs={{0,8},{2,10},{4,12},{6,14},{8,0},{10,2},{12,4},{14,6},{16,24},{18,... | collective-permute-start | bytes 737288 | tf_op jit(solution)/shard_map/ppermute | solution.py:982
  216.1 20.4 %collective-permute-start.27 = (bf16[1,64,1920]{2,1,0:T(8,128)(2,1)}, bf16[1,64,1920]{2,1,0:T(8,128)(2,1)S(1)}, u32[]{:S(2)}, u32[]{:S(2)}) collective-permute-start(bf16[1,64,1920]{2,1,0:T(8,128)(2,1)} %get-tuple-element.238), channel_id=1, source_target_pairs={{0,16},{2,18},{4,20},{6,22},{8,24},{10,26},{12,28},{14,30},{16,0},... | collective-permute-start | bytes 737288 | tf_op jit(solution)/shard_map/ppermute | solution.py:982
  218.0 18.5 %collective-permute-start.28 = (bf16[1,64,1920]{2,1,0:T(8,128)(2,1)}, bf16[1,64,1920]{2,1,0:T(8,128)(2,1)}, u32[]{:S(2)}, u32[]{:S(2)}) collective-permute-start(bf16[1,64,1920]{2,1,0:T(8,128)(2,1)} %get-tuple-element.239), channel_id=1, source_target_pairs={{0,24},{2,26},{4,28},{6,30},{8,16},{10,18},{12,20},{14,22},{16,8},... | collective-permute-start | bytes 737288 | tf_op jit(solution)/shard_map/ppermute | solution.py:982
  (15 other events, 85.9 us)
where the time goes:
time: 241 us; the launch traced here: 239 us
  Pallas kernels  154 us (64%)
  starting transfers between devices  41.1 us (17%)
  waiting for transfers between devices  35.1 us (15%)
  local copies, waits for them, and re-layouts  6.67 us (3%)
    pallas_call x2, Pallas kernels, attn_bwd(): pl.pallas_call(partial(attn_bwd_kernel, groups, box_groups, first), grid_...  42.3 us
    pallas_call x2, Pallas kernels, attn_fwd(): pl.pallas_call(partial(attn_fwd_kernel, groups, which_page), grid_spec=pl...  34.1 us
    ppermute x21, starting transfers between devices, over_dp(): return lax.ppermute(value, 'dp', swap_perm(shards_dp, flip))  31.1 us
    ppermute x21, waiting for transfers between devices, over_dp(): return lax.ppermute(value, 'dp', swap_perm(shards_dp, flip))  30.6 us
    pallas_call x1, Pallas kernels, feed_forward(): pl.pallas_call(partial(ff_kernel, groups), grid_spec=pltpu.PrefetchScalar...  24.8 us
    pallas_call x2, Pallas kernels, ff_grad(): pl.pallas_call(ff_keep_kernel, grid_spec=pltpu.PrefetchScalarGridSpec(num...  11.2 us
    pallas_call x2, Pallas kernels, ff_grad(): pl.pallas_call(ff_send_kernel, grid_spec=pltpu.PrefetchScalarGridSpec(num...  10.1 us
    ppermute x8, starting transfers between devices, over_head(): return lax.ppermute(value, 'head', [(0, 1), (1, 0)])  10 us
  transfers between devices with their start and end apart: 29, of which 10 were waited for; matrix products, arithmetic and copies ran while one was open for 2% of the time, Pallas kernels for 51%

commit v1 on v0

--- a/solution.py
+++ b/solution.py
@@ -74,14 +74,18 @@
 
 def attn_fwd_kernel(
     groups, which_page, pick, res, tok_ref, box_ref, freq_ref, wq_ref, wk_ref, wv_ref, bq_ref, bv_ref, wbt_ref, wo_ref,
-    part_ref, p_ref, q_ref, k_ref, v_ref, ctx_ref, s_ref, c_ref, tok_t_ref, codes, mixed, acc, biases,
+    part_ref, p_ref, q_ref, k_ref, v_ref, ctx_ref, s_ref, c_ref, tok_t_ref, codes, mixed, acc, biases, s_keep, c_keep, t_keep, sems,
 ):
     step = pl.program_id(0)
-    half = s_ref.shape[1]
+    half = s_keep.shape[1]
+
+    def leaving():
+        pairs = ((s_keep, s_ref), (c_keep, c_ref), (t_keep, tok_t_ref))
+        return [pltpu.make_async_copy(a, b, sems.at[n]) for n, (a, b) in enumerate(pairs)]
 
     @pl.when(step == 0)
     def _():
-        rows = s_ref.shape[0]
+        rows = s_keep.shape[0]
         lanes = lax.broadcasted_iota(jnp.int32, (rows, half), 1)
         level = res[pick[which_page]]
         width = (612 + 204 * level).astype(F32)
@@ -92,16 +96,18 @@
         both = jnp.concatenate([centre_x, centre_y, jnp.zeros((6, rows), F32)], axis=0).T
         centre = jnp.where(lanes < half // 2, both[:, 0:1], both[:, 1:2])
         sine, cosine = sin_cos(centre * freq_ref[...])
-        s_ref[...] = sine
-        c_ref[...] = cosine
+        s_keep[...] = sine
+        c_keep[...] = cosine
         codes[:, :half] = cosine.astype(BF16)
         codes[:, half : 2 * half] = sine.astype(BF16)
         acc[...] = jnp.zeros_like(acc)
         biases[0:1] = bq_ref[...].astype(F32).reshape(1, -1)
         biases[1:2] = bv_ref[...].astype(F32).reshape(1, -1)
         tok_t = split_rows(tok_ref[...].T, groups)
-        tok_t_ref[0] = tok_t[:half]
-        tok_t_ref[1] = tok_t[half:]
+        t_keep[0] = tok_t[:half]
+        t_keep[1] = tok_t[half:]
+        for copy in leaving():
+            copy.start()
 
     tok = tok_ref[...]
     rows = tok.shape[0]
@@ -115,7 +121,7 @@
     k_ref[...] = k2
     v_ref[...] = v2
     codes[:, 2 * half :] = k2
-    sine, cosine = s_ref[...], c_ref[...]
+    sine, cosine = s_keep[...], c_keep[...]
     for which in range(2):
         span = slice(which * rows, (which + 1) * rows)
         qm = keep(lane_mask(q2.shape, which), q2)
@@ -141,6 +147,8 @@
     @pl.when(step == pl.num_programs(0) - 1)
     def _():
         part_ref[...] = acc[...].astype(BF16)
+        for copy in leaving():
+            copy.wait()
 
 
 def attn_fwd(which_page, pick, res, tokens, boxes, freq, wq, wk, wv, bq, bv, wbt, wo, length, groups):
@@ -178,15 +186,19 @@
                 pl.BlockSpec((length, wide), cols),
                 pl.BlockSpec((length, wide), cols),
                 pl.BlockSpec((length, wide), cols),
-                pl.BlockSpec((length, dim // 2), fixed),
-                pl.BlockSpec((length, dim // 2), fixed),
-                pl.BlockSpec((2, dim // 2, length), lambda i, pick, res: (0, 0, 0)),
+                pl.BlockSpec(memory_space=pl.ANY),
+                pl.BlockSpec(memory_space=pl.ANY),
+                pl.BlockSpec(memory_space=pl.ANY),
             ],
             scratch_shapes=[
                 pltpu.VMEM((length, dim + wide), BF16),
                 pltpu.VMEM((2 * length, dim + wide), BF16),
                 pltpu.VMEM((length, dim), F32),
                 pltpu.VMEM((8, inner), F32),
+                pltpu.VMEM((length, dim // 2), F32),
+                pltpu.VMEM((length, dim // 2), F32),
+                pltpu.VMEM((2, dim // 2, length), BF16),
+                pltpu.SemaphoreType.DMA((3,)),
             ],
         ),
         out_shape=[
@@ -410,7 +422,7 @@
     bi_here, bi_there,
     wi_here, wb_here, wi0, wi1, wi2, wi3, wb0, wb1, wb2, wb3,
     out_ref, df_ref, lhs_ref, rhs_ref, small_ref,
-    wi, wb, slope, norm_low, grad_low, acc, wide, bi_ref, sems,
+    wi, wb, slope, norm_low, grad_low, acc, wide, bi_ref, rhs, sems,
 ):
     blocks, dim, cols = wi.shape
     here = blocks // 2
@@ -461,6 +473,9 @@
     lhs_ref[0, 0] = low_t[:split]
     lhs_ref[1, 0] = low_t[split:]
 
+    def leaving(m, j):
+        return pltpu.make_async_copy(rhs.at[m, j], rhs_ref.at[m, j], sems.at[2 + m, j])
+
     def forward(j, _):
         for p in range(2):
             pltpu.make_async_copy(wi0, wi.at[j, :, pl.ds(0, piece)], sems.at[0, 2 * j + p]).wait()
@@ -468,7 +483,8 @@
         pre = mm(norm_low[...], wi[j]) + bi_ref[pl.ds(place(j), 1), :]
         phi, step = gelu_parts(pre)
         act = (pre * phi).astype(BF16)
-        rhs_ref[1, j] = act
+        rhs[1, j] = act
+        leaving(1, j).start()
         slope[j] = step
         acc[...] += mm(act, wb[j])
         return 0
@@ -491,7 +507,8 @@
     def backward(j, _):
         grad_act = mm_nt(grad_low[...], wb[j]).astype(BF16).astype(F32)
         grad_pre = (grad_act * slope[j]).astype(BF16)
-        rhs_ref[0, j] = grad_pre
+        rhs[0, j] = grad_pre
+        leaving(0, j).start()
         bi_ref[pl.ds(place(j), 1), :] = column_sum(grad_pre.astype(F32))
         acc[...] += mm_nt(grad_pre, wi[j])
         return 0
@@ -509,6 +526,9 @@
     grad_first = norm_back(grad_normed * g1, scaled1, inv1)
     small_out = column_sum(grad_first)
     df_ref[...] = grad_first.astype(BF16)
+    for m in range(2):
+        for j in range(blocks):
+            leaving(m, j).wait()
     small_ref[...] = jnp.concatenate(
         [
             jnp.concatenate([small_gain2, small_bias2], axis=1),
@@ -551,7 +571,7 @@
                 whole,
                 whole,
                 pl.BlockSpec((2, 2, dim // 2, length), lambda i, pick: (0, 0, 0, 0)),
-                pl.BlockSpec((2, blocks, length, cols), lambda i, pick: (0, 0, 0, 0)),
+                anywhere,
                 pl.BlockSpec((8, 2 * dim), fixed),
             ],
             scratch_shapes=[
@@ -563,7 +583,8 @@
                 pltpu.VMEM((length, dim), F32),
                 pltpu.VMEM((length, dim), F32),
                 pltpu.VMEM((blocks, cols), F32),
-                pltpu.SemaphoreType.DMA((2, 2 * blocks)),
+                pltpu.VMEM((2, blocks, length, cols), BF16),
+                pltpu.SemaphoreType.DMA((4, 2 * blocks)),
             ],
         ),
         out_shape=[
@@ -732,26 +753,25 @@
         ref[0, at:] = wide_tail(small[0:1])
 
 
-def add_x_kernel(tailed, pick, keep_ref, got_ref, small_ref, own, s1, s2, s3, *rest):
-    shard = own.shape[1]
+def add_x_kernel(tailed, pick, keep_ref, got_ref, small_ref, own, sent, *rest):
+    shard = own.shape[1] // 2
     z = pick[5]
+    for i, d in enumerate((0, 2, 1, 3)):
+        at = pl.multiple_of((z ^ d) * shard, 16)
+        ref = own if i < 2 else sent
+        ref[:, (i % 2) * shard : (i % 2 + 1) * shard] = (
+            keep_ref[:, pl.ds(at, shard), :].astype(F32) + got_ref[:, pl.ds(at, shard), :].astype(F32)
+        ).astype(BF16)
     if tailed:
         small = rounded(small_ref[...]) + tail_sum(got_ref, 4 * shard)
         rest[0][...] = small
-    for d, ref in enumerate((own, s1, s2, s3)):
-        at = pl.multiple_of((z ^ d) * shard, 16)
-        ref[:, :shard] = (
-            keep_ref[:, pl.ds(at, shard), :].astype(F32) + got_ref[:, pl.ds(at, shard), :].astype(F32)
-        ).astype(BF16)
-        if d and tailed:
-            put_tail(ref, shard, small)
+        put_tail(sent, 2 * shard, small)
 
 
 def add_x(pick, kept, got, small, tailed):
     mats, rows, cols = kept.shape
-    shard = rows // 4
-    own = hbm((mats, shard, cols), BF16)
-    sent = hbm((mats, shard + (TAIL if tailed else 0), cols), BF16)
+    own = hbm((mats, rows // 2, cols), BF16)
+    sent = hbm((mats, rows // 2 + (TAIL if tailed else 0), cols), BF16)
     full = lambda s: pl.BlockSpec(s.shape, lambda i, pick: (0,) * len(s.shape))
     extra = [hbm(small.shape, F32)] if tailed else []
     return pl.pallas_call(
@@ -760,50 +780,72 @@
             num_scalar_prefetch=1,
             grid=(1,),
             in_specs=[full(kept), full(got), full(small)],
-            out_specs=[full(own)] + [full(sent)] * 3 + [full(s) for s in extra],
+            out_specs=[full(s) for s in [own, sent] + extra],
         ),
-        out_shape=[own] + [sent] * 3 + extra,
+        out_shape=[own, sent] + extra,
         compiler_params=params(1),
         cost_estimate=cost(kept.size, 6 * kept.size),
         name="add_x",
     )(pick, kept, got, small)
 
 
-def sum4(own, r1, r2, r3):
-    return (own.astype(F32) + r1.astype(F32)) + (r2.astype(F32) + r3.astype(F32))
-
-
-def small4(small_ref, others, at):
-    terms = [tail_sum(r, at) for r in others]
-    return (rounded(small_ref[...]) + terms[0]) + (terms[1] + terms[2])
-
-
-def add_z_kernel(own, r1, r2, r3, small_ref, out, small_out):
+def whole_call(kernel, out_shape, estimate, name, *args):
+    full = lambda s: pl.BlockSpec(s.shape, lambda i: (0,) * len(s.shape))
+    return pl.pallas_call(
+        kernel,
+        grid=(1,),
+        in_specs=[full(a) for a in args],
+        out_specs=[full(s) for s in out_shape],
+        out_shape=out_shape,
+        compiler_params=params(1),
+        cost_estimate=estimate,
+        name=name,
+    )(*args)
+
+
+def both(a, b):
+    return a.astype(F32) + b.astype(F32)
+
+
+def add_z_kernel(tailed, keep_ref, got_ref, small_ref, own, sent, *rest):
     shard = own.shape[1]
-    out[:, :shard] = sum4(own[...], r1[:, :shard], r2[:, :shard], r3[:, :shard]).astype(BF16)
-    small = small4(small_ref, (r1, r2, r3), shard)
+    own[...] = both(keep_ref[:, :shard], got_ref[:, :shard]).astype(BF16)
+    sent[:, :shard] = both(keep_ref[:, shard:], got_ref[:, shard : 2 * shard]).astype(BF16)
+    if tailed:
+        small = rounded(small_ref[...]) + tail_sum(got_ref, 2 * shard)
+        rest[0][...] = small
+        put_tail(sent, shard, small)
+
+
+def add_z(kept, got, small, tailed):
+    mats, rows, cols = kept.shape
+    shard = rows // 2
+    out = [hbm((mats, shard, cols), BF16), hbm((mats, shard + (TAIL if tailed else 0), cols), BF16)]
+    if tailed:
+        out.append(hbm(small.shape, F32))
+    return whole_call(
+        partial(add_z_kernel, tailed), out, cost(4e10, 6 * kept.size), "add_z", kept, got, small
+    )
+
+
+def for_head_kernel(own, got, small_ref, out, small_out):
+    shard = own.shape[1]
+    out[:, :shard] = both(own[...], got[:, :shard]).astype(BF16)
+    small = rounded(small_ref[...]) + tail_sum(got, shard)
     small_out[...] = small
     put_tail(out, shard, small)
 
 
-def add_z(blocks, small):
-    return pl.pallas_call(
-        add_z_kernel,
-        out_shape=[
-            hbm(blocks[1].shape, BF16),
-            hbm(small.shape, F32),
-        ],
-        compiler_params=pltpu.CompilerParams(vmem_limit_bytes=VMEM_LIMIT),
-        cost_estimate=cost(4 * blocks[0].size, 10 * blocks[0].size),
-        name="add_z",
-    )(*blocks, small)
-
-
-def ff_last_kernel(pick, own, r1, r2, r3, got, small_ref, in_out, back_out, *vectors):
+def for_head(own, got, small):
+    out = [hbm(got.shape, BF16), hbm(small.shape, F32)]
+    return whole_call(for_head_kernel, out, cost(4e10, 6 * own.size), "for_head", own, got, small)
+
+
+def ff_last_kernel(pick, own, z_got, got, small_ref, in_out, back_out, *vectors):
     small_out = vectors[-1]
     shard = own.shape[1]
-    in_out[...] = sum4(own[0], r1[0], r2[0], r3[0]) + got[0, :shard].astype(F32)
-    back_out[...] = sum4(own[1], r1[1, :shard], r2[1, :shard], r3[1, :shard]) + got[1, :shard].astype(F32)
+    in_out[...] = both(own[0], z_got[0]) + got[0, :shard].astype(F32)
+    back_out[...] = both(own[1], z_got[1]) + got[1, :shard].astype(F32)
     small = rounded(small_ref[...]) + tail_sum(got, shard)
     small_out[...] = small
     dim = small.shape[1] // 2
@@ -812,21 +854,17 @@
     vectors[6][...] = small_out[pl.ds(3 + pick[0], 1), :].reshape(2 * dim)
 
 
-def ff_last(pick, blocks, got, small):
-    _, rows, cols = blocks[0].shape
+def ff_last(pick, own, z_got, got, small):
+    _, rows, cols = own.shape
     dim = cols // 2
     full = lambda s: pl.BlockSpec(s.shape, lambda i, pick: (0,) * len(s.shape))
-    out_shape = (
-        [hbm((rows, cols), F32)] * 2
-        + [hbm((dim,), F32)] * 6
-        + [hbm((cols,), F32)]
-    )
+    out_shape = [hbm((rows, cols), F32)] * 2 + [hbm((dim,), F32)] * 6 + [hbm((cols,), F32)]
     return pl.pallas_call(
         ff_last_kernel,
         grid_spec=pltpu.PrefetchScalarGridSpec(
             num_scalar_prefetch=1,
             grid=(1,),
-            in_specs=[full(b) for b in blocks] + [full(got), full(small)],
+            in_specs=[full(own), full(z_got), full(got), full(small)],
             out_specs=[full(s) for s in out_shape],
             scratch_shapes=[pltpu.VMEM(small.shape, F32)],
         ),
@@ -834,36 +872,29 @@
         compiler_params=params(1),
         cost_estimate=cost(10 * got.size, 20 * got.size),
         name="ff_last",
-    )(pick, *blocks, got, small)
-
-
-def attn_last_kernel(own, r1, r2, r3, small_ref, q_out, k_out, v_out, box_out, wo_out, bq_out, bv_out):
+    )(pick, own, z_got, got, small)
+
+
+def attn_last_kernel(own, got, small_ref, q_out, k_out, v_out, box_out, wo_out, bq_out, bv_out):
     shard = own.shape[1]
     wide = 2 * HEAD
     pairs = q_out.shape[1] // wide
-    small = small4(small_ref, (r1, r2, r3), shard)
+    small = rounded(small_ref[...]) + tail_sum(got, shard)
     for p in range(pairs):
         at = slice(p * wide, (p + 1) * wide)
         for i, ref in enumerate((q_out, k_out, v_out, wo_out, box_out)):
             span = slice((5 * p + i) * wide, (5 * p + i + 1) * wide)
-            ref[:, at] = sum4(own[0, :, span], r1[0, :shard, span], r2[0, :shard, span], r3[0, :shard, span])
+            ref[:, at] = both(own[0, :, span], got[0, :shard, span])
     for i, ref in enumerate((bq_out, bv_out)):
         row = [small[0:1, (5 * p + i) * wide : (5 * p + i + 1) * wide] for p in range(pairs)]
         ref[...] = jnp.concatenate(row, axis=1).reshape(pairs * wide)
 
 
-def attn_last(blocks, small):
-    _, rows, cols = blocks[0].shape
+def attn_last(own, got, small):
+    _, rows, cols = own.shape
     cols = cols // 5
-    flat = hbm((rows, cols), F32)
-    vector = hbm((cols,), F32)
-    return pl.pallas_call(
-        attn_last_kernel,
-        out_shape=[flat] * 5 + [vector, vector],
-        compiler_params=pltpu.CompilerParams(vmem_limit_bytes=VMEM_LIMIT),
-        cost_estimate=cost(4 * blocks[0].size, 12 * blocks[0].size),
-        name="attn_last",
-    )(*blocks, small)
+    out = [hbm((rows, cols), F32)] * 5 + [hbm((cols,), F32)] * 2
+    return whole_call(attn_last_kernel, out, cost(4 * own.size, 12 * own.size), "attn_last", own, got, small)
 
 
 def place_grad_kernel(pick, df_ref, a_ref, b_ref, *refs):
@@ -1033,14 +1064,15 @@
         xs_b, xk_b, small_b = ff_grad(pick, lhs, after(rhs, xs_a), small, False, got_b)
         df_own = after(df_own, xs_b)
     *part_a, inp_own = attend_back(df_own, saved_own)
-    inp_own_got = over_head(inp_own)
-
     if fast:
         xg_a, df_other, xs_b = after((xg_a, df_other, xs_b), inp_own)
+        own_a, sent_a, small_2 = add_x(pick, xk_a, after(xg_a, df_other), small_1, True)
+        zg_a = over_dp(sent_a, 4)
+        inp_send, df_other = after((inp_own, df_other), sent_a)
         xg_b = over_dp(xs_b, 2)
-        *z_a, small_2 = add_x(pick, xk_a, after(xg_a, df_other), small_1, True)
-        zg_a = [z_a[0]] + [over_dp(z_a[d], 4 * d) for d in (1, 2, 3)]
-        df_other = after(df_other, z_a[0])
+    else:
+        inp_send = inp_own
+    inp_own_got = over_head(inp_send)
 
     pick_back = pick if fast else pick.at[2:4].set(jnp.arange(2, dtype=jnp.int32))
     sent, kept, a_small, inp_other = attend_back(df_other, saved_other, part_a, out_own, pick_back)
@@ -1048,27 +1080,31 @@
 
     if fast:
         xg_b, zg_a, inp_own_got = after((xg_b, zg_a, inp_own_got), inp_other)
-        sent, xk_b = after((sent, xk_b), xg_b, zg_a, inp_own_got)
+        sent, xk_b, zg_a = after((sent, xk_b, zg_a), xg_b, zg_a, inp_own_got)
         sent_got = over_dp(sent, 1)
-        z_b = add_x(pick, xk_b, xg_b, small_b, False)
-        a_sum, small_3 = add_z([after(zg_a[0], z_b[0])] + zg_a[1:], small_2)
-        xs, xk, a_small = attn_split(pick, kept, after(sent_got, a_sum), a_small)
+        own_a, sent_a, small_3 = add_z(own_a, zg_a, small_2, True)
+        own_b, sent_b = add_x(pick, after(xk_b, sent_a), xg_b, small_b, False)
+        xs, xk, a_small = attn_split(pick, kept, after(sent_got, sent_b), a_small)
         xg = over_dp(xs, 2)
-        z_b = after(z_b, xs)
-        zg_b = [z_b[0]] + [over_dp(z_b[d], 4 * d) for d in (1, 2, 3)]
+        zg_a, zg_b = over_dp(sent_a, 8), over_dp(sent_b, 4)
         grad_input = place_grad(1, pick, after(df_other, xs), inp_other, inp_own_got, pages)
-        *blocks, a_small = add_x(pick, after(xk, grad_input), xg, a_small, True)
-        zg_b = after(zg_b, blocks)
-        blocks, a_sum, df_own = after((blocks, a_sum, df_own), zg_b)
-        blocks = [blocks[0]] + [over_dp(blocks[d], 4 * d) for d in (1, 2, 3)]
+        zg_a, zg_b = after((zg_a, zg_b), grad_input)
+        own_b, sent_b = add_z(own_b, after(zg_b, zg_a), small_b, False)
+        own, sent, a_small = add_x(pick, after(xk, sent_b), xg, a_small, True)
+        zg = over_dp(sent, 4)
+        zg_b = over_dp(sent_b, 8)
+        a_sum, small_3 = for_head(own_a, after(zg_a, sent), small_3)
+        df_own, inp_other_got = after((df_own, inp_other_got), a_sum)
         a_sum = over_head(a_sum)
         grad_input = place_grad(0, pick, df_own, inp_own, inp_other_got, pages, grad_input)
+        own, sent, a_small = add_z(after(own, grad_input), zg, a_small, True)
+        zg = over_dp(sent, 8)
         grad_in, grad_back, n2g, n2b, bias_back_sum, n1g, n1b, bias_out_sum, bias_in_sum = ff_last(
-            pick, after(zg_b, grad_input), a_sum, small_3
+            pick, after(own_b, sent), zg_b, a_sum, small_3
         )
         output = place_output(pick, after(out_own, grad_in), inp_other_got)
-        blocks = after(blocks, output)
-        grad_q, grad_k, grad_v, grad_box, grad_wo, bq_sum, bv_sum = attn_last(blocks, a_small)
+        own = after(own, output)
+        grad_q, grad_k, grad_v, grad_box, grad_wo, bq_sum, bv_sum = attn_last(own, zg, a_small)
         grad_back, grad_wo = grad_back.T, grad_wo.T
     else:
         scatter = lambda value, axis: lax.psum_scatter(

time: 241 us -> 233 us (0.967)
  starting transfers between devices: 41.1 us -> 26.7 us
  Pallas kernels: 154 us -> 159 us
    ppermute x21 -> x18, starting transfers between devices: 31.1 us -> 16.2 us  [over_dp(): return lax.ppermute(value, 'dp', swap_perm(shards_dp, flip))]
    pallas_call x2 -> x5, Pallas kernels: 4.32 us -> 10.1 us  [whole_call(): pl.pallas_call(kernel, grid=(1,), in_specs=[full(a) for a in args], out_s...]
    ppermute x8, waiting for transfers between devices: 4.53 us -> 8.89 us  [over_head(): return lax.ppermute(value, 'head', [(0, 1), (1, 0)])]
    ppermute x21 -> x18, waiting for transfers between devices: 30.6 us -> 28.5 us  [over_dp(): return lax.ppermute(value, 'dp', swap_perm(shards_dp, flip))]
  transfers between devices with their start and end apart: 29 -> 26, of which waited for: 10 -> 13; matrix products, arithmetic and copies ran while one was open for 2% -> 2% of each run, Pallas kernels for 51% -> 55%
where the time goes in v1:
time: 233 us; the launch traced here: 232 us
  Pallas kernels  159 us (68%)
  waiting for transfers between devices  37.4 us (16%)
  starting transfers between devices  26.7 us (11%)
  local copies, waits for them, and re-layouts  7.45 us (3%)
    pallas_call x2, Pallas kernels, attn_bwd(): pl.pallas_call(partial(attn_bwd_kernel, groups, box_groups, first), grid_...  42.3 us
    pallas_call x2, Pallas kernels, attn_fwd(): pl.pallas_call(partial(attn_fwd_kernel, groups, which_page), grid_spec=pl...  32.5 us
    ppermute x18, waiting for transfers between devices, over_dp(): return lax.ppermute(value, 'dp', swap_perm(shards_dp, flip))  28.5 us
    pallas_call x1, Pallas kernels, feed_forward(): pl.pallas_call(partial(ff_kernel, groups), grid_spec=pltpu.PrefetchScalar...  25 us
    ppermute x18, starting transfers between devices, over_dp(): return lax.ppermute(value, 'dp', swap_perm(shards_dp, flip))  16.2 us
    pallas_call x2, Pallas kernels, ff_grad(): pl.pallas_call(ff_keep_kernel, grid_spec=pltpu.PrefetchScalarGridSpec(num...  11.2 us
    ppermute x8, starting transfers between devices, over_head(): return lax.ppermute(value, 'head', [(0, 1), (1, 0)])  10.5 us
    pallas_call x3, Pallas kernels, add_x(): pl.pallas_call(partial(add_x_kernel, tailed), grid_spec=pltpu.PrefetchSca...  10.3 us
  transfers between devices with their start and end apart: 26, of which 13 were waited for; matrix products, arithmetic and copies ran while one was open for 2% of the time, Pallas kernels for 55%

profile of v1, /device:TPU:0, one launch (start us, length us, event | category | flops | bytes accessed | tf_op | source)
XLA Modules:
  0.0 232.2 jit_solution(10201684341909456845)
XLA Ops:
  1.9 3.0 %collective-permute-start.2 = (bf16[768,384]{1,0:T(8,128)(2,1)S(1)}, bf16[768,384]{1,0:T(8,128)(2,1)}, u32[]{:S(2)}, u32[]{:S(2)}) collective-permute-start(bf16[768,384]{1,0:T(8,128)(2,1)S(1)} %constant_dynamic-slice_fusion.1), channel_id=1, source_target_pairs={{0,1},{1,0},{2,3},{3,2},{4,5},{5,4},{6,7},{7,6},{8,9},{9,8},{10,11... | collective-permute-start | bytes 1769480 | tf_op jit(solution)/shard_map/ppermute | solution.py:1010
  9.3 16.3 %attn_fwd.2 = (bf16[512,768]{1,0:T(8,128)(2,1)}, bf16[6,512,512]{2,1,0:T(8,128)(2,1)}, bf16[512,384]{1,0:T(8,128)(2,1)}, bf16[512,384]{1,0:T(8,128)(2,1)}, bf16[...) custom-call(s32[9]{0:T(128)} %stack.39.pick, ...), custom_call_target="tpu_custom_call" | custom-call | flops 4328521728 | bytes 10000000 | tf_op jit(solution)/shard_map/attn_fwd/pallas_call | solution.py:165
  25.6 5.3 %collective-permute-done.3.wb0 = bf16[384,768]{1,0:T(8,128)(2,1)} collective-permute-done((bf16[384,768]{1,0:T(8,128)(2,1)}, bf16[384,768]{1,0:T(8,128)(2,1)}, u32[]{:S(2)}, u32[]{:S(2)}) %collective-permute-start.3) | collective-permute-done | bytes 589856 | tf_op jit(solution)/shard_map/ppermute | solution.py:1010
  36.3 16.2 %attn_fwd.3 = (bf16[512,768]{1,0:T(8,128)(2,1)}, bf16[6,512,512]{2,1,0:T(8,128)(2,1)}, bf16[512,384]{1,0:T(8,128)(2,1)}, bf16[512,384]{1,0:T(8,128)(2,1)}, bf16[...) custom-call(s32[9]{0:T(128)} %stack.39.pick, ...), custom_call_target="tpu_custom_call" | custom-call | flops 4328521728 | bytes 10000000 | tf_op jit(solution)/shard_map/attn_fwd/pallas_call | solution.py:165
  57.4 25.0 %feed_forward.1 = (bf16[512,768]{1,0:T(8,128)(2,1)}, bf16[512,768]{1,0:T(8,128)(2,1)}, bf16[2,2,384,512]{3,2,1,0:T(8,128)(2,1)}, bf16[2,4,512,768]{3,2,1,0:T(8,128)(2,1)}, f32[8,1536]{1,0:T(8,128)}) custom-call(s32[9]{0:T(128)} %stack.39.pick, bf16[1024,768]{1,0:T(8,128)(2,1)} %tok_ref.4, bf16[512,768]{1,0:T(8,128)(2,1)} %get-tuple-element.129.part_ref, ...), custom_call_target="tpu_custom_call" | custom-call | flops 9663676416 | bytes 22020096 | tf_op jit(solution)/shard_map/feed_forward/pallas_call | solution.py:556
  82.4 5.0 %ff_grad_send.2 = bf16[2,400,1536]{2,1,0:T(8,128)(2,1)} custom-call(s32[9]{0:T(128)} %stack.39.pick, bf16[2,2,384,512]{3,2,1,0:T(8,128)(2,1)} %get-tuple-element.136.lhs_ref, bf16[2,4,512,768]{3,2,1,0:T(8,128)(2,1)} %get-tuple-element.142.rhs_ref, f32[8,1536]{1,0:T(8,128)} %get-tuple-element.138.small_ref), custom_call_target="tpu_custom_call" | custom-call | flops 1207959552 | bytes 10000000 | tf_op jit(solution)/shard_map/ff_grad_send/pallas_call | solution.py:661
  87.6 5.1 %ff_grad_send.3 = bf16[2,400,1536]{2,1,0:T(8,128)(2,1)} custom-call(s32[9]{0:T(128)} %stack.39.pick, bf16[2,2,384,512]{3,2,1,0:T(8,128)(2,1)} %get-tuple-element.136.lhs_ref, bf16[2,4,512,768]{3,2,1,0:T(8,128)(2,1)} %get-tuple-element.142.rhs_ref, f32[8,1536]{1,0:T(8,128)} %get-tuple-element.138.small_ref), custom_call_target="tpu_custom_call" | custom-call | flops 1207959552 | bytes 10000000 | tf_op jit(solution)/shard_map/ff_grad_send/pallas_call | solution.py:661
  93.0 5.6 %ff_grad_keep.2 = (bf16[2,208,1536]{2,1,0:T(8,128)(2,1)}, bf16[2,192,1536]{2,1,0:T(8,128)(2,1)}, f32[8,1536]{1,0:T(8,128)}) custom-call(s32[9]{0:T(128)} %stack.39.pick, bf16[2,2,384,512]{3,2,1,0:T(8,128)(2,1)} %get-tuple-element.136.lhs_ref, bf16[2,4,512,768]{3,2,1,0:T(8,128)(2,1)} %get-tuple-element.142.rhs_ref, ...), custom_call_target="tpu_custom_call" | custom-call | flops 1207959552 | bytes 10000000 | tf_op jit(solution)/shard_map/ff_grad_keep/pallas_call | solution.py:674
  100.6 5.6 %ff_grad_keep.3 = (bf16[2,208,1536]{2,1,0:T(8,128)(2,1)}, bf16[2,192,1536]{2,1,0:T(8,128)(2,1)}, f32[8,1536]{1,0:T(8,128)}) custom-call(s32[9]{0:T(128)} %stack.39.pick, bf16[2,2,384,512]{3,2,1,0:T(8,128)(2,1)} %get-tuple-element.136.lhs_ref, bf16[2,4,512,768]{3,2,1,0:T(8,128)(2,1)} %get-tuple-element.142.rhs_ref, ...), custom_call_target="tpu_custom_call" | custom-call | flops 1207959552 | bytes 10000000 | tf_op jit(solution)/shard_map/ff_grad_keep/pallas_call | solution.py:674
  106.2 20.6 %attn_bwd.2 = (bf16[2,384,1920]{2,1,0:T(8,128)(2,1)}, f32[1,1920]{1,0:T(1,128)}, bf16[512,768]{1,0:T(8,128)(2,1)}) custom-call(s32[9]{0:T(128)} %stack.39.pick, bf16[512,768]{1,0:T(8,128)(2,1)} %get-tuple-element.209.refs_0_.df_ref, bf16[2,384,512]{2,1,0:T(8,128)(2,1)} %get-tuple-element.146.refs_1_, bf16[512,384]{1,0:T(8,128)(2,1)} %get-tuple-element.147.refs_2_, ...), custom_call_target="tpu_custom_call" | custom-call | flops 6543114240 | bytes 14000000 | tf_op jit(solution)/shard_map/attn_bwd/pallas_call | solution.py:341
  129.7 3.7 %add_x.3 = (bf16[2,96,1536]{2,1,0:T(8,128)(2,1)}, bf16[2,112,1536]{2,1,0:T(8,128)(2,1)}, f32[8,1536]{1,0:T(8,128)}) custom-call(s32[9]{0:T(128)} %stack.39.pick, bf16[2,192,1536]{2,1,0:T(8,128)(2,1)} %get-tuple-element.156.keep_ref, bf16[2,208,1536]{2,1,0:T(8,128)(2,1)} %collective-permute-done.12.got_ref, f32[8,1536]{1,0:T(8,128)} %get-tuple-element.159.small_ref), custom_call_target="tpu_custom_call" | custom-call | flops 589824 | bytes 3538944 | tf_op jit(solution)/shard_map/add_x/pallas_call | solution.py:777
  135.3 21.7 %attn_bwd.3 = (bf16[400,1920]{1,0:T(8,128)(2,1)}, bf16[384,1920]{1,0:T(8,128)(2,1)}, f32[1,1920]{1,0:T(1,128)}, bf16[1024,768]{1,0:T(8,128)(2,1)}) custom-call(s32[9]{0:T(128)} %stack.39.pick, bf16[512,768]{1,0:T(8,128)(2,1)} %collective-permute-done.13.refs_0_.df_ref, bf16[2,384,512]{2,1,0:T(8,128)(2,1)} %get-tuple-element.162.refs_1_, ...), custom_call_target="tpu_custom_call" | custom-call | flops 6543114240 | bytes 14000000 | tf_op jit(solution)/shard_map/attn_bwd/pallas_call | solution.py:341
  161.2 3.5 %add_x.4 = (bf16[2,96,1536]{2,1,0:T(8,128)(2,1)}, bf16[2,96,1536]{2,1,0:T(8,128)(2,1)}) custom-call(s32[9]{0:T(128)} %stack.39.pick, bf16[2,192,1536]{2,1,0:T(8,128)(2,1)} %get-tuple-element.185.keep_ref, bf16[2,208,1536]{2,1,0:T(8,128)(2,1)} %collective-permute-done.14.got_ref, f32[8,1536]{1,0:T(8,128)} %get-tuple-element.186.small_ref), custom_call_target="tpu_custom_call" | custom-call | flops 589824 | bytes 3538944 | tf_op jit(solution)/shard_map/add_x/pallas_call | solution.py:777
  169.3 4.7 %attn_split.1 = (bf16[1,208,1920]{2,1,0:T(8,128)(2,1)}, bf16[1,192,1920]{2,1,0:T(8,128)(2,1)}, f32[8,1920]{1,0:T(8,128)}) custom-call(s32[9]{0:T(128)} %stack.39.pick, bf16[384,1920]{1,0:T(8,128)(2,1)} %get-tuple-element.189.kept_ref, bf16[400,1920]{1,0:T(8,128)(2,1)} %collective-permute-done.19.got_ref, f32[1,1920]{1,0:T(1,128)} %get-tuple-element.192.small_ref), custom_call_target="tpu_custom_call" | custom-call | flops 737280 | bytes 4423680 | tf_op jit(solution)/shard_map/attn_split/pallas_call | solution.py:721
  174.5 3.3 %place_grad.2.refs_0_ = f32[1024,768]{1,0:T(8,128)} custom-call(s32[9]{0:T(128)} %stack.39.pick, bf16[512,768]{1,0:T(8,128)(2,1)} %collective-permute-done.13.refs_0_.df_ref, bf16[1024,768]{1,0:T(8,128)(2,1)} %get-tuple-element.176.a_ref, bf16[512,768]{1,0:T(8,128)(2,1)} %collective-permute-done.16.b_ref), custom_call_target="tpu_custom_call" | custom-call | flops 1179648 | bytes 3932160 | tf_op jit(solution)/shard_map/place_grad/pallas_call | solution.py:909
  177.7 9.5 %collective-permute-done.17.got = bf16[2,64,1536]{2,1,0:T(8,128)(2,1)} collective-permute-done((bf16[2,64,1536]{2,1,0:T(8,128)(2,1)}, bf16[2,64,1536]{2,1,0:T(8,128)(2,1)}, u32[]{:S(2)}, u32[]{:S(2)}) %collective-permute-start.17) | collective-permute-done | bytes 393248 | tf_op jit(solution)/shard_map/ppermute | solution.py:1013
  194.5 3.1 %add_x.5 = (bf16[1,96,1920]{2,1,0:T(8,128)(2,1)}, bf16[1,112,1920]{2,1,0:T(8,128)(2,1)}, f32[8,1920]{1,0:T(8,128)}) custom-call(s32[9]{0:T(128)} %stack.39.pick, bf16[1,192,1920]{2,1,0:T(8,128)(2,1)} %get-tuple-element.201.keep_ref, bf16[1,208,1920]{2,1,0:T(8,128)(2,1)} %copy-done, f32[8,1920]{1,0:T(8,128)} %get-tuple-element.202.small_ref), custom_call_target="tpu_custom_call" | custom-call | flops 368640 | bytes 2211840 | tf_op jit(solution)/shard_map/add_x/pallas_call | solution.py:777
  201.8 3.5 %collective-permute-done.21.b_ref = bf16[1024,768]{1,0:T(8,128)(2,1)} collective-permute-done((bf16[1024,768]{1,0:T(8,128)(2,1)}, bf16[1024,768]{1,0:T(8,128)(2,1)}, u32[]{:S(2)}, u32[]{:S(2)}) %collective-permute-start.21) | collective-permute-done | bytes 1572896 | tf_op jit(solution)/shard_map/ppermute | solution.py:1010
  205.4 3.3 %place_grad.3 = f32[1024,768]{1,0:T(8,128)} custom-call(s32[9]{0:T(128)} %stack.39.pick, bf16[512,768]{1,0:T(8,128)(2,1)} %get-tuple-element.209.refs_0_.df_ref, bf16[512,768]{1,0:T(8,128)(2,1)} %get-tuple-element.175.a_ref, bf16[1024,768]{1,0:T(8,128)(2,1)} %collective-permute-done.21.b_ref, ...), custom_call_target="tpu_custom_call", output_to_operand_aliasing={{}: (4, {})} | custom-call | flops 1179648 | bytes 3932160 | tf_op jit(solution)/shard_map/place_grad/pallas_call | solution.py:909
  208.7 4.0 %collective-permute-done.22.got_ref = bf16[1,112,1920]{2,1,0:T(8,128)(2,1)S(1)} collective-permute-done((bf16[1,112,1920]{2,1,0:T(8,128)(2,1)}, bf16[1,112,1920]{2,1,0:T(8,128)(2,1)S(1)}, u32[]{:S(2)}, u32[]{:S(2)}) %collective-permute-start.22) | collective-permute-done | bytes 430112 | tf_op jit(solution)/shard_map/ppermute | solution.py:1013
  215.4 3.5 %collective-permute-start.25 = (bf16[1,64,1920]{2,1,0:T(8,128)(2,1)}, bf16[1,64,1920]{2,1,0:T(8,128)(2,1)S(1)}, u32[]{:S(2)}, u32[]{:S(2)}) collective-permute-start(bf16[1,64,1920]{2,1,0:T(8,128)(2,1)} %get-tuple-element.213), channel_id=1, source_target_pairs={{0,16},{2,18},{4,20},{6,22},{8,24},{10,26},{12,28},{14,30},{16,0},... | collective-permute-start | bytes 737288 | tf_op jit(solution)/shard_map/ppermute | solution.py:1013
  219.7 2.7 %ff_last.1 = (f32[48,1536]{1,0:T(8,128)}, f32[48,1536]{1,0:T(8,128)}, f32[768]{0:T(1024)}, f32[768]{0:T(1024)}, f32[768]{0:T(1024)}, /*index=5*/f32[768]{0:T(102...) custom-call(s32[9]{0:T(128)} %stack.39.pick, bf16[2,48,1536]{2,1,0:T(8,128)(2,1)} %get-tuple-element.214.own, ...), custom_call_target="tpu_custom_call" | custom-call | flops 1966080 | bytes 3932160 | tf_op jit(solution)/shard_map/ff_last/pallas_call | solution.py:862
  222.4 3.3 %place_output.1 = bf16[1024,768]{1,0:T(8,128)(2,1)} custom-call(s32[9]{0:T(128)} %stack.39.pick, bf16[512,768]{1,0:T(8,128)(2,1)} %get-tuple-element.217.refs_16_.a_ref, bf16[1024,768]{1,0:T(8,128)(2,1)} %collective-permute-done.21.b_ref), custom_call_target="tpu_custom_call" | custom-call | flops 393216 | bytes 3145728 | tf_op jit(solution)/shard_map/place_output/pallas_call | solution.py:936
  225.7 4.0 %collective-permute-done.25.got = bf16[1,64,1920]{2,1,0:T(8,128)(2,1)S(1)} collective-permute-done((bf16[1,64,1920]{2,1,0:T(8,128)(2,1)}, bf16[1,64,1920]{2,1,0:T(8,128)(2,1)S(1)}, u32[]{:S(2)}, u32[]{:S(2)}) %collective-permute-start.25) | collective-permute-done | bytes 245792 | tf_op jit(solution)/shard_map/ppermute | solution.py:1013
  (79 shorter events, 49.9 us)
Async XLA Ops:
  1.9 23.8 %collective-permute-start.2 = (bf16[768,384]{1,0:T(8,128)(2,1)S(1)}, bf16[768,384]{1,0:T(8,128)(2,1)}, u32[]{:S(2)}, u32[]{:S(2)}) collective-permute-start(bf16[768,384]{1,0:T(8,128)(2,1)S(1)} %constant_dynamic-slice_fusion.1), channel_id=1, source_target_pairs={{0,1},{1,0},{2,3},{3,2},{4,5},{5,4},{6,7},{7,6},{8,9},{9,8},{10,11... | collective-permute-start | bytes 1769480 | tf_op jit(solution)/shard_map/ppermute | solution.py:1010
  6.8 24.2 %collective-permute-start.3 = (bf16[384,768]{1,0:T(8,128)(2,1)}, bf16[384,768]{1,0:T(8,128)(2,1)}, u32[]{:S(2)}, u32[]{:S(2)}) collective-permute-start(bf16[384,768]{1,0:T(8,128)(2,1)} %constant_dynamic-slice_fusion), channel_id=1, source_target_pairs={{0,1},{1,0},{2,3},{3,2},{4,5},{5,4},{6,7},{7,6},{8,9},{9,8},{10,11... | collective-permute-start | bytes 1769480 | tf_op jit(solution)/shard_map/ppermute | solution.py:1010
  31.0 21.6 %collective-permute-start.5 = (bf16[768,384]{1,0:T(8,128)(2,1)}, bf16[768,384]{1,0:T(8,128)(2,1)}, u32[]{:S(2)}, u32[]{:S(2)}) collective-permute-start(bf16[768,384]{1,0:T(8,128)(2,1)} %collective-permute-done.2.wi0), channel_id=1, source_target_pairs={{0,4},{2,6},{4,0},{6,2},{8,12},{10,14},{12,8},{14,10},{16,20},{18,... | collective-permute-start | bytes 1769480 | tf_op jit(solution)/shard_map/ppermute | solution.py:1013
  32.7 20.4 %collective-permute-start.6 = (bf16[384,768]{1,0:T(8,128)(2,1)}, bf16[384,768]{1,0:T(8,128)(2,1)}, u32[]{:S(2)}, u32[]{:S(2)}) collective-permute-start(bf16[384,768]{1,0:T(8,128)(2,1)} %collective-permute-done.3.wb0), channel_id=1, source_target_pairs={{0,8},{2,10},{4,12},{6,14},{8,0},{10,2},{12,4},{14,6},{16,24},{18,... | collective-permute-start | bytes 1769480 | tf_op jit(solution)/shard_map/ppermute | solution.py:1013
  34.3 19.3 %collective-permute-start = (bf16[512,768]{1,0:T(8,128)(2,1)}, bf16[512,768]{1,0:T(8,128)(2,1)S(1)}, u32[]{:S(2)}, u32[]{:S(2)}) collective-permute-start(bf16[512,768]{1,0:T(8,128)(2,1)} %get-tuple-element.127), channel_id=1, source_target_pairs={{0,1},{1,0},{2,3},{3,2},{4,5},{5,4},{6,7},{7,6},{8,9},{9,8},{10,11... | collective-permute-start | bytes 2359304 | tf_op jit(solution)/shard_map/ppermute | solution.py:1010
  35.8 17.3 %collective-permute-start.1 = (bf16[1536]{0:T(1024)(128)(2,1)S(1)}, bf16[1536]{0:T(1024)(128)(2,1)S(1)}, u32[]{:S(2)}, u32[]{:S(2)}) collective-permute-start(bf16[1536]{0:T(1024)(128)(2,1)S(1)} %copy-done.8), channel_id=1, source_target_pairs={{0,1},{1,0},{2,3},{3,2},{4,5},{5,4},{6,7},{7,6},{8,9},{9,8},{10,11... | collective-permute-start | bytes 9224 | tf_op jit(solution)/shard_map/ppermute | solution.py:1010
  53.0 3.5 %collective-permute-start.7 = (bf16[768,384]{1,0:T(8,128)(2,1)}, bf16[768,384]{1,0:T(8,128)(2,1)}, u32[]{:S(2)}, u32[]{:S(2)}) collective-permute-start(bf16[768,384]{1,0:T(8,128)(2,1)} %collective-permute-done.5.wi2), channel_id=1, source_target_pairs={{0,2},{2,0},{4,6},{6,4},{8,10},{10,8},{12,14},{14,12},{16,18},{18,... | collective-permute-start | bytes 1769480 | tf_op jit(solution)/shard_map/ppermute | solution.py:1013
  53.1 4.3 %collective-permute-start.9 = (bf16[384,768]{1,0:T(8,128)(2,1)}, bf16[384,768]{1,0:T(8,128)(2,1)}, u32[]{:S(2)}, u32[]{:S(2)}) collective-permute-start(bf16[384,768]{1,0:T(8,128)(2,1)} %collective-permute-done.6.wb2), channel_id=1, source_target_pairs={{0,2},{2,0},{4,6},{6,4},{8,10},{10,8},{12,14},{14,12},{16,18},{18,... | collective-permute-start | bytes 1769480 | tf_op jit(solution)/shard_map/ppermute | solution.py:1013
  87.4 5.6 %collective-permute-start.10 = (bf16[2,400,1536]{2,1,0:T(8,128)(2,1)}, bf16[2,400,1536]{2,1,0:T(8,128)(2,1)}, u32[]{:S(2)}, u32[]{:S(2)}) collective-permute-start(bf16[2,400,1536]{2,1,0:T(8,128)(2,1)} %ff_grad_send.2), channel_id=1, source_target_pairs={{0,2},{2,0},{4,6},{6,4},{8,10},{10,8},{12,14},{14,12},{16,18},{18,... | collective-permute-start | bytes 7372808 | tf_op jit(solution)/shard_map/ppermute | solution.py:1013
  92.6 8.0 %collective-permute-start.11 = (bf16[2,400,1536]{2,1,0:T(8,128)(2,1)}, bf16[2,400,1536]{2,1,0:T(8,128)(2,1)}, u32[]{:S(2)}, u32[]{:S(2)}) collective-permute-start(bf16[2,400,1536]{2,1,0:T(8,128)(2,1)} %ff_grad_send.3), channel_id=1, source_target_pairs={{0,2},{2,0},{4,6},{6,4},{8,10},{10,8},{12,14},{14,12},{16,18},{18,... | collective-permute-start | bytes 7372808 | tf_op jit(solution)/shard_map/ppermute | solution.py:1013
  98.7 30.6 %collective-permute-start.12 = (bf16[2,208,1536]{2,1,0:T(8,128)(2,1)}, bf16[2,208,1536]{2,1,0:T(8,128)(2,1)}, u32[]{:S(2)}, u32[]{:S(2)}) collective-permute-start(bf16[2,208,1536]{2,1,0:T(8,128)(2,1)} %get-tuple-element.141), channel_id=1, source_target_pairs={{0,4},{2,6},{4,0},{6,2},{8,12},{10,14},{12,8},{14,10},{16,20},{18,... | collective-permute-start | bytes 3833864 | tf_op jit(solution)/shard_map/ppermute | solution.py:1013
  99.1 27.7 %collective-permute-start.13 = (bf16[512,768]{1,0:T(8,128)(2,1)S(1)}, bf16[512,768]{1,0:T(8,128)(2,1)}, u32[]{:S(2)}, u32[]{:S(2)}) collective-permute-start(bf16[512,768]{1,0:T(8,128)(2,1)S(1)} %copy-done.1), channel_id=1, source_target_pairs={{0,1},{1,0},{2,3},{3,2},{4,5},{5,4},{6,7},{7,6},{8,9},{9,8},{10,11... | collective-permute-start | bytes 2359304 | tf_op jit(solution)/shard_map/ppermute | solution.py:1010
  129.2 29.8 %collective-permute-start.14 = (bf16[2,208,1536]{2,1,0:T(8,128)(2,1)}, bf16[2,208,1536]{2,1,0:T(8,128)(2,1)}, u32[]{:S(2)}, u32[]{:S(2)}) collective-permute-start(bf16[2,208,1536]{2,1,0:T(8,128)(2,1)} %get-tuple-element.174), channel_id=1, source_target_pairs={{0,4},{2,6},{4,0},{6,2},{8,12},{10,14},{12,8},{14,10},{16,20},{18,... | collective-permute-start | bytes 3833864 | tf_op jit(solution)/shard_map/ppermute | solution.py:1013
  133.3 23.7 %collective-permute-start.16 = (bf16[512,768]{1,0:T(8,128)(2,1)S(1)}, bf16[512,768]{1,0:T(8,128)(2,1)}, u32[]{:S(2)}, u32[]{:S(2)}) collective-permute-start(bf16[512,768]{1,0:T(8,128)(2,1)S(1)} %copy-done.2), channel_id=1, source_target_pairs={{0,1},{1,0},{2,3},{3,2},{4,5},{5,4},{6,7},{7,6},{8,9},{9,8},{10,11... | collective-permute-start | bytes 2359304 | tf_op jit(solution)/shard_map/ppermute | solution.py:1010
  134.9 22.1 %collective-permute-start.15 = (bf16[2,112,1536]{2,1,0:T(8,128)(2,1)}, bf16[2,112,1536]{2,1,0:T(8,128)(2,1)}, u32[]{:S(2)}, u32[]{:S(2)}) collective-permute-start(bf16[2,112,1536]{2,1,0:T(8,128)(2,1)} %get-tuple-element.160), channel_id=1, source_target_pairs={{0,8},{2,10},{4,12},{6,14},{8,0},{10,2},{12,4},{14,6},{16,24},{18,... | collective-permute-start | bytes 2064392 | tf_op jit(solution)/shard_map/ppermute | solution.py:1013
  159.0 10.3 %collective-permute-start.19 = (bf16[400,1920]{1,0:T(8,128)(2,1)}, bf16[400,1920]{1,0:T(8,128)(2,1)}, u32[]{:S(2)}, u32[]{:S(2)}) collective-permute-start(bf16[400,1920]{1,0:T(8,128)(2,1)} %get-tuple-element.190), channel_id=1, source_target_pairs={{0,2},{2,0},{4,6},{6,4},{8,10},{10,8},{12,14},{14,12},{16,18},{18,... | collective-permute-start | bytes 4608008 | tf_op jit(solution)/shard_map/ppermute | solution.py:1013
  164.8 24.5 %collective-permute-start.18 = (bf16[2,96,1536]{2,1,0:T(8,128)(2,1)}, bf16[2,96,1536]{2,1,0:T(8,128)(2,1)}, u32[]{:S(2)}, u32[]{:S(2)}) collective-permute-start(bf16[2,96,1536]{2,1,0:T(8,128)(2,1)} %get-tuple-element.188), channel_id=1, source_target_pairs={{0,8},{2,10},{4,12},{6,14},{8,0},{10,2},{12,4},{14,6},{16,24},{18,... | collective-permute-start | bytes 1769480 | tf_op jit(solution)/shard_map/ppermute | solution.py:1013
  165.2 22.0 %collective-permute-start.17 = (bf16[2,64,1536]{2,1,0:T(8,128)(2,1)}, bf16[2,64,1536]{2,1,0:T(8,128)(2,1)}, u32[]{:S(2)}, u32[]{:S(2)}) collective-permute-start(bf16[2,64,1536]{2,1,0:T(8,128)(2,1)} %get-tuple-element.184), channel_id=1, source_target_pairs={{0,16},{2,18},{4,20},{6,22},{8,24},{10,26},{12,28},{14,30},{16,0},... | collective-permute-start | bytes 1179656 | tf_op jit(solution)/shard_map/ppermute | solution.py:1013
  167.8 37.6 %collective-permute-start.21 = (bf16[1024,768]{1,0:T(8,128)(2,1)}, bf16[1024,768]{1,0:T(8,128)(2,1)}, u32[]{:S(2)}, u32[]{:S(2)}) collective-permute-start(bf16[1024,768]{1,0:T(8,128)(2,1)} %get-tuple-element.176.a_ref), channel_id=1, source_target_pairs={{0,1},{1,0},{2,3},{3,2},{4,5},{5,4},{6,7},{7,6},{8,9},{9,8},{10,11... | collective-permute-start | bytes 4718600 | tf_op jit(solution)/shard_map/ppermute | solution.py:1010
  174.0 19.6 %collective-permute-start.20 = (bf16[1,208,1920]{2,1,0:T(8,128)(2,1)}, bf16[1,208,1920]{2,1,0:T(8,128)(2,1)S(1)}, u32[]{:S(2)}, u32[]{:S(2)}) collective-permute-start(bf16[1,208,1920]{2,1,0:T(8,128)(2,1)} %get-tuple-element.193), channel_id=1, source_target_pairs={{0,4},{2,6},{4,0},{6,2},{8,12},{10,14},{12,8},{14,10},{16,20},{18,... | collective-permute-start | bytes 2396168 | tf_op jit(solution)/shard_map/ppermute | solution.py:1013
  191.4 27.6 %collective-permute-start.23 = (bf16[2,48,1536]{2,1,0:T(8,128)(2,1)}, bf16[2,48,1536]{2,1,0:T(8,128)(2,1)}, u32[]{:S(2)}, u32[]{:S(2)}) collective-permute-start(bf16[2,48,1536]{2,1,0:T(8,128)(2,1)} %get-tuple-element.200), channel_id=1, source_target_pairs={{0,16},{2,18},{4,20},{6,22},{8,24},{10,26},{12,28},{14,30},{16,0},... | collective-permute-start | bytes 884744 | tf_op jit(solution)/shard_map/ppermute | solution.py:1013
  197.5 15.1 %collective-permute-start.22 = (bf16[1,112,1920]{2,1,0:T(8,128)(2,1)}, bf16[1,112,1920]{2,1,0:T(8,128)(2,1)S(1)}, u32[]{:S(2)}, u32[]{:S(2)}) collective-permute-start(bf16[1,112,1920]{2,1,0:T(8,128)(2,1)} %get-tuple-element.205), channel_id=1, source_target_pairs={{0,8},{2,10},{4,12},{6,14},{8,0},{10,2},{12,4},{14,6},{16,24},{18,... | collective-permute-start | bytes 1290248 | tf_op jit(solution)/shard_map/ppermute | solution.py:1013
  201.1 17.9 %collective-permute-start.24 = (bf16[2,64,1536]{2,1,0:T(8,128)(2,1)}, bf16[2,64,1536]{2,1,0:T(8,128)(2,1)S(1)}, u32[]{:S(2)}, u32[]{:S(2)}) collective-permute-start(bf16[2,64,1536]{2,1,0:T(8,128)(2,1)} %get-tuple-element.208), channel_id=1, source_target_pairs={{0,1},{1,0},{2,3},{3,2},{4,5},{5,4},{6,7},{7,6},{8,9},{9,8},{10,11... | collective-permute-start | bytes 1179656 | tf_op jit(solution)/shard_map/ppermute | solution.py:1010
  215.4 14.3 %collective-permute-start.25 = (bf16[1,64,1920]{2,1,0:T(8,128)(2,1)}, bf16[1,64,1920]{2,1,0:T(8,128)(2,1)S(1)}, u32[]{:S(2)}, u32[]{:S(2)}) collective-permute-start(bf16[1,64,1920]{2,1,0:T(8,128)(2,1)} %get-tuple-element.213), channel_id=1, source_target_pairs={{0,16},{2,18},{4,20},{6,22},{8,24},{10,26},{12,28},{14,30},{16,0},... | collective-permute-start | bytes 737288 | tf_op jit(solution)/shard_map/ppermute | solution.py:1013
  (12 other events, 62.5 us)

commit v2 on v1

--- a/solution.py
+++ b/solution.py
@@ -422,7 +422,7 @@
     bi_here, bi_there,
     wi_here, wb_here, wi0, wi1, wi2, wi3, wb0, wb1, wb2, wb3,
     out_ref, df_ref, lhs_ref, rhs_ref, small_ref,
-    wi, wb, slope, norm_low, grad_low, acc, wide, bi_ref, rhs, sems,
+    wi, wb, slope, norm_low, grad_low, acc, wide, bi_ref, rhs, gout_keep, out_keep, lhs, more_sems, sems,
 ):
     blocks, dim, cols = wi.shape
     here = blocks // 2
@@ -444,6 +444,13 @@
         else:
             pltpu.make_async_copy(source[1], wb.at[slot, span_back, :], sems.at[1, slot]).start()
 
+    fetch = pltpu.make_async_copy(
+        gout_ref.at[pl.ds(pl.multiple_of(pick[0] * gout_keep.shape[0], 8), gout_keep.shape[0]), :], gout_keep, more_sems.at[0]
+    )
+    fetch.start()
+    out_copy = pltpu.make_async_copy(out_keep, out_ref, more_sems.at[1])
+    lhs_copies = [pltpu.make_async_copy(lhs.at[m], lhs_ref.at[:, m], more_sems.at[2 + m]) for m in range(2)]
+
     def vec(ref):
         return ref[...].astype(F32).reshape(1, -1)
 
@@ -470,8 +477,9 @@
     acc[...] = jnp.zeros_like(acc)
     low_t = split_rows(low.T, groups)
     split = low_t.shape[0] // 2
-    lhs_ref[0, 0] = low_t[:split]
-    lhs_ref[1, 0] = low_t[split:]
+    lhs[0, 0] = low_t[:split]
+    lhs[0, 1] = low_t[split:]
+    lhs_copies[0].start()
 
     def leaving(m, j):
         return pltpu.make_async_copy(rhs.at[m, j], rhs_ref.at[m, j], sems.at[2 + m, j])
@@ -491,8 +499,10 @@
 
     lax.fori_loop(0, blocks, forward, 0)
     scaled2, inv2 = norm_stats(wide[...] + acc[...])
-    out_ref[...] = (scaled2 * g2 + b2).astype(BF16)
-    gout = gout_ref[...].astype(F32)
+    out_keep[...] = (scaled2 * g2 + b2).astype(BF16)
+    out_copy.start()
+    fetch.wait()
+    gout = gout_keep[...].astype(F32)
     small_gain2 = column_sum(gout * scaled2)
     small_bias2 = column_sum(gout)
     grad_second = norm_back(gout * g2, scaled2, inv2)
@@ -500,8 +510,9 @@
     low2 = grad_second.astype(BF16)
     grad_low[...] = low2
     low2_t = split_rows(low2.T, groups)
-    lhs_ref[0, 1] = low2_t[:split]
-    lhs_ref[1, 1] = low2_t[split:]
+    lhs[1, 0] = low2_t[:split]
+    lhs[1, 1] = low2_t[split:]
+    lhs_copies[1].start()
     acc[...] = grad_second
 
     def backward(j, _):
@@ -529,6 +540,8 @@
     for m in range(2):
         for j in range(blocks):
             leaving(m, j).wait()
+    for copy in [out_copy, *lhs_copies]:
+        copy.wait()
     small_ref[...] = jnp.concatenate(
         [
             jnp.concatenate([small_gain2, small_bias2], axis=1),
@@ -562,15 +575,15 @@
                 pl.BlockSpec((length, dim), page),
                 whole,
                 whole,
-                pl.BlockSpec((length, dim), page),
+                anywhere,
                 row, row, row, row, row, row,
                 bias_row, bias_row,
             ]
             + [anywhere] * 10,
             out_specs=[
+                anywhere,
                 whole,
-                whole,
-                pl.BlockSpec((2, 2, dim // 2, length), lambda i, pick: (0, 0, 0, 0)),
+                anywhere,
                 anywhere,
                 pl.BlockSpec((8, 2 * dim), fixed),
             ],
@@ -584,6 +597,10 @@
                 pltpu.VMEM((length, dim), F32),
                 pltpu.VMEM((blocks, cols), F32),
                 pltpu.VMEM((2, blocks, length, cols), BF16),
+                pltpu.VMEM((length, dim), BF16),
+                pltpu.VMEM((length, dim), BF16),
+                pltpu.VMEM((2, 2, dim // 2, length), BF16),
+                pltpu.SemaphoreType.DMA((4,)),
                 pltpu.SemaphoreType.DMA((4, 2 * blocks)),
             ],
         ),
@@ -600,7 +617,7 @@
     )(pick, tokens, part, got, grad_out, *rows, bias_in, bias_there, wi_here, wb_here, *wi_pieces, *wb_pieces)
 
 
-TAIL = 16
+TAIL = 8
 
 
 def split2(x):
@@ -614,6 +631,8 @@
 
 
 def tall(x):
+    if x.shape[0] == TAIL:
+        return x
     return jnp.concatenate([x, jnp.zeros((TAIL - x.shape[0],) + x.shape[1:], x.dtype)], axis=0)
 
 
@@ -1032,11 +1051,12 @@
 
     part_other, *saved_other = attend(1, tokens)
     got = over_head(part_other)
-    in_first, back_first = after((in_first, back_first), part_other)
+    in_first, back_first, bias_there = after((in_first, back_first, bias_there), part_other)
     in_second, back_second = over_dp(in_first, 2), over_dp(back_first, 4)
     in_near, back_near = over_dp(in_first, 1), over_dp(back_first, 1)
-    part_own, *saved_own = attend(0, after(tokens, part_other))
-    in_second, back_second = after((in_second, back_second), part_own)
+    part_own, *saved_own = attend(0, after(tokens, bias_there))
+    in_near, back_near = after((in_near, back_near), part_own)
+    in_second, back_second = after((in_second, back_second), in_near, back_near)
     in_pieces = [in_first, in_near, in_second, over_dp(in_second, 1)]
     back_pieces = [back_first, back_near, back_second, over_dp(back_second, 1)]
 

time: 233 us -> 225 us (0.966)
  waiting for transfers between devices: 37.4 us -> 30.5 us
    ppermute x18, waiting for transfers between devices: 28.5 us -> 21.5 us  [over_dp(): return lax.ppermute(value, 'dp', swap_perm(shards_dp, flip))]
  transfers between devices with their start and end apart: 26 -> 26, of which waited for: 13 -> 12; matrix products, arithmetic and copies ran while one was open for 2% -> 2% of each run, Pallas kernels for 55% -> 56%
where the time goes in v2:
time: 225 us; the launch traced here: 224 us
  Pallas kernels  157 us (70%)
  waiting for transfers between devices  30.5 us (14%)
  starting transfers between devices  27.4 us (12%)
  local copies, waits for them, and re-layouts  7.39 us (3%)
    pallas_call x2, Pallas kernels, attn_bwd(): pl.pallas_call(partial(attn_bwd_kernel, groups, box_groups, first), grid_...  42.2 us
    pallas_call x2, Pallas kernels, attn_fwd(): pl.pallas_call(partial(attn_fwd_kernel, groups, which_page), grid_spec=pl...  32.3 us
    pallas_call x1, Pallas kernels, feed_forward(): pl.pallas_call(partial(ff_kernel, groups), grid_spec=pltpu.PrefetchScalar...  24 us
    ppermute x18, waiting for transfers between devices, over_dp(): return lax.ppermute(value, 'dp', swap_perm(shards_dp, flip))  21.5 us
    ppermute x18, starting transfers between devices, over_dp(): return lax.ppermute(value, 'dp', swap_perm(shards_dp, flip))  17.4 us
    pallas_call x2, Pallas kernels, ff_grad(): pl.pallas_call(ff_keep_kernel, grid_spec=pltpu.PrefetchScalarGridSpec(num...  11.2 us
    pallas_call x3, Pallas kernels, add_x(): pl.pallas_call(partial(add_x_kernel, tailed), grid_spec=pltpu.PrefetchSca...  10.1 us
    ppermute x8, starting transfers between devices, over_head(): return lax.ppermute(value, 'head', [(0, 1), (1, 0)])  10 us
  transfers between devices with their start and end apart: 26, of which 12 were waited for; matrix products, arithmetic and copies ran while one was open for 2% of the time, Pallas kernels for 56%

profile of v2, /device:TPU:0, one launch (start us, length us, event | category | flops | bytes accessed | tf_op | source)
XLA Modules:
  0.0 224.4 jit_solution(7146635504107020893)
XLA Ops:
  1.9 3.0 %collective-permute-start = (bf16[768,384]{1,0:T(8,128)(2,1)S(1)}, bf16[768,384]{1,0:T(8,128)(2,1)}, u32[]{:S(2)}, u32[]{:S(2)}) collective-permute-start(bf16[768,384]{1,0:T(8,128)(2,1)S(1)} %constant_dynamic-slice_fusion.1), channel_id=1, source_target_pairs={{0,1},{1,0},{2,3},{3,2},{4,5},{5,4},{6,7},{7,6},{8,9},{9,8},{10,11... | collective-permute-start | bytes 1769480 | tf_op jit(solution)/shard_map/ppermute | solution.py:1029
  11.3 16.2 %attn_fwd.2 = (bf16[512,768]{1,0:T(8,128)(2,1)}, bf16[6,512,512]{2,1,0:T(8,128)(2,1)}, bf16[512,384]{1,0:T(8,128)(2,1)}, bf16[512,384]{1,0:T(8,128)(2,1)}, bf16[...) custom-call(s32[9]{0:T(128)} %stack.39.pick, ...), custom_call_target="tpu_custom_call" | custom-call | flops 4328521728 | bytes 10000000 | tf_op jit(solution)/shard_map/attn_fwd/pallas_call | solution.py:165
  27.5 3.6 %collective-permute-done.2.bi_there = bf16[1536]{0:T(1024)(128)(2,1)S(1)} collective-permute-done((bf16[1536]{0:T(1024)(128)(2,1)S(1)}, bf16[1536]{0:T(1024)(128)(2,1)S(1)}, u32[]{:S(2)}, u32[]{:S(2)}) %collective-permute-start.2) | collective-permute-done | bytes 3104 | tf_op jit(solution)/shard_map/ppermute | solution.py:1029
  36.4 16.2 %attn_fwd.3 = (bf16[512,768]{1,0:T(8,128)(2,1)}, bf16[6,512,512]{2,1,0:T(8,128)(2,1)}, bf16[512,384]{1,0:T(8,128)(2,1)}, bf16[512,384]{1,0:T(8,128)(2,1)}, bf16[...) custom-call(s32[9]{0:T(128)} %stack.39.pick, ...), custom_call_target="tpu_custom_call" | custom-call | flops 4328521728 | bytes 10000000 | tf_op jit(solution)/shard_map/attn_fwd/pallas_call | solution.py:165
  55.9 24.0 %feed_forward.1 = (bf16[512,768]{1,0:T(8,128)(2,1)}, bf16[512,768]{1,0:T(8,128)(2,1)}, bf16[2,2,384,512]{3,2,1,0:T(8,128)(2,1)}, bf16[2,4,512,768]{3,2,1,0:T(8,128)(2,1)}, f32[8,1536]{1,0:T(8,128)}) custom-call(s32[9]{0:T(128)} %stack.39.pick, bf16[1024,768]{1,0:T(8,128)(2,1)} %tok_ref.4, bf16[512,768]{1,0:T(8,128)(2,1)} %get-tuple-element.133.part_ref, ...), custom_call_target="tpu_custom_call" | custom-call | flops 9663676416 | bytes 22020096 | tf_op jit(solution)/shard_map/feed_forward/pallas_call | solution.py:569
  80.0 5.0 %ff_grad_send.2 = bf16[2,392,1536]{2,1,0:T(8,128)(2,1)} custom-call(s32[9]{0:T(128)} %stack.39.pick, bf16[2,2,384,512]{3,2,1,0:T(8,128)(2,1)} %get-tuple-element.142.lhs_ref, bf16[2,4,512,768]{3,2,1,0:T(8,128)(2,1)} %get-tuple-element.148.rhs_ref, f32[8,1536]{1,0:T(8,128)} %get-tuple-element.144.small_ref), custom_call_target="tpu_custom_call" | custom-call | flops 1207959552 | bytes 10000000 | tf_op jit(solution)/shard_map/ff_grad_send/pallas_call | solution.py:680
  85.1 5.0 %ff_grad_send.3 = bf16[2,392,1536]{2,1,0:T(8,128)(2,1)} custom-call(s32[9]{0:T(128)} %stack.39.pick, bf16[2,2,384,512]{3,2,1,0:T(8,128)(2,1)} %get-tuple-element.142.lhs_ref, bf16[2,4,512,768]{3,2,1,0:T(8,128)(2,1)} %get-tuple-element.148.rhs_ref, f32[8,1536]{1,0:T(8,128)} %get-tuple-element.144.small_ref), custom_call_target="tpu_custom_call" | custom-call | flops 1207959552 | bytes 10000000 | tf_op jit(solution)/shard_map/ff_grad_send/pallas_call | solution.py:680
  90.5 5.6 %ff_grad_keep.2 = (bf16[2,200,1536]{2,1,0:T(8,128)(2,1)}, bf16[2,192,1536]{2,1,0:T(8,128)(2,1)}, f32[8,1536]{1,0:T(8,128)}) custom-call(s32[9]{0:T(128)} %stack.39.pick, bf16[2,2,384,512]{3,2,1,0:T(8,128)(2,1)} %get-tuple-element.142.lhs_ref, bf16[2,4,512,768]{3,2,1,0:T(8,128)(2,1)} %get-tuple-element.148.rhs_ref, ...), custom_call_target="tpu_custom_call" | custom-call | flops 1207959552 | bytes 10000000 | tf_op jit(solution)/shard_map/ff_grad_keep/pallas_call | solution.py:693
  97.2 5.5 %ff_grad_keep.3 = (bf16[2,200,1536]{2,1,0:T(8,128)(2,1)}, bf16[2,192,1536]{2,1,0:T(8,128)(2,1)}, f32[8,1536]{1,0:T(8,128)}) custom-call(s32[9]{0:T(128)} %stack.39.pick, bf16[2,2,384,512]{3,2,1,0:T(8,128)(2,1)} %get-tuple-element.142.lhs_ref, bf16[2,4,512,768]{3,2,1,0:T(8,128)(2,1)} %get-tuple-element.148.rhs_ref, ...), custom_call_target="tpu_custom_call" | custom-call | flops 1207959552 | bytes 10000000 | tf_op jit(solution)/shard_map/ff_grad_keep/pallas_call | solution.py:693
  102.8 20.6 %attn_bwd.2 = (bf16[2,384,1920]{2,1,0:T(8,128)(2,1)}, f32[1,1920]{1,0:T(1,128)}, bf16[512,768]{1,0:T(8,128)(2,1)}) custom-call(s32[9]{0:T(128)} %stack.39.pick, bf16[512,768]{1,0:T(8,128)(2,1)} %get-tuple-element.215.refs_0_.df_ref, bf16[2,384,512]{2,1,0:T(8,128)(2,1)} %get-tuple-element.152.refs_1_, bf16[512,384]{1,0:T(8,128)(2,1)} %get-tuple-element.153.refs_2_, ...), custom_call_target="tpu_custom_call" | custom-call | flops 6543114240 | bytes 14000000 | tf_op jit(solution)/shard_map/attn_bwd/pallas_call | solution.py:341
  126.1 3.6 %add_x.3 = (bf16[2,96,1536]{2,1,0:T(8,128)(2,1)}, bf16[2,104,1536]{2,1,0:T(8,128)(2,1)}, f32[8,1536]{1,0:T(8,128)}) custom-call(s32[9]{0:T(128)} %stack.39.pick, bf16[2,192,1536]{2,1,0:T(8,128)(2,1)} %get-tuple-element.162.keep_ref, bf16[2,200,1536]{2,1,0:T(8,128)(2,1)} %collective-permute-done.12.got_ref, f32[8,1536]{1,0:T(8,128)} %get-tuple-element.165.small_ref), custom_call_target="tpu_custom_call" | custom-call | flops 589824 | bytes 3538944 | tf_op jit(solution)/shard_map/add_x/pallas_call | solution.py:796
  130.6 21.7 %attn_bwd.3 = (bf16[392,1920]{1,0:T(8,128)(2,1)}, bf16[384,1920]{1,0:T(8,128)(2,1)}, f32[1,1920]{1,0:T(1,128)}, bf16[1024,768]{1,0:T(8,128)(2,1)}) custom-call(s32[9]{0:T(128)} %stack.39.pick, bf16[512,768]{1,0:T(8,128)(2,1)} %collective-permute-done.13.refs_0_.df_ref, bf16[2,384,512]{2,1,0:T(8,128)(2,1)} %get-tuple-element.168.refs_1_, ...), custom_call_target="tpu_custom_call" | custom-call | flops 6543114240 | bytes 14000000 | tf_op jit(solution)/shard_map/attn_bwd/pallas_call | solution.py:341
  156.6 3.5 %add_x.4 = (bf16[2,96,1536]{2,1,0:T(8,128)(2,1)}, bf16[2,96,1536]{2,1,0:T(8,128)(2,1)}) custom-call(s32[9]{0:T(128)} %stack.39.pick, bf16[2,192,1536]{2,1,0:T(8,128)(2,1)} %get-tuple-element.191.keep_ref, bf16[2,200,1536]{2,1,0:T(8,128)(2,1)} %collective-permute-done.14.got_ref, f32[8,1536]{1,0:T(8,128)} %get-tuple-element.192.small_ref), custom_call_target="tpu_custom_call" | custom-call | flops 589824 | bytes 3538944 | tf_op jit(solution)/shard_map/add_x/pallas_call | solution.py:796
  160.5 2.6 %collective-permute-start.17 = (bf16[2,56,1536]{2,1,0:T(8,128)(2,1)}, bf16[2,56,1536]{2,1,0:T(8,128)(2,1)}, u32[]{:S(2)}, u32[]{:S(2)}) collective-permute-start(bf16[2,56,1536]{2,1,0:T(8,128)(2,1)} %get-tuple-element.190), channel_id=1, source_target_pairs={{0,16},{2,18},{4,20},{6,22},{8,24},{10,26},{12,28},{14,30},{16,0},... | collective-permute-start | bytes 1032200 | tf_op jit(solution)/shard_map/ppermute | solution.py:1032
  163.8 4.6 %attn_split.1 = (bf16[1,200,1920]{2,1,0:T(8,128)(2,1)}, bf16[1,192,1920]{2,1,0:T(8,128)(2,1)}, f32[8,1920]{1,0:T(8,128)}) custom-call(s32[9]{0:T(128)} %stack.39.pick, bf16[384,1920]{1,0:T(8,128)(2,1)} %get-tuple-element.195.kept_ref, bf16[392,1920]{1,0:T(8,128)(2,1)} %collective-permute-done.19.got_ref, f32[1,1920]{1,0:T(1,128)} %get-tuple-element.198.small_ref), custom_call_target="tpu_custom_call" | custom-call | flops 737280 | bytes 4423680 | tf_op jit(solution)/shard_map/attn_split/pallas_call | solution.py:740
  170.0 3.3 %place_grad.2.refs_0_ = f32[1024,768]{1,0:T(8,128)} custom-call(s32[9]{0:T(128)} %stack.39.pick, bf16[512,768]{1,0:T(8,128)(2,1)} %collective-permute-done.13.refs_0_.df_ref, bf16[1024,768]{1,0:T(8,128)(2,1)} %get-tuple-element.182.a_ref, bf16[512,768]{1,0:T(8,128)(2,1)} %collective-permute-done.16.b_ref), custom_call_target="tpu_custom_call" | custom-call | flops 1179648 | bytes 3932160 | tf_op jit(solution)/shard_map/place_grad/pallas_call | solution.py:928
  173.3 8.1 %collective-permute-done.17.got = bf16[2,56,1536]{2,1,0:T(8,128)(2,1)} collective-permute-done((bf16[2,56,1536]{2,1,0:T(8,128)(2,1)}, bf16[2,56,1536]{2,1,0:T(8,128)(2,1)}, u32[]{:S(2)}, u32[]{:S(2)}) %collective-permute-start.17) | collective-permute-done | bytes 344096 | tf_op jit(solution)/shard_map/ppermute | solution.py:1032
  188.3 3.0 %add_x.5 = (bf16[1,96,1920]{2,1,0:T(8,128)(2,1)}, bf16[1,104,1920]{2,1,0:T(8,128)(2,1)}, f32[8,1920]{1,0:T(8,128)}) custom-call(s32[9]{0:T(128)} %stack.39.pick, bf16[1,192,1920]{2,1,0:T(8,128)(2,1)} %get-tuple-element.207.keep_ref, bf16[1,200,1920]{2,1,0:T(8,128)(2,1)} %copy-done.2, f32[8,1920]{1,0:T(8,128)} %get-tuple-element.208.small_ref), custom_call_target="tpu_custom_call" | custom-call | flops 368640 | bytes 2211840 | tf_op jit(solution)/shard_map/add_x/pallas_call | solution.py:796
  196.1 4.6 %collective-permute-done.21.b_ref = bf16[1024,768]{1,0:T(8,128)(2,1)} collective-permute-done((bf16[1024,768]{1,0:T(8,128)(2,1)}, bf16[1024,768]{1,0:T(8,128)(2,1)}, u32[]{:S(2)}, u32[]{:S(2)}) %collective-permute-start.21) | collective-permute-done | bytes 1572896 | tf_op jit(solution)/shard_map/ppermute | solution.py:1029
  200.7 3.3 %place_grad.3 = f32[1024,768]{1,0:T(8,128)} custom-call(s32[9]{0:T(128)} %stack.39.pick, bf16[512,768]{1,0:T(8,128)(2,1)} %get-tuple-element.215.refs_0_.df_ref, bf16[512,768]{1,0:T(8,128)(2,1)} %get-tuple-element.181.a_ref, bf16[1024,768]{1,0:T(8,128)(2,1)} %collective-permute-done.21.b_ref, ...), custom_call_target="tpu_custom_call", output_to_operand_aliasing={{}: (4, {})} | custom-call | flops 1179648 | bytes 3932160 | tf_op jit(solution)/shard_map/place_grad/pallas_call | solution.py:928
  208.6 3.8 %collective-permute-start.25 = (bf16[1,56,1920]{2,1,0:T(8,128)(2,1)}, bf16[1,56,1920]{2,1,0:T(8,128)(2,1)S(1)}, u32[]{:S(2)}, u32[]{:S(2)}) collective-permute-start(bf16[1,56,1920]{2,1,0:T(8,128)(2,1)} %get-tuple-element.219), channel_id=1, source_target_pairs={{0,16},{2,18},{4,20},{6,22},{8,24},{10,26},{12,28},{14,30},{16,0},... | collective-permute-start | bytes 645128 | tf_op jit(solution)/shard_map/ppermute | solution.py:1032
  213.2 2.7 %ff_last.1 = (f32[48,1536]{1,0:T(8,128)}, f32[48,1536]{1,0:T(8,128)}, f32[768]{0:T(1024)}, f32[768]{0:T(1024)}, f32[768]{0:T(1024)}, /*index=5*/f32[768]{0:T(102...) custom-call(s32[9]{0:T(128)} %stack.39.pick, bf16[2,48,1536]{2,1,0:T(8,128)(2,1)} %get-tuple-element.220.own, ...), custom_call_target="tpu_custom_call" | custom-call | flops 1720320 | bytes 3440640 | tf_op jit(solution)/shard_map/ff_last/pallas_call | solution.py:881
  215.9 3.3 %place_output.1 = bf16[1024,768]{1,0:T(8,128)(2,1)} custom-call(s32[9]{0:T(128)} %stack.39.pick, bf16[512,768]{1,0:T(8,128)(2,1)} %get-tuple-element.223.refs_16_.a_ref, bf16[1024,768]{1,0:T(8,128)(2,1)} %collective-permute-done.21.b_ref), custom_call_target="tpu_custom_call" | custom-call | flops 393216 | bytes 3145728 | tf_op jit(solution)/shard_map/place_output/pallas_call | solution.py:955
  219.2 2.8 %collective-permute-done.25.got = bf16[1,56,1920]{2,1,0:T(8,128)(2,1)S(1)} collective-permute-done((bf16[1,56,1920]{2,1,0:T(8,128)(2,1)}, bf16[1,56,1920]{2,1,0:T(8,128)(2,1)S(1)}, u32[]{:S(2)}, u32[]{:S(2)}) %collective-permute-start.25) | collective-permute-done | bytes 215072 | tf_op jit(solution)/shard_map/ppermute | solution.py:1032
  (79 shorter events, 47.8 us)
Async XLA Ops:
  1.9 29.2 %collective-permute-start = (bf16[768,384]{1,0:T(8,128)(2,1)S(1)}, bf16[768,384]{1,0:T(8,128)(2,1)}, u32[]{:S(2)}, u32[]{:S(2)}) collective-permute-start(bf16[768,384]{1,0:T(8,128)(2,1)S(1)} %constant_dynamic-slice_fusion.1), channel_id=1, source_target_pairs={{0,1},{1,0},{2,3},{3,2},{4,5},{5,4},{6,7},{7,6},{8,9},{9,8},{10,11... | collective-permute-start | bytes 1769480 | tf_op jit(solution)/shard_map/ppermute | solution.py:1029
  6.8 24.2 %collective-permute-start.1 = (bf16[384,768]{1,0:T(8,128)(2,1)}, bf16[384,768]{1,0:T(8,128)(2,1)}, u32[]{:S(2)}, u32[]{:S(2)}) collective-permute-start(bf16[384,768]{1,0:T(8,128)(2,1)} %constant_dynamic-slice_fusion), channel_id=1, source_target_pairs={{0,1},{1,0},{2,3},{3,2},{4,5},{5,4},{6,7},{7,6},{8,9},{9,8},{10,11... | collective-permute-start | bytes 1769480 | tf_op jit(solution)/shard_map/ppermute | solution.py:1029
  6.9 24.1 %collective-permute-start.2 = (bf16[1536]{0:T(1024)(128)(2,1)S(1)}, bf16[1536]{0:T(1024)(128)(2,1)S(1)}, u32[]{:S(2)}, u32[]{:S(2)}) collective-permute-start(bf16[1536]{0:T(1024)(128)(2,1)S(1)} %copy-done.8), channel_id=1, source_target_pairs={{0,1},{1,0},{2,3},{3,2},{4,5},{5,4},{6,7},{7,6},{8,9},{9,8},{10,11... | collective-permute-start | bytes 9224 | tf_op jit(solution)/shard_map/ppermute | solution.py:1029
  31.0 21.6 %collective-permute-start.4 = (bf16[768,384]{1,0:T(8,128)(2,1)}, bf16[768,384]{1,0:T(8,128)(2,1)}, u32[]{:S(2)}, u32[]{:S(2)}) collective-permute-start(bf16[768,384]{1,0:T(8,128)(2,1)} %collective-permute-done.wi0), channel_id=1, source_target_pairs={{0,2},{2,0},{4,6},{6,4},{8,10},{10,8},{12,14},{14,12},{16,18},{18,... | collective-permute-start | bytes 1769480 | tf_op jit(solution)/shard_map/ppermute | solution.py:1032
  31.1 21.5 %collective-permute-start.5 = (bf16[384,768]{1,0:T(8,128)(2,1)}, bf16[384,768]{1,0:T(8,128)(2,1)}, u32[]{:S(2)}, u32[]{:S(2)}) collective-permute-start(bf16[384,768]{1,0:T(8,128)(2,1)} %collective-permute-done.1.wb0), channel_id=1, source_target_pairs={{0,2},{2,0},{4,6},{6,4},{8,10},{10,8},{12,14},{14,12},{16,18},{18,... | collective-permute-start | bytes 1769480 | tf_op jit(solution)/shard_map/ppermute | solution.py:1032
  31.6 21.0 %collective-permute-start.6 = (bf16[768,384]{1,0:T(8,128)(2,1)}, bf16[768,384]{1,0:T(8,128)(2,1)}, u32[]{:S(2)}, u32[]{:S(2)}) collective-permute-start(bf16[768,384]{1,0:T(8,128)(2,1)} %collective-permute-done.wi0), channel_id=1, source_target_pairs={{0,4},{2,6},{4,0},{6,2},{8,12},{10,14},{12,8},{14,10},{16,20},{18,... | collective-permute-start | bytes 1769480 | tf_op jit(solution)/shard_map/ppermute | solution.py:1032
  33.3 19.3 %collective-permute-start.7 = (bf16[384,768]{1,0:T(8,128)(2,1)}, bf16[384,768]{1,0:T(8,128)(2,1)}, u32[]{:S(2)}, u32[]{:S(2)}) collective-permute-start(bf16[384,768]{1,0:T(8,128)(2,1)} %collective-permute-done.1.wb0), channel_id=1, source_target_pairs={{0,8},{2,10},{4,12},{6,14},{8,0},{10,2},{12,4},{14,6},{16,24},{18,... | collective-permute-start | bytes 1769480 | tf_op jit(solution)/shard_map/ppermute | solution.py:1032
  34.9 19.2 %collective-permute-start.3 = (bf16[512,768]{1,0:T(8,128)(2,1)}, bf16[512,768]{1,0:T(8,128)(2,1)S(1)}, u32[]{:S(2)}, u32[]{:S(2)}) collective-permute-start(bf16[512,768]{1,0:T(8,128)(2,1)} %get-tuple-element.130), channel_id=1, source_target_pairs={{0,1},{1,0},{2,3},{3,2},{4,5},{5,4},{6,7},{7,6},{8,9},{9,8},{10,11... | collective-permute-start | bytes 2359304 | tf_op jit(solution)/shard_map/ppermute | solution.py:1029
  85.0 5.5 %collective-permute-start.10 = (bf16[2,392,1536]{2,1,0:T(8,128)(2,1)}, bf16[2,392,1536]{2,1,0:T(8,128)(2,1)}, u32[]{:S(2)}, u32[]{:S(2)}) collective-permute-start(bf16[2,392,1536]{2,1,0:T(8,128)(2,1)} %ff_grad_send.2), channel_id=1, source_target_pairs={{0,2},{2,0},{4,6},{6,4},{8,10},{10,8},{12,14},{14,12},{16,18},{18,... | collective-permute-start | bytes 7225352 | tf_op jit(solution)/shard_map/ppermute | solution.py:1032
  90.1 7.1 %collective-permute-start.11 = (bf16[2,392,1536]{2,1,0:T(8,128)(2,1)}, bf16[2,392,1536]{2,1,0:T(8,128)(2,1)}, u32[]{:S(2)}, u32[]{:S(2)}) collective-permute-start(bf16[2,392,1536]{2,1,0:T(8,128)(2,1)} %ff_grad_send.3), channel_id=1, source_target_pairs={{0,2},{2,0},{4,6},{6,4},{8,10},{10,8},{12,14},{14,12},{16,18},{18,... | collective-permute-start | bytes 7225352 | tf_op jit(solution)/shard_map/ppermute | solution.py:1032
  96.1 29.5 %collective-permute-start.12 = (bf16[2,200,1536]{2,1,0:T(8,128)(2,1)}, bf16[2,200,1536]{2,1,0:T(8,128)(2,1)}, u32[]{:S(2)}, u32[]{:S(2)}) collective-permute-start(bf16[2,200,1536]{2,1,0:T(8,128)(2,1)} %get-tuple-element.147), channel_id=1, source_target_pairs={{0,4},{2,6},{4,0},{6,2},{8,12},{10,14},{12,8},{14,10},{16,20},{18,... | collective-permute-start | bytes 3686408 | tf_op jit(solution)/shard_map/ppermute | solution.py:1032
  96.6 26.7 %collective-permute-start.13 = (bf16[512,768]{1,0:T(8,128)(2,1)S(1)}, bf16[512,768]{1,0:T(8,128)(2,1)}, u32[]{:S(2)}, u32[]{:S(2)}) collective-permute-start(bf16[512,768]{1,0:T(8,128)(2,1)S(1)} %copy-done), channel_id=1, source_target_pairs={{0,1},{1,0},{2,3},{3,2},{4,5},{5,4},{6,7},{7,6},{8,9},{9,8},{10,11... | collective-permute-start | bytes 2359304 | tf_op jit(solution)/shard_map/ppermute | solution.py:1029
  125.7 28.7 %collective-permute-start.14 = (bf16[2,200,1536]{2,1,0:T(8,128)(2,1)}, bf16[2,200,1536]{2,1,0:T(8,128)(2,1)}, u32[]{:S(2)}, u32[]{:S(2)}) collective-permute-start(bf16[2,200,1536]{2,1,0:T(8,128)(2,1)} %get-tuple-element.180), channel_id=1, source_target_pairs={{0,4},{2,6},{4,0},{6,2},{8,12},{10,14},{12,8},{14,10},{16,20},{18,... | collective-permute-start | bytes 3686408 | tf_op jit(solution)/shard_map/ppermute | solution.py:1032
  129.7 22.6 %collective-permute-start.16 = (bf16[512,768]{1,0:T(8,128)(2,1)S(1)}, bf16[512,768]{1,0:T(8,128)(2,1)}, u32[]{:S(2)}, u32[]{:S(2)}) collective-permute-start(bf16[512,768]{1,0:T(8,128)(2,1)S(1)} %copy-done.1), channel_id=1, source_target_pairs={{0,1},{1,0},{2,3},{3,2},{4,5},{5,4},{6,7},{7,6},{8,9},{9,8},{10,11... | collective-permute-start | bytes 2359304 | tf_op jit(solution)/shard_map/ppermute | solution.py:1029
  130.2 22.1 %collective-permute-start.15 = (bf16[2,104,1536]{2,1,0:T(8,128)(2,1)}, bf16[2,104,1536]{2,1,0:T(8,128)(2,1)}, u32[]{:S(2)}, u32[]{:S(2)}) collective-permute-start(bf16[2,104,1536]{2,1,0:T(8,128)(2,1)} %get-tuple-element.166), channel_id=1, source_target_pairs={{0,8},{2,10},{4,12},{6,14},{8,0},{10,2},{12,4},{14,6},{16,24},{18,... | collective-permute-start | bytes 1916936 | tf_op jit(solution)/shard_map/ppermute | solution.py:1032
  154.4 9.5 %collective-permute-start.19 = (bf16[392,1920]{1,0:T(8,128)(2,1)}, bf16[392,1920]{1,0:T(8,128)(2,1)}, u32[]{:S(2)}, u32[]{:S(2)}) collective-permute-start(bf16[392,1920]{1,0:T(8,128)(2,1)} %get-tuple-element.196), channel_id=1, source_target_pairs={{0,2},{2,0},{4,6},{6,4},{8,10},{10,8},{12,14},{14,12},{16,18},{18,... | collective-permute-start | bytes 4515848 | tf_op jit(solution)/shard_map/ppermute | solution.py:1032
  160.1 23.4 %collective-permute-start.18 = (bf16[2,96,1536]{2,1,0:T(8,128)(2,1)}, bf16[2,96,1536]{2,1,0:T(8,128)(2,1)}, u32[]{:S(2)}, u32[]{:S(2)}) collective-permute-start(bf16[2,96,1536]{2,1,0:T(8,128)(2,1)} %get-tuple-element.194), channel_id=1, source_target_pairs={{0,8},{2,10},{4,12},{6,14},{8,0},{10,2},{12,4},{14,6},{16,24},{18,... | collective-permute-start | bytes 1769480 | tf_op jit(solution)/shard_map/ppermute | solution.py:1032
  160.5 20.9 %collective-permute-start.17 = (bf16[2,56,1536]{2,1,0:T(8,128)(2,1)}, bf16[2,56,1536]{2,1,0:T(8,128)(2,1)}, u32[]{:S(2)}, u32[]{:S(2)}) collective-permute-start(bf16[2,56,1536]{2,1,0:T(8,128)(2,1)} %get-tuple-element.190), channel_id=1, source_target_pairs={{0,16},{2,18},{4,20},{6,22},{8,24},{10,26},{12,28},{14,30},{16,0},... | collective-permute-start | bytes 1032200 | tf_op jit(solution)/shard_map/ppermute | solution.py:1032
  163.1 37.6 %collective-permute-start.21 = (bf16[1024,768]{1,0:T(8,128)(2,1)}, bf16[1024,768]{1,0:T(8,128)(2,1)}, u32[]{:S(2)}, u32[]{:S(2)}) collective-permute-start(bf16[1024,768]{1,0:T(8,128)(2,1)} %get-tuple-element.182.a_ref), channel_id=1, source_target_pairs={{0,1},{1,0},{2,3},{3,2},{4,5},{5,4},{6,7},{7,6},{8,9},{9,8},{10,11... | collective-permute-start | bytes 4718600 | tf_op jit(solution)/shard_map/ppermute | solution.py:1029
  168.5 18.9 %collective-permute-start.20 = (bf16[1,200,1920]{2,1,0:T(8,128)(2,1)}, bf16[1,200,1920]{2,1,0:T(8,128)(2,1)S(1)}, u32[]{:S(2)}, u32[]{:S(2)}) collective-permute-start(bf16[1,200,1920]{2,1,0:T(8,128)(2,1)} %get-tuple-element.199), channel_id=1, source_target_pairs={{0,4},{2,6},{4,0},{6,2},{8,12},{10,14},{12,8},{14,10},{16,20},{18,... | collective-permute-start | bytes 2304008 | tf_op jit(solution)/shard_map/ppermute | solution.py:1032
  185.6 26.8 %collective-permute-start.23 = (bf16[2,48,1536]{2,1,0:T(8,128)(2,1)}, bf16[2,48,1536]{2,1,0:T(8,128)(2,1)}, u32[]{:S(2)}, u32[]{:S(2)}) collective-permute-start(bf16[2,48,1536]{2,1,0:T(8,128)(2,1)} %get-tuple-element.206), channel_id=1, source_target_pairs={{0,16},{2,18},{4,20},{6,22},{8,24},{10,26},{12,28},{14,30},{16,0},... | collective-permute-start | bytes 884744 | tf_op jit(solution)/shard_map/ppermute | solution.py:1032
  191.3 14.6 %collective-permute-start.22 = (bf16[1,104,1920]{2,1,0:T(8,128)(2,1)}, bf16[1,104,1920]{2,1,0:T(8,128)(2,1)S(1)}, u32[]{:S(2)}, u32[]{:S(2)}) collective-permute-start(bf16[1,104,1920]{2,1,0:T(8,128)(2,1)} %get-tuple-element.211), channel_id=1, source_target_pairs={{0,8},{2,10},{4,12},{6,14},{8,0},{10,2},{12,4},{14,6},{16,24},{18,... | collective-permute-start | bytes 1198088 | tf_op jit(solution)/shard_map/ppermute | solution.py:1032
  194.5 18.0 %collective-permute-start.24 = (bf16[2,56,1536]{2,1,0:T(8,128)(2,1)}, bf16[2,56,1536]{2,1,0:T(8,128)(2,1)S(1)}, u32[]{:S(2)}, u32[]{:S(2)}) collective-permute-start(bf16[2,56,1536]{2,1,0:T(8,128)(2,1)} %get-tuple-element.214), channel_id=1, source_target_pairs={{0,1},{1,0},{2,3},{3,2},{4,5},{5,4},{6,7},{7,6},{8,9},{9,8},{10,11... | collective-permute-start | bytes 1032200 | tf_op jit(solution)/shard_map/ppermute | solution.py:1029
  208.6 13.4 %collective-permute-start.25 = (bf16[1,56,1920]{2,1,0:T(8,128)(2,1)}, bf16[1,56,1920]{2,1,0:T(8,128)(2,1)S(1)}, u32[]{:S(2)}, u32[]{:S(2)}) collective-permute-start(bf16[1,56,1920]{2,1,0:T(8,128)(2,1)} %get-tuple-element.219), channel_id=1, source_target_pairs={{0,16},{2,18},{4,20},{6,22},{8,24},{10,26},{12,28},{14,30},{16,0},... | collective-permute-start | bytes 645128 | tf_op jit(solution)/shard_map/ppermute | solution.py:1032
  (12 other events, 59.4 us)

commit v3 on v2

--- a/solution.py
+++ b/solution.py
@@ -936,7 +936,7 @@
         out_shape=hbm((pages * length, dim), F32),
         input_output_aliases={} if into is None else {4: 0},
         compiler_params=params(1),
-        cost_estimate=cost(3 * df.size, 10 * df.size),
+        cost_estimate=cost(4e10, 10 * df.size),
         name="place_grad",
     )(pick, *args)
 
@@ -1108,12 +1108,12 @@
         xg = over_dp(xs, 2)
         zg_a, zg_b = over_dp(sent_a, 8), over_dp(sent_b, 4)
         grad_input = place_grad(1, pick, after(df_other, xs), inp_other, inp_own_got, pages)
-        zg_a, zg_b = after((zg_a, zg_b), grad_input)
-        own_b, sent_b = add_z(own_b, after(zg_b, zg_a), small_b, False)
-        own, sent, a_small = add_x(pick, after(xk, sent_b), xg, a_small, True)
+        own, sent, a_small = add_x(pick, after(xk, grad_input), xg, a_small, True)
         zg = over_dp(sent, 4)
+        zg_a, zg_b = after((zg_a, zg_b), sent)
+        own_b, sent_b = add_z(own_b, zg_b, small_b, False)
         zg_b = over_dp(sent_b, 8)
-        a_sum, small_3 = for_head(own_a, after(zg_a, sent), small_3)
+        a_sum, small_3 = for_head(own_a, after(zg_a, sent_b), small_3)
         df_own, inp_other_got = after((df_own, inp_other_got), a_sum)
         a_sum = over_head(a_sum)
         grad_input = place_grad(0, pick, df_own, inp_own, inp_other_got, pages, grad_input)

time: 225 us -> 223 us (level)
  starting transfers between devices: 27.4 us -> 22.8 us
  waiting for transfers between devices: 30.5 us -> 33.5 us
    ppermute x18, waiting for transfers between devices: 21.5 us -> 29.1 us  [over_dp(): return lax.ppermute(value, 'dp', swap_perm(shards_dp, flip))]
    ppermute x8, waiting for transfers between devices: 9 us -> 4.43 us  [over_head(): return lax.ppermute(value, 'head', [(0, 1), (1, 0)])]
    ppermute x18, starting transfers between devices: 17.4 us -> 13.1 us  [over_dp(): return lax.ppermute(value, 'dp', swap_perm(shards_dp, flip))]
  transfers between devices with their start and end apart: 26 -> 26, of which waited for: 12 -> 10; matrix products, arithmetic and copies ran while one was open for 2% -> 2% of each run, Pallas kernels for 56% -> 57%
where the time goes in v3:
time: 223 us; the launch traced here: 222 us
  Pallas kernels  157 us (70%)
  waiting for transfers between devices  33.5 us (15%)
  starting transfers between devices  22.8 us (10%)
  local copies, waits for them, and re-layouts  6.74 us (3%)
    pallas_call x2, Pallas kernels, attn_bwd(): pl.pallas_call(partial(attn_bwd_kernel, groups, box_groups, first), grid_...  42.2 us
    pallas_call x2, Pallas kernels, attn_fwd(): pl.pallas_call(partial(attn_fwd_kernel, groups, which_page), grid_spec=pl...  32.3 us
    ppermute x18, waiting for transfers between devices, over_dp(): return lax.ppermute(value, 'dp', swap_perm(shards_dp, flip))  29.1 us
    pallas_call x1, Pallas kernels, feed_forward(): pl.pallas_call(partial(ff_kernel, groups), grid_spec=pltpu.PrefetchScalar...  24 us
    ppermute x18, starting transfers between devices, over_dp(): return lax.ppermute(value, 'dp', swap_perm(shards_dp, flip))  13.1 us
    pallas_call x2, Pallas kernels, ff_grad(): pl.pallas_call(ff_keep_kernel, grid_spec=pltpu.PrefetchScalarGridSpec(num...  11.2 us
    pallas_call x3, Pallas kernels, add_x(): pl.pallas_call(partial(add_x_kernel, tailed), grid_spec=pltpu.PrefetchSca...  10.1 us
    pallas_call x2, Pallas kernels, ff_grad(): pl.pallas_call(ff_send_kernel, grid_spec=pltpu.PrefetchScalarGridSpec(num...  10 us
  transfers between devices with their start and end apart: 26, of which 10 were waited for; matrix products, arithmetic and copies ran while one was open for 2% of the time, Pallas kernels for 57%

profile of v3, /device:TPU:0, one launch (start us, length us, event | category | flops | bytes accessed | tf_op | source)
XLA Modules:
  0.0 222.2 jit_solution(15258453733401086687)
XLA Ops:
  1.9 3.0 %collective-permute-start = (bf16[768,384]{1,0:T(8,128)(2,1)S(1)}, bf16[768,384]{1,0:T(8,128)(2,1)}, u32[]{:S(2)}, u32[]{:S(2)}) collective-permute-start(bf16[768,384]{1,0:T(8,128)(2,1)S(1)} %constant_dynamic-slice_fusion.1), channel_id=1, source_target_pairs={{0,1},{1,0},{2,3},{3,2},{4,5},{5,4},{6,7},{7,6},{8,9},{9,8},{10,11... | collective-permute-start | bytes 1769480 | tf_op jit(solution)/shard_map/ppermute | solution.py:1029
  11.3 16.2 %attn_fwd.2 = (bf16[512,768]{1,0:T(8,128)(2,1)}, bf16[6,512,512]{2,1,0:T(8,128)(2,1)}, bf16[512,384]{1,0:T(8,128)(2,1)}, bf16[512,384]{1,0:T(8,128)(2,1)}, bf16[...) custom-call(s32[9]{0:T(128)} %stack.39.pick, ...), custom_call_target="tpu_custom_call" | custom-call | flops 4328521728 | bytes 10000000 | tf_op jit(solution)/shard_map/attn_fwd/pallas_call | solution.py:165
  27.5 3.6 %collective-permute-done.2.bi_there = bf16[1536]{0:T(1024)(128)(2,1)S(1)} collective-permute-done((bf16[1536]{0:T(1024)(128)(2,1)S(1)}, bf16[1536]{0:T(1024)(128)(2,1)S(1)}, u32[]{:S(2)}, u32[]{:S(2)}) %collective-permute-start.2) | collective-permute-done | bytes 3104 | tf_op jit(solution)/shard_map/ppermute | solution.py:1029
  36.4 16.2 %attn_fwd.3 = (bf16[512,768]{1,0:T(8,128)(2,1)}, bf16[6,512,512]{2,1,0:T(8,128)(2,1)}, bf16[512,384]{1,0:T(8,128)(2,1)}, bf16[512,384]{1,0:T(8,128)(2,1)}, bf16[...) custom-call(s32[9]{0:T(128)} %stack.39.pick, ...), custom_call_target="tpu_custom_call" | custom-call | flops 4328521728 | bytes 10000000 | tf_op jit(solution)/shard_map/attn_fwd/pallas_call | solution.py:165
  55.9 24.0 %feed_forward.1 = (bf16[512,768]{1,0:T(8,128)(2,1)}, bf16[512,768]{1,0:T(8,128)(2,1)}, bf16[2,2,384,512]{3,2,1,0:T(8,128)(2,1)}, bf16[2,4,512,768]{3,2,1,0:T(8,128)(2,1)}, f32[8,1536]{1,0:T(8,128)}) custom-call(s32[9]{0:T(128)} %stack.39.pick, bf16[1024,768]{1,0:T(8,128)(2,1)} %tok_ref.4, bf16[512,768]{1,0:T(8,128)(2,1)} %get-tuple-element.132.part_ref, ...), custom_call_target="tpu_custom_call" | custom-call | flops 9663676416 | bytes 22020096 | tf_op jit(solution)/shard_map/feed_forward/pallas_call | solution.py:569
  80.0 5.0 %ff_grad_send.2 = bf16[2,392,1536]{2,1,0:T(8,128)(2,1)} custom-call(s32[9]{0:T(128)} %stack.39.pick, bf16[2,2,384,512]{3,2,1,0:T(8,128)(2,1)} %get-tuple-element.141.lhs_ref, bf16[2,4,512,768]{3,2,1,0:T(8,128)(2,1)} %get-tuple-element.147.rhs_ref, f32[8,1536]{1,0:T(8,128)} %get-tuple-element.143.small_ref), custom_call_target="tpu_custom_call" | custom-call | flops 1207959552 | bytes 10000000 | tf_op jit(solution)/shard_map/ff_grad_send/pallas_call | solution.py:680
  85.1 5.0 %ff_grad_send.3 = bf16[2,392,1536]{2,1,0:T(8,128)(2,1)} custom-call(s32[9]{0:T(128)} %stack.39.pick, bf16[2,2,384,512]{3,2,1,0:T(8,128)(2,1)} %get-tuple-element.141.lhs_ref, bf16[2,4,512,768]{3,2,1,0:T(8,128)(2,1)} %get-tuple-element.147.rhs_ref, f32[8,1536]{1,0:T(8,128)} %get-tuple-element.143.small_ref), custom_call_target="tpu_custom_call" | custom-call | flops 1207959552 | bytes 10000000 | tf_op jit(solution)/shard_map/ff_grad_send/pallas_call | solution.py:680
  90.5 5.6 %ff_grad_keep.2 = (bf16[2,200,1536]{2,1,0:T(8,128)(2,1)}, bf16[2,192,1536]{2,1,0:T(8,128)(2,1)}, f32[8,1536]{1,0:T(8,128)}) custom-call(s32[9]{0:T(128)} %stack.39.pick, bf16[2,2,384,512]{3,2,1,0:T(8,128)(2,1)} %get-tuple-element.141.lhs_ref, bf16[2,4,512,768]{3,2,1,0:T(8,128)(2,1)} %get-tuple-element.147.rhs_ref, ...), custom_call_target="tpu_custom_call" | custom-call | flops 1207959552 | bytes 10000000 | tf_op jit(solution)/shard_map/ff_grad_keep/pallas_call | solution.py:693
  97.2 5.5 %ff_grad_keep.3 = (bf16[2,200,1536]{2,1,0:T(8,128)(2,1)}, bf16[2,192,1536]{2,1,0:T(8,128)(2,1)}, f32[8,1536]{1,0:T(8,128)}) custom-call(s32[9]{0:T(128)} %stack.39.pick, bf16[2,2,384,512]{3,2,1,0:T(8,128)(2,1)} %get-tuple-element.141.lhs_ref, bf16[2,4,512,768]{3,2,1,0:T(8,128)(2,1)} %get-tuple-element.147.rhs_ref, ...), custom_call_target="tpu_custom_call" | custom-call | flops 1207959552 | bytes 10000000 | tf_op jit(solution)/shard_map/ff_grad_keep/pallas_call | solution.py:693
  102.8 20.6 %attn_bwd.2 = (bf16[2,384,1920]{2,1,0:T(8,128)(2,1)}, f32[1,1920]{1,0:T(1,128)}, bf16[512,768]{1,0:T(8,128)(2,1)}) custom-call(s32[9]{0:T(128)} %stack.39.pick, bf16[512,768]{1,0:T(8,128)(2,1)} %get-tuple-element.213.refs_0_.df_ref, bf16[2,384,512]{2,1,0:T(8,128)(2,1)} %get-tuple-element.151.refs_1_, bf16[512,384]{1,0:T(8,128)(2,1)} %get-tuple-element.152.refs_2_, ...), custom_call_target="tpu_custom_call" | custom-call | flops 6543114240 | bytes 14000000 | tf_op jit(solution)/shard_map/attn_bwd/pallas_call | solution.py:341
  123.4 2.3 %collective-permute-done.12.got_ref = bf16[2,200,1536]{2,1,0:T(8,128)(2,1)} collective-permute-done((bf16[2,200,1536]{2,1,0:T(8,128)(2,1)}, bf16[2,200,1536]{2,1,0:T(8,128)(2,1)}, u32[]{:S(2)}, u32[]{:S(2)}) %collective-permute-start.12) | collective-permute-done | bytes 1228832 | tf_op jit(solution)/shard_map/ppermute | solution.py:1032
  126.1 3.6 %add_x.3 = (bf16[2,96,1536]{2,1,0:T(8,128)(2,1)}, bf16[2,104,1536]{2,1,0:T(8,128)(2,1)}, f32[8,1536]{1,0:T(8,128)}) custom-call(s32[9]{0:T(128)} %stack.39.pick, bf16[2,192,1536]{2,1,0:T(8,128)(2,1)} %get-tuple-element.161.keep_ref, bf16[2,200,1536]{2,1,0:T(8,128)(2,1)} %collective-permute-done.12.got_ref, f32[8,1536]{1,0:T(8,128)} %get-tuple-element.164.small_ref), custom_call_target="tpu_custom_call" | custom-call | flops 589824 | bytes 3538944 | tf_op jit(solution)/shard_map/add_x/pallas_call | solution.py:796
  130.6 21.7 %attn_bwd.3 = (bf16[392,1920]{1,0:T(8,128)(2,1)}, bf16[384,1920]{1,0:T(8,128)(2,1)}, f32[1,1920]{1,0:T(1,128)}, bf16[1024,768]{1,0:T(8,128)(2,1)}) custom-call(s32[9]{0:T(128)} %stack.39.pick, bf16[512,768]{1,0:T(8,128)(2,1)} %collective-permute-done.13.refs_0_.df_ref, bf16[2,384,512]{2,1,0:T(8,128)(2,1)} %get-tuple-element.167.refs_1_, ...), custom_call_target="tpu_custom_call" | custom-call | flops 6543114240 | bytes 14000000 | tf_op jit(solution)/shard_map/attn_bwd/pallas_call | solution.py:341
  156.6 2.6 %collective-permute-start.17 = (bf16[2,56,1536]{2,1,0:T(8,128)(2,1)}, bf16[2,56,1536]{2,1,0:T(8,128)(2,1)}, u32[]{:S(2)}, u32[]{:S(2)}) collective-permute-start(bf16[2,56,1536]{2,1,0:T(8,128)(2,1)} %get-tuple-element.189), channel_id=1, source_target_pairs={{0,16},{2,18},{4,20},{6,22},{8,24},{10,26},{12,28},{14,30},{16,0},... | collective-permute-start | bytes 1032200 | tf_op jit(solution)/shard_map/ppermute | solution.py:1032
  159.1 3.5 %add_x.4 = (bf16[2,96,1536]{2,1,0:T(8,128)(2,1)}, bf16[2,96,1536]{2,1,0:T(8,128)(2,1)}) custom-call(s32[9]{0:T(128)} %stack.39.pick, bf16[2,192,1536]{2,1,0:T(8,128)(2,1)} %get-tuple-element.190.keep_ref, bf16[2,200,1536]{2,1,0:T(8,128)(2,1)} %collective-permute-done.14.got_ref, f32[8,1536]{1,0:T(8,128)} %get-tuple-element.191.small_ref), custom_call_target="tpu_custom_call" | custom-call | flops 589824 | bytes 3538944 | tf_op jit(solution)/shard_map/add_x/pallas_call | solution.py:796
  163.9 4.6 %attn_split.1 = (bf16[1,200,1920]{2,1,0:T(8,128)(2,1)}, bf16[1,192,1920]{2,1,0:T(8,128)(2,1)}, f32[8,1920]{1,0:T(8,128)}) custom-call(s32[9]{0:T(128)} %stack.39.pick, bf16[384,1920]{1,0:T(8,128)(2,1)} %get-tuple-element.194.kept_ref, bf16[392,1920]{1,0:T(8,128)(2,1)} %collective-permute-done.19.got_ref, f32[1,1920]{1,0:T(1,128)} %get-tuple-element.197.small_ref), custom_call_target="tpu_custom_call" | custom-call | flops 737280 | bytes 4423680 | tf_op jit(solution)/shard_map/attn_split/pallas_call | solution.py:740
  170.1 3.3 %place_grad.2.refs_0_ = f32[1024,768]{1,0:T(8,128)} custom-call(s32[9]{0:T(128)} %stack.39.pick, bf16[512,768]{1,0:T(8,128)(2,1)} %collective-permute-done.13.refs_0_.df_ref, bf16[1024,768]{1,0:T(8,128)(2,1)} %get-tuple-element.181.a_ref, bf16[512,768]{1,0:T(8,128)(2,1)} %collective-permute-done.16.b_ref), custom_call_target="tpu_custom_call" | custom-call | flops 40000000000 | bytes 3932160 | tf_op jit(solution)/shard_map/place_grad/pallas_call | solution.py:928
  173.3 14.4 %collective-permute-done.20.got_ref = bf16[1,200,1920]{2,1,0:T(8,128)(2,1)S(1)} collective-permute-done((bf16[1,200,1920]{2,1,0:T(8,128)(2,1)}, bf16[1,200,1920]{2,1,0:T(8,128)(2,1)S(1)}, u32[]{:S(2)}, u32[]{:S(2)}) %collective-permute-start.20) | collective-permute-done | bytes 768032 | tf_op jit(solution)/shard_map/ppermute | solution.py:1032
  188.6 3.0 %add_x.5 = (bf16[1,96,1920]{2,1,0:T(8,128)(2,1)}, bf16[1,104,1920]{2,1,0:T(8,128)(2,1)}, f32[8,1920]{1,0:T(8,128)}) custom-call(s32[9]{0:T(128)} %stack.39.pick, bf16[1,192,1920]{2,1,0:T(8,128)(2,1)} %get-tuple-element.201.keep_ref, bf16[1,200,1920]{2,1,0:T(8,128)(2,1)} %copy-done, f32[8,1920]{1,0:T(8,128)} %get-tuple-element.202.small_ref), custom_call_target="tpu_custom_call" | custom-call | flops 368640 | bytes 2211840 | tf_op jit(solution)/shard_map/add_x/pallas_call | solution.py:796
  197.2 3.3 %place_grad.3 = f32[1024,768]{1,0:T(8,128)} custom-call(s32[9]{0:T(128)} %stack.39.pick, bf16[512,768]{1,0:T(8,128)(2,1)} %get-tuple-element.213.refs_0_.df_ref, bf16[512,768]{1,0:T(8,128)(2,1)} %get-tuple-element.180.a_ref, bf16[1024,768]{1,0:T(8,128)(2,1)} %collective-permute-done.21.b_ref, ...), custom_call_target="tpu_custom_call", output_to_operand_aliasing={{}: (4, {})} | custom-call | flops 40000000000 | bytes 3932160 | tf_op jit(solution)/shard_map/place_grad/pallas_call | solution.py:928
  200.5 6.5 %collective-permute-done.22.got_ref = bf16[1,104,1920]{2,1,0:T(8,128)(2,1)} collective-permute-done((bf16[1,104,1920]{2,1,0:T(8,128)(2,1)}, bf16[1,104,1920]{2,1,0:T(8,128)(2,1)}, u32[]{:S(2)}, u32[]{:S(2)}) %collective-permute-start.22) | collective-permute-done | bytes 399392 | tf_op jit(solution)/shard_map/ppermute | solution.py:1032
  210.7 2.7 %ff_last.1 = (f32[48,1536]{1,0:T(8,128)}, f32[48,1536]{1,0:T(8,128)}, f32[768]{0:T(1024)}, f32[768]{0:T(1024)}, f32[768]{0:T(1024)}, /*index=5*/f32[768]{0:T(102...) custom-call(s32[9]{0:T(128)} %stack.39.pick, bf16[2,48,1536]{2,1,0:T(8,128)(2,1)} %get-tuple-element.218.own, ...), custom_call_target="tpu_custom_call" | custom-call | flops 1720320 | bytes 3440640 | tf_op jit(solution)/shard_map/ff_last/pallas_call | solution.py:881
  213.4 3.3 %place_output.1 = bf16[1024,768]{1,0:T(8,128)(2,1)} custom-call(s32[9]{0:T(128)} %stack.39.pick, bf16[512,768]{1,0:T(8,128)(2,1)} %get-tuple-element.221.refs_16_.a_ref, bf16[1024,768]{1,0:T(8,128)(2,1)} %collective-permute-done.21.b_ref), custom_call_target="tpu_custom_call" | custom-call | flops 393216 | bytes 3145728 | tf_op jit(solution)/shard_map/place_output/pallas_call | solution.py:955
  216.7 3.0 %collective-permute-done.25.got = bf16[1,56,1920]{2,1,0:T(8,128)(2,1)S(1)} collective-permute-done((bf16[1,56,1920]{2,1,0:T(8,128)(2,1)}, bf16[1,56,1920]{2,1,0:T(8,128)(2,1)S(1)}, u32[]{:S(2)}, u32[]{:S(2)}) %collective-permute-start.25) | collective-permute-done | bytes 215072 | tf_op jit(solution)/shard_map/ppermute | solution.py:1032
  (79 shorter events, 38.7 us)
Async XLA Ops:
  1.9 29.2 %collective-permute-start = (bf16[768,384]{1,0:T(8,128)(2,1)S(1)}, bf16[768,384]{1,0:T(8,128)(2,1)}, u32[]{:S(2)}, u32[]{:S(2)}) collective-permute-start(bf16[768,384]{1,0:T(8,128)(2,1)S(1)} %constant_dynamic-slice_fusion.1), channel_id=1, source_target_pairs={{0,1},{1,0},{2,3},{3,2},{4,5},{5,4},{6,7},{7,6},{8,9},{9,8},{10,11... | collective-permute-start | bytes 1769480 | tf_op jit(solution)/shard_map/ppermute | solution.py:1029
  6.8 24.2 %collective-permute-start.1 = (bf16[384,768]{1,0:T(8,128)(2,1)}, bf16[384,768]{1,0:T(8,128)(2,1)}, u32[]{:S(2)}, u32[]{:S(2)}) collective-permute-start(bf16[384,768]{1,0:T(8,128)(2,1)} %constant_dynamic-slice_fusion), channel_id=1, source_target_pairs={{0,1},{1,0},{2,3},{3,2},{4,5},{5,4},{6,7},{7,6},{8,9},{9,8},{10,11... | collective-permute-start | bytes 1769480 | tf_op jit(solution)/shard_map/ppermute | solution.py:1029
  6.9 24.1 %collective-permute-start.2 = (bf16[1536]{0:T(1024)(128)(2,1)S(1)}, bf16[1536]{0:T(1024)(128)(2,1)S(1)}, u32[]{:S(2)}, u32[]{:S(2)}) collective-permute-start(bf16[1536]{0:T(1024)(128)(2,1)S(1)} %copy-done.8), channel_id=1, source_target_pairs={{0,1},{1,0},{2,3},{3,2},{4,5},{5,4},{6,7},{7,6},{8,9},{9,8},{10,11... | collective-permute-start | bytes 9224 | tf_op jit(solution)/shard_map/ppermute | solution.py:1029
  31.0 21.6 %collective-permute-start.4 = (bf16[768,384]{1,0:T(8,128)(2,1)}, bf16[768,384]{1,0:T(8,128)(2,1)}, u32[]{:S(2)}, u32[]{:S(2)}) collective-permute-start(bf16[768,384]{1,0:T(8,128)(2,1)} %collective-permute-done.wi0), channel_id=1, source_target_pairs={{0,2},{2,0},{4,6},{6,4},{8,10},{10,8},{12,14},{14,12},{16,18},{18,... | collective-permute-start | bytes 1769480 | tf_op jit(solution)/shard_map/ppermute | solution.py:1032
  31.1 21.5 %collective-permute-start.5 = (bf16[384,768]{1,0:T(8,128)(2,1)}, bf16[384,768]{1,0:T(8,128)(2,1)}, u32[]{:S(2)}, u32[]{:S(2)}) collective-permute-start(bf16[384,768]{1,0:T(8,128)(2,1)} %collective-permute-done.1.wb0), channel_id=1, source_target_pairs={{0,2},{2,0},{4,6},{6,4},{8,10},{10,8},{12,14},{14,12},{16,18},{18,... | collective-permute-start | bytes 1769480 | tf_op jit(solution)/shard_map/ppermute | solution.py:1032
  31.6 21.0 %collective-permute-start.6 = (bf16[768,384]{1,0:T(8,128)(2,1)}, bf16[768,384]{1,0:T(8,128)(2,1)}, u32[]{:S(2)}, u32[]{:S(2)}) collective-permute-start(bf16[768,384]{1,0:T(8,128)(2,1)} %collective-permute-done.wi0), channel_id=1, source_target_pairs={{0,4},{2,6},{4,0},{6,2},{8,12},{10,14},{12,8},{14,10},{16,20},{18,... | collective-permute-start | bytes 1769480 | tf_op jit(solution)/shard_map/ppermute | solution.py:1032
  33.3 19.3 %collective-permute-start.7 = (bf16[384,768]{1,0:T(8,128)(2,1)}, bf16[384,768]{1,0:T(8,128)(2,1)}, u32[]{:S(2)}, u32[]{:S(2)}) collective-permute-start(bf16[384,768]{1,0:T(8,128)(2,1)} %collective-permute-done.1.wb0), channel_id=1, source_target_pairs={{0,8},{2,10},{4,12},{6,14},{8,0},{10,2},{12,4},{14,6},{16,24},{18,... | collective-permute-start | bytes 1769480 | tf_op jit(solution)/shard_map/ppermute | solution.py:1032
  34.9 19.2 %collective-permute-start.3 = (bf16[512,768]{1,0:T(8,128)(2,1)}, bf16[512,768]{1,0:T(8,128)(2,1)S(1)}, u32[]{:S(2)}, u32[]{:S(2)}) collective-permute-start(bf16[512,768]{1,0:T(8,128)(2,1)} %get-tuple-element.129), channel_id=1, source_target_pairs={{0,1},{1,0},{2,3},{3,2},{4,5},{5,4},{6,7},{7,6},{8,9},{9,8},{10,11... | collective-permute-start | bytes 2359304 | tf_op jit(solution)/shard_map/ppermute | solution.py:1029
  85.0 5.5 %collective-permute-start.10 = (bf16[2,392,1536]{2,1,0:T(8,128)(2,1)}, bf16[2,392,1536]{2,1,0:T(8,128)(2,1)}, u32[]{:S(2)}, u32[]{:S(2)}) collective-permute-start(bf16[2,392,1536]{2,1,0:T(8,128)(2,1)} %ff_grad_send.2), channel_id=1, source_target_pairs={{0,2},{2,0},{4,6},{6,4},{8,10},{10,8},{12,14},{14,12},{16,18},{18,... | collective-permute-start | bytes 7225352 | tf_op jit(solution)/shard_map/ppermute | solution.py:1032
  90.1 7.1 %collective-permute-start.11 = (bf16[2,392,1536]{2,1,0:T(8,128)(2,1)}, bf16[2,392,1536]{2,1,0:T(8,128)(2,1)}, u32[]{:S(2)}, u32[]{:S(2)}) collective-permute-start(bf16[2,392,1536]{2,1,0:T(8,128)(2,1)} %ff_grad_send.3), channel_id=1, source_target_pairs={{0,2},{2,0},{4,6},{6,4},{8,10},{10,8},{12,14},{14,12},{16,18},{18,... | collective-permute-start | bytes 7225352 | tf_op jit(solution)/shard_map/ppermute | solution.py:1032
  96.1 29.5 %collective-permute-start.12 = (bf16[2,200,1536]{2,1,0:T(8,128)(2,1)}, bf16[2,200,1536]{2,1,0:T(8,128)(2,1)}, u32[]{:S(2)}, u32[]{:S(2)}) collective-permute-start(bf16[2,200,1536]{2,1,0:T(8,128)(2,1)} %get-tuple-element.146), channel_id=1, source_target_pairs={{0,4},{2,6},{4,0},{6,2},{8,12},{10,14},{12,8},{14,10},{16,20},{18,... | collective-permute-start | bytes 3686408 | tf_op jit(solution)/shard_map/ppermute | solution.py:1032
  96.6 26.7 %collective-permute-start.13 = (bf16[512,768]{1,0:T(8,128)(2,1)S(1)}, bf16[512,768]{1,0:T(8,128)(2,1)}, u32[]{:S(2)}, u32[]{:S(2)}) collective-permute-start(bf16[512,768]{1,0:T(8,128)(2,1)S(1)} %copy-done.5), channel_id=1, source_target_pairs={{0,1},{1,0},{2,3},{3,2},{4,5},{5,4},{6,7},{7,6},{8,9},{9,8},{10,11... | collective-permute-start | bytes 2359304 | tf_op jit(solution)/shard_map/ppermute | solution.py:1029
  125.7 28.7 %collective-permute-start.14 = (bf16[2,200,1536]{2,1,0:T(8,128)(2,1)}, bf16[2,200,1536]{2,1,0:T(8,128)(2,1)}, u32[]{:S(2)}, u32[]{:S(2)}) collective-permute-start(bf16[2,200,1536]{2,1,0:T(8,128)(2,1)} %get-tuple-element.179), channel_id=1, source_target_pairs={{0,4},{2,6},{4,0},{6,2},{8,12},{10,14},{12,8},{14,10},{16,20},{18,... | collective-permute-start | bytes 3686408 | tf_op jit(solution)/shard_map/ppermute | solution.py:1032
  129.7 24.2 %collective-permute-start.16 = (bf16[512,768]{1,0:T(8,128)(2,1)S(1)}, bf16[512,768]{1,0:T(8,128)(2,1)}, u32[]{:S(2)}, u32[]{:S(2)}) collective-permute-start(bf16[512,768]{1,0:T(8,128)(2,1)S(1)} %copy-done.6), channel_id=1, source_target_pairs={{0,1},{1,0},{2,3},{3,2},{4,5},{5,4},{6,7},{7,6},{8,9},{9,8},{10,11... | collective-permute-start | bytes 2359304 | tf_op jit(solution)/shard_map/ppermute | solution.py:1029
  130.2 23.7 %collective-permute-start.15 = (bf16[2,104,1536]{2,1,0:T(8,128)(2,1)}, bf16[2,104,1536]{2,1,0:T(8,128)(2,1)}, u32[]{:S(2)}, u32[]{:S(2)}) collective-permute-start(bf16[2,104,1536]{2,1,0:T(8,128)(2,1)} %get-tuple-element.165), channel_id=1, source_target_pairs={{0,8},{2,10},{4,12},{6,14},{8,0},{10,2},{12,4},{14,6},{16,24},{18,... | collective-permute-start | bytes 1916936 | tf_op jit(solution)/shard_map/ppermute | solution.py:1032
  152.3 44.9 %collective-permute-start.21 = (bf16[1024,768]{1,0:T(8,128)(2,1)}, bf16[1024,768]{1,0:T(8,128)(2,1)}, u32[]{:S(2)}, u32[]{:S(2)}) collective-permute-start(bf16[1024,768]{1,0:T(8,128)(2,1)} %get-tuple-element.181.a_ref), channel_id=1, source_target_pairs={{0,1},{1,0},{2,3},{3,2},{4,5},{5,4},{6,7},{7,6},{8,9},{9,8},{10,11... | collective-permute-start | bytes 4718600 | tf_op jit(solution)/shard_map/ppermute | solution.py:1029
  154.4 9.5 %collective-permute-start.19 = (bf16[392,1920]{1,0:T(8,128)(2,1)}, bf16[392,1920]{1,0:T(8,128)(2,1)}, u32[]{:S(2)}, u32[]{:S(2)}) collective-permute-start(bf16[392,1920]{1,0:T(8,128)(2,1)} %get-tuple-element.195), channel_id=1, source_target_pairs={{0,2},{2,0},{4,6},{6,4},{8,10},{10,8},{12,14},{14,12},{16,18},{18,... | collective-permute-start | bytes 4515848 | tf_op jit(solution)/shard_map/ppermute | solution.py:1032
  156.6 35.9 %collective-permute-start.17 = (bf16[2,56,1536]{2,1,0:T(8,128)(2,1)}, bf16[2,56,1536]{2,1,0:T(8,128)(2,1)}, u32[]{:S(2)}, u32[]{:S(2)}) collective-permute-start(bf16[2,56,1536]{2,1,0:T(8,128)(2,1)} %get-tuple-element.189), channel_id=1, source_target_pairs={{0,16},{2,18},{4,20},{6,22},{8,24},{10,26},{12,28},{14,30},{16,0},... | collective-permute-start | bytes 1032200 | tf_op jit(solution)/shard_map/ppermute | solution.py:1032
  162.6 29.8 %collective-permute-start.18 = (bf16[2,96,1536]{2,1,0:T(8,128)(2,1)}, bf16[2,96,1536]{2,1,0:T(8,128)(2,1)}, u32[]{:S(2)}, u32[]{:S(2)}) collective-permute-start(bf16[2,96,1536]{2,1,0:T(8,128)(2,1)} %get-tuple-element.193), channel_id=1, source_target_pairs={{0,8},{2,10},{4,12},{6,14},{8,0},{10,2},{12,4},{14,6},{16,24},{18,... | collective-permute-start | bytes 1769480 | tf_op jit(solution)/shard_map/ppermute | solution.py:1032
  168.5 19.2 %collective-permute-start.20 = (bf16[1,200,1920]{2,1,0:T(8,128)(2,1)}, bf16[1,200,1920]{2,1,0:T(8,128)(2,1)S(1)}, u32[]{:S(2)}, u32[]{:S(2)}) collective-permute-start(bf16[1,200,1920]{2,1,0:T(8,128)(2,1)} %get-tuple-element.199), channel_id=1, source_target_pairs={{0,4},{2,6},{4,0},{6,2},{8,12},{10,14},{12,8},{14,10},{16,20},{18,... | collective-permute-start | bytes 2304008 | tf_op jit(solution)/shard_map/ppermute | solution.py:1032
  191.6 15.4 %collective-permute-start.22 = (bf16[1,104,1920]{2,1,0:T(8,128)(2,1)}, bf16[1,104,1920]{2,1,0:T(8,128)(2,1)}, u32[]{:S(2)}, u32[]{:S(2)}) collective-permute-start(bf16[1,104,1920]{2,1,0:T(8,128)(2,1)} %get-tuple-element.203), channel_id=1, source_target_pairs={{0,8},{2,10},{4,12},{6,14},{8,0},{10,2},{12,4},{14,6},{16,24},{18,... | collective-permute-start | bytes 1198088 | tf_op jit(solution)/shard_map/ppermute | solution.py:1032
  194.6 15.3 %collective-permute-start.23 = (bf16[2,48,1536]{2,1,0:T(8,128)(2,1)}, bf16[2,48,1536]{2,1,0:T(8,128)(2,1)S(1)}, u32[]{:S(2)}, u32[]{:S(2)}) collective-permute-start(bf16[2,48,1536]{2,1,0:T(8,128)(2,1)} %get-tuple-element.209), channel_id=1, source_target_pairs={{0,16},{2,18},{4,20},{6,22},{8,24},{10,26},{12,28},{14,30},{16,0},... | collective-permute-start | bytes 884744 | tf_op jit(solution)/shard_map/ppermute | solution.py:1032
  196.8 13.1 %collective-permute-start.24 = (bf16[2,56,1536]{2,1,0:T(8,128)(2,1)}, bf16[2,56,1536]{2,1,0:T(8,128)(2,1)S(1)}, u32[]{:S(2)}, u32[]{:S(2)}) collective-permute-start(bf16[2,56,1536]{2,1,0:T(8,128)(2,1)} %get-tuple-element.212), channel_id=1, source_target_pairs={{0,1},{1,0},{2,3},{3,2},{4,5},{5,4},{6,7},{7,6},{8,9},{9,8},{10,11... | collective-permute-start | bytes 1032200 | tf_op jit(solution)/shard_map/ppermute | solution.py:1029
  209.1 10.7 %collective-permute-start.25 = (bf16[1,56,1920]{2,1,0:T(8,128)(2,1)}, bf16[1,56,1920]{2,1,0:T(8,128)(2,1)S(1)}, u32[]{:S(2)}, u32[]{:S(2)}) collective-permute-start(bf16[1,56,1920]{2,1,0:T(8,128)(2,1)} %get-tuple-element.217), channel_id=1, source_target_pairs={{0,16},{2,18},{4,20},{6,22},{8,24},{10,26},{12,28},{14,30},{16,0},... | collective-permute-start | bytes 645128 | tf_op jit(solution)/shard_map/ppermute | solution.py:1032
  (12 other events, 59.4 us)

commit v4 on v3

--- a/solution.py
+++ b/solution.py
@@ -734,7 +734,7 @@
 
 def attn_split(pick, kept, got, small):
     rows, cols = kept.shape
-    steps = 3
+    steps = 1
     column = lambda height: pl.BlockSpec((height, cols // steps), lambda i, pick: (0, i))
     deep = lambda height: pl.BlockSpec((1, height, cols // steps), lambda i, pick: (0, 0, i))
     return pl.pallas_call(
@@ -922,7 +922,7 @@
 
 def place_grad(which, pick, df, mine, got, pages, into=None):
     length, dim = df.shape
-    steps = 2
+    steps = 1
     part = pl.BlockSpec((length // steps, dim), lambda i, pick: (i, 0))
     args = [df, mine, got] + ([] if into is None else [into])
     return pl.pallas_call(

time: 223 us -> 223 us (level)
  no operation moved by 1% of the time
where the time goes in v4:
time: 223 us; the launch traced here: 222 us
  Pallas kernels  157 us (70%)
  waiting for transfers between devices  32.8 us (15%)
  starting transfers between devices  22.8 us (10%)
  local copies, waits for them, and re-layouts  6.74 us (3%)
    pallas_call x2, Pallas kernels, attn_bwd(): pl.pallas_call(partial(attn_bwd_kernel, groups, box_groups, first), grid_...  42.2 us
    pallas_call x2, Pallas kernels, attn_fwd(): pl.pallas_call(partial(attn_fwd_kernel, groups, which_page), grid_spec=pl...  32.3 us
    ppermute x18, waiting for transfers between devices, over_dp(): return lax.ppermute(value, 'dp', swap_perm(shards_dp, flip))  28.3 us
    pallas_call x1, Pallas kernels, feed_forward(): pl.pallas_call(partial(ff_kernel, groups), grid_spec=pltpu.PrefetchScalar...  24 us
    ppermute x18, starting transfers between devices, over_dp(): return lax.ppermute(value, 'dp', swap_perm(shards_dp, flip))  13.1 us
    pallas_call x2, Pallas kernels, ff_grad(): pl.pallas_call(ff_keep_kernel, grid_spec=pltpu.PrefetchScalarGridSpec(num...  11.2 us
    pallas_call x3, Pallas kernels, add_x(): pl.pallas_call(partial(add_x_kernel, tailed), grid_spec=pltpu.PrefetchSca...  10.1 us
    pallas_call x2, Pallas kernels, ff_grad(): pl.pallas_call(ff_send_kernel, grid_spec=pltpu.PrefetchScalarGridSpec(num...  10 us
  transfers between devices with their start and end apart: 26, of which 10 were waited for; matrix products, arithmetic and copies ran while one was open for 2% of the time, Pallas kernels for 57%

profile of v4, /device:TPU:0, one launch (start us, length us, event | category | flops | bytes accessed | tf_op | source)
XLA Modules:
  0.0 221.7 jit_solution(10770984799700017892)
XLA Ops:
  1.9 3.0 %collective-permute-start = (bf16[768,384]{1,0:T(8,128)(2,1)S(1)}, bf16[768,384]{1,0:T(8,128)(2,1)}, u32[]{:S(2)}, u32[]{:S(2)}) collective-permute-start(bf16[768,384]{1,0:T(8,128)(2,1)S(1)} %constant_dynamic-slice_fusion.1), channel_id=1, source_target_pairs={{0,1},{1,0},{2,3},{3,2},{4,5},{5,4},{6,7},{7,6},{8,9},{9,8},{10,11... | collective-permute-start | bytes 1769480 | tf_op jit(solution)/shard_map/ppermute | solution.py:1029
  11.3 16.2 %attn_fwd.2 = (bf16[512,768]{1,0:T(8,128)(2,1)}, bf16[6,512,512]{2,1,0:T(8,128)(2,1)}, bf16[512,384]{1,0:T(8,128)(2,1)}, bf16[512,384]{1,0:T(8,128)(2,1)}, bf16[...) custom-call(s32[9]{0:T(128)} %stack.39.pick, ...), custom_call_target="tpu_custom_call" | custom-call | flops 4328521728 | bytes 10000000 | tf_op jit(solution)/shard_map/attn_fwd/pallas_call | solution.py:165
  27.5 3.6 %collective-permute-done.2.bi_there = bf16[1536]{0:T(1024)(128)(2,1)S(1)} collective-permute-done((bf16[1536]{0:T(1024)(128)(2,1)S(1)}, bf16[1536]{0:T(1024)(128)(2,1)S(1)}, u32[]{:S(2)}, u32[]{:S(2)}) %collective-permute-start.2) | collective-permute-done | bytes 3104 | tf_op jit(solution)/shard_map/ppermute | solution.py:1029
  36.4 16.2 %attn_fwd.3 = (bf16[512,768]{1,0:T(8,128)(2,1)}, bf16[6,512,512]{2,1,0:T(8,128)(2,1)}, bf16[512,384]{1,0:T(8,128)(2,1)}, bf16[512,384]{1,0:T(8,128)(2,1)}, bf16[...) custom-call(s32[9]{0:T(128)} %stack.39.pick, ...), custom_call_target="tpu_custom_call" | custom-call | flops 4328521728 | bytes 10000000 | tf_op jit(solution)/shard_map/attn_fwd/pallas_call | solution.py:165
  55.9 24.0 %feed_forward.1 = (bf16[512,768]{1,0:T(8,128)(2,1)}, bf16[512,768]{1,0:T(8,128)(2,1)}, bf16[2,2,384,512]{3,2,1,0:T(8,128)(2,1)}, bf16[2,4,512,768]{3,2,1,0:T(8,128)(2,1)}, f32[8,1536]{1,0:T(8,128)}) custom-call(s32[9]{0:T(128)} %stack.39.pick, bf16[1024,768]{1,0:T(8,128)(2,1)} %tok_ref.4, bf16[512,768]{1,0:T(8,128)(2,1)} %get-tuple-element.132.part_ref, ...), custom_call_target="tpu_custom_call" | custom-call | flops 9663676416 | bytes 22020096 | tf_op jit(solution)/shard_map/feed_forward/pallas_call | solution.py:569
  80.0 5.0 %ff_grad_send.2 = bf16[2,392,1536]{2,1,0:T(8,128)(2,1)} custom-call(s32[9]{0:T(128)} %stack.39.pick, bf16[2,2,384,512]{3,2,1,0:T(8,128)(2,1)} %get-tuple-element.141.lhs_ref, bf16[2,4,512,768]{3,2,1,0:T(8,128)(2,1)} %get-tuple-element.147.rhs_ref, f32[8,1536]{1,0:T(8,128)} %get-tuple-element.143.small_ref), custom_call_target="tpu_custom_call" | custom-call | flops 1207959552 | bytes 10000000 | tf_op jit(solution)/shard_map/ff_grad_send/pallas_call | solution.py:680
  85.1 5.0 %ff_grad_send.3 = bf16[2,392,1536]{2,1,0:T(8,128)(2,1)} custom-call(s32[9]{0:T(128)} %stack.39.pick, bf16[2,2,384,512]{3,2,1,0:T(8,128)(2,1)} %get-tuple-element.141.lhs_ref, bf16[2,4,512,768]{3,2,1,0:T(8,128)(2,1)} %get-tuple-element.147.rhs_ref, f32[8,1536]{1,0:T(8,128)} %get-tuple-element.143.small_ref), custom_call_target="tpu_custom_call" | custom-call | flops 1207959552 | bytes 10000000 | tf_op jit(solution)/shard_map/ff_grad_send/pallas_call | solution.py:680
  90.5 5.6 %ff_grad_keep.2 = (bf16[2,200,1536]{2,1,0:T(8,128)(2,1)}, bf16[2,192,1536]{2,1,0:T(8,128)(2,1)}, f32[8,1536]{1,0:T(8,128)}) custom-call(s32[9]{0:T(128)} %stack.39.pick, bf16[2,2,384,512]{3,2,1,0:T(8,128)(2,1)} %get-tuple-element.141.lhs_ref, bf16[2,4,512,768]{3,2,1,0:T(8,128)(2,1)} %get-tuple-element.147.rhs_ref, ...), custom_call_target="tpu_custom_call" | custom-call | flops 1207959552 | bytes 10000000 | tf_op jit(solution)/shard_map/ff_grad_keep/pallas_call | solution.py:693
  97.2 5.5 %ff_grad_keep.3 = (bf16[2,200,1536]{2,1,0:T(8,128)(2,1)}, bf16[2,192,1536]{2,1,0:T(8,128)(2,1)}, f32[8,1536]{1,0:T(8,128)}) custom-call(s32[9]{0:T(128)} %stack.39.pick, bf16[2,2,384,512]{3,2,1,0:T(8,128)(2,1)} %get-tuple-element.141.lhs_ref, bf16[2,4,512,768]{3,2,1,0:T(8,128)(2,1)} %get-tuple-element.147.rhs_ref, ...), custom_call_target="tpu_custom_call" | custom-call | flops 1207959552 | bytes 10000000 | tf_op jit(solution)/shard_map/ff_grad_keep/pallas_call | solution.py:693
  102.8 20.6 %attn_bwd.2 = (bf16[2,384,1920]{2,1,0:T(8,128)(2,1)}, f32[1,1920]{1,0:T(1,128)}, bf16[512,768]{1,0:T(8,128)(2,1)}) custom-call(s32[9]{0:T(128)} %stack.39.pick, bf16[512,768]{1,0:T(8,128)(2,1)} %get-tuple-element.213.refs_0_.df_ref, bf16[2,384,512]{2,1,0:T(8,128)(2,1)} %get-tuple-element.151.refs_1_, bf16[512,384]{1,0:T(8,128)(2,1)} %get-tuple-element.152.refs_2_, ...), custom_call_target="tpu_custom_call" | custom-call | flops 6543114240 | bytes 14000000 | tf_op jit(solution)/shard_map/attn_bwd/pallas_call | solution.py:341
  123.4 2.3 %collective-permute-done.12.got_ref = bf16[2,200,1536]{2,1,0:T(8,128)(2,1)} collective-permute-done((bf16[2,200,1536]{2,1,0:T(8,128)(2,1)}, bf16[2,200,1536]{2,1,0:T(8,128)(2,1)}, u32[]{:S(2)}, u32[]{:S(2)}) %collective-permute-start.12) | collective-permute-done | bytes 1228832 | tf_op jit(solution)/shard_map/ppermute | solution.py:1032
  126.1 3.6 %add_x.3 = (bf16[2,96,1536]{2,1,0:T(8,128)(2,1)}, bf16[2,104,1536]{2,1,0:T(8,128)(2,1)}, f32[8,1536]{1,0:T(8,128)}) custom-call(s32[9]{0:T(128)} %stack.39.pick, bf16[2,192,1536]{2,1,0:T(8,128)(2,1)} %get-tuple-element.161.keep_ref, bf16[2,200,1536]{2,1,0:T(8,128)(2,1)} %collective-permute-done.12.got_ref, f32[8,1536]{1,0:T(8,128)} %get-tuple-element.164.small_ref), custom_call_target="tpu_custom_call" | custom-call | flops 589824 | bytes 3538944 | tf_op jit(solution)/shard_map/add_x/pallas_call | solution.py:796
  130.6 21.7 %attn_bwd.3 = (bf16[392,1920]{1,0:T(8,128)(2,1)}, bf16[384,1920]{1,0:T(8,128)(2,1)}, f32[1,1920]{1,0:T(1,128)}, bf16[1024,768]{1,0:T(8,128)(2,1)}) custom-call(s32[9]{0:T(128)} %stack.39.pick, bf16[512,768]{1,0:T(8,128)(2,1)} %collective-permute-done.13.refs_0_.df_ref, bf16[2,384,512]{2,1,0:T(8,128)(2,1)} %get-tuple-element.167.refs_1_, ...), custom_call_target="tpu_custom_call" | custom-call | flops 6543114240 | bytes 14000000 | tf_op jit(solution)/shard_map/attn_bwd/pallas_call | solution.py:341
  156.6 2.6 %collective-permute-start.17 = (bf16[2,56,1536]{2,1,0:T(8,128)(2,1)}, bf16[2,56,1536]{2,1,0:T(8,128)(2,1)}, u32[]{:S(2)}, u32[]{:S(2)}) collective-permute-start(bf16[2,56,1536]{2,1,0:T(8,128)(2,1)} %get-tuple-element.189), channel_id=1, source_target_pairs={{0,16},{2,18},{4,20},{6,22},{8,24},{10,26},{12,28},{14,30},{16,0},... | collective-permute-start | bytes 1032200 | tf_op jit(solution)/shard_map/ppermute | solution.py:1032
  159.1 3.5 %add_x.4 = (bf16[2,96,1536]{2,1,0:T(8,128)(2,1)}, bf16[2,96,1536]{2,1,0:T(8,128)(2,1)}) custom-call(s32[9]{0:T(128)} %stack.39.pick, bf16[2,192,1536]{2,1,0:T(8,128)(2,1)} %get-tuple-element.190.keep_ref, bf16[2,200,1536]{2,1,0:T(8,128)(2,1)} %collective-permute-done.14.got_ref, f32[8,1536]{1,0:T(8,128)} %get-tuple-element.191.small_ref), custom_call_target="tpu_custom_call" | custom-call | flops 589824 | bytes 3538944 | tf_op jit(solution)/shard_map/add_x/pallas_call | solution.py:796
  163.9 4.2 %attn_split.1 = (bf16[1,200,1920]{2,1,0:T(8,128)(2,1)}, bf16[1,192,1920]{2,1,0:T(8,128)(2,1)}, f32[8,1920]{1,0:T(8,128)}) custom-call(s32[9]{0:T(128)} %stack.39.pick, bf16[384,1920]{1,0:T(8,128)(2,1)} %get-tuple-element.194.kept_ref, bf16[392,1920]{1,0:T(8,128)(2,1)} %collective-permute-done.19.got_ref, f32[1,1920]{1,0:T(1,128)} %get-tuple-element.197.small_ref), custom_call_target="tpu_custom_call" | custom-call | flops 737280 | bytes 4423680 | tf_op jit(solution)/shard_map/attn_split/pallas_call | solution.py:740
  169.6 3.7 %place_grad.2.refs_0_ = f32[1024,768]{1,0:T(8,128)} custom-call(s32[9]{0:T(128)} %stack.39.pick, bf16[512,768]{1,0:T(8,128)(2,1)} %collective-permute-done.13.refs_0_.df_ref, bf16[1024,768]{1,0:T(8,128)(2,1)} %get-tuple-element.181.a_ref, bf16[512,768]{1,0:T(8,128)(2,1)} %collective-permute-done.16.b_ref), custom_call_target="tpu_custom_call" | custom-call | flops 40000000000 | bytes 3932160 | tf_op jit(solution)/shard_map/place_grad/pallas_call | solution.py:928
  173.3 14.0 %collective-permute-done.20.got_ref = bf16[1,200,1920]{2,1,0:T(8,128)(2,1)S(1)} collective-permute-done((bf16[1,200,1920]{2,1,0:T(8,128)(2,1)}, bf16[1,200,1920]{2,1,0:T(8,128)(2,1)S(1)}, u32[]{:S(2)}, u32[]{:S(2)}) %collective-permute-start.20) | collective-permute-done | bytes 768032 | tf_op jit(solution)/shard_map/ppermute | solution.py:1032
  188.1 3.0 %add_x.5 = (bf16[1,96,1920]{2,1,0:T(8,128)(2,1)}, bf16[1,104,1920]{2,1,0:T(8,128)(2,1)}, f32[8,1920]{1,0:T(8,128)}) custom-call(s32[9]{0:T(128)} %stack.39.pick, bf16[1,192,1920]{2,1,0:T(8,128)(2,1)} %get-tuple-element.201.keep_ref, bf16[1,200,1920]{2,1,0:T(8,128)(2,1)} %copy-done, f32[8,1920]{1,0:T(8,128)} %get-tuple-element.202.small_ref), custom_call_target="tpu_custom_call" | custom-call | flops 368640 | bytes 2211840 | tf_op jit(solution)/shard_map/add_x/pallas_call | solution.py:796
  196.8 3.7 %place_grad.3 = f32[1024,768]{1,0:T(8,128)} custom-call(s32[9]{0:T(128)} %stack.39.pick, bf16[512,768]{1,0:T(8,128)(2,1)} %get-tuple-element.213.refs_0_.df_ref, bf16[512,768]{1,0:T(8,128)(2,1)} %get-tuple-element.180.a_ref, bf16[1024,768]{1,0:T(8,128)(2,1)} %collective-permute-done.21.b_ref, ...), custom_call_target="tpu_custom_call", output_to_operand_aliasing={{}: (4, {})} | custom-call | flops 40000000000 | bytes 3932160 | tf_op jit(solution)/shard_map/place_grad/pallas_call | solution.py:928
  200.4 6.2 %collective-permute-done.22.got_ref = bf16[1,104,1920]{2,1,0:T(8,128)(2,1)} collective-permute-done((bf16[1,104,1920]{2,1,0:T(8,128)(2,1)}, bf16[1,104,1920]{2,1,0:T(8,128)(2,1)}, u32[]{:S(2)}, u32[]{:S(2)}) %collective-permute-start.22) | collective-permute-done | bytes 399392 | tf_op jit(solution)/shard_map/ppermute | solution.py:1032
  210.2 2.7 %ff_last.1 = (f32[48,1536]{1,0:T(8,128)}, f32[48,1536]{1,0:T(8,128)}, f32[768]{0:T(1024)}, f32[768]{0:T(1024)}, f32[768]{0:T(1024)}, /*index=5*/f32[768]{0:T(102...) custom-call(s32[9]{0:T(128)} %stack.39.pick, bf16[2,48,1536]{2,1,0:T(8,128)(2,1)} %get-tuple-element.218.own, ...), custom_call_target="tpu_custom_call" | custom-call | flops 1720320 | bytes 3440640 | tf_op jit(solution)/shard_map/ff_last/pallas_call | solution.py:881
  213.0 3.3 %place_output.1 = bf16[1024,768]{1,0:T(8,128)(2,1)} custom-call(s32[9]{0:T(128)} %stack.39.pick, bf16[512,768]{1,0:T(8,128)(2,1)} %get-tuple-element.221.refs_16_.a_ref, bf16[1024,768]{1,0:T(8,128)(2,1)} %collective-permute-done.21.b_ref), custom_call_target="tpu_custom_call" | custom-call | flops 393216 | bytes 3145728 | tf_op jit(solution)/shard_map/place_output/pallas_call | solution.py:955
  216.2 3.0 %collective-permute-done.25.got = bf16[1,56,1920]{2,1,0:T(8,128)(2,1)S(1)} collective-permute-done((bf16[1,56,1920]{2,1,0:T(8,128)(2,1)}, bf16[1,56,1920]{2,1,0:T(8,128)(2,1)S(1)}, u32[]{:S(2)}, u32[]{:S(2)}) %collective-permute-start.25) | collective-permute-done | bytes 215072 | tf_op jit(solution)/shard_map/ppermute | solution.py:1032
  (79 shorter events, 38.7 us)
Async XLA Ops:
  1.9 29.2 %collective-permute-start = (bf16[768,384]{1,0:T(8,128)(2,1)S(1)}, bf16[768,384]{1,0:T(8,128)(2,1)}, u32[]{:S(2)}, u32[]{:S(2)}) collective-permute-start(bf16[768,384]{1,0:T(8,128)(2,1)S(1)} %constant_dynamic-slice_fusion.1), channel_id=1, source_target_pairs={{0,1},{1,0},{2,3},{3,2},{4,5},{5,4},{6,7},{7,6},{8,9},{9,8},{10,11... | collective-permute-start | bytes 1769480 | tf_op jit(solution)/shard_map/ppermute | solution.py:1029
  6.8 24.2 %collective-permute-start.1 = (bf16[384,768]{1,0:T(8,128)(2,1)}, bf16[384,768]{1,0:T(8,128)(2,1)}, u32[]{:S(2)}, u32[]{:S(2)}) collective-permute-start(bf16[384,768]{1,0:T(8,128)(2,1)} %constant_dynamic-slice_fusion), channel_id=1, source_target_pairs={{0,1},{1,0},{2,3},{3,2},{4,5},{5,4},{6,7},{7,6},{8,9},{9,8},{10,11... | collective-permute-start | bytes 1769480 | tf_op jit(solution)/shard_map/ppermute | solution.py:1029
  6.9 24.1 %collective-permute-start.2 = (bf16[1536]{0:T(1024)(128)(2,1)S(1)}, bf16[1536]{0:T(1024)(128)(2,1)S(1)}, u32[]{:S(2)}, u32[]{:S(2)}) collective-permute-start(bf16[1536]{0:T(1024)(128)(2,1)S(1)} %copy-done.8), channel_id=1, source_target_pairs={{0,1},{1,0},{2,3},{3,2},{4,5},{5,4},{6,7},{7,6},{8,9},{9,8},{10,11... | collective-permute-start | bytes 9224 | tf_op jit(solution)/shard_map/ppermute | solution.py:1029
  31.0 21.6 %collective-permute-start.4 = (bf16[768,384]{1,0:T(8,128)(2,1)}, bf16[768,384]{1,0:T(8,128)(2,1)}, u32[]{:S(2)}, u32[]{:S(2)}) collective-permute-start(bf16[768,384]{1,0:T(8,128)(2,1)} %collective-permute-done.wi0), channel_id=1, source_target_pairs={{0,2},{2,0},{4,6},{6,4},{8,10},{10,8},{12,14},{14,12},{16,18},{18,... | collective-permute-start | bytes 1769480 | tf_op jit(solution)/shard_map/ppermute | solution.py:1032
  31.1 21.5 %collective-permute-start.5 = (bf16[384,768]{1,0:T(8,128)(2,1)}, bf16[384,768]{1,0:T(8,128)(2,1)}, u32[]{:S(2)}, u32[]{:S(2)}) collective-permute-start(bf16[384,768]{1,0:T(8,128)(2,1)} %collective-permute-done.1.wb0), channel_id=1, source_target_pairs={{0,2},{2,0},{4,6},{6,4},{8,10},{10,8},{12,14},{14,12},{16,18},{18,... | collective-permute-start | bytes 1769480 | tf_op jit(solution)/shard_map/ppermute | solution.py:1032
  31.6 21.0 %collective-permute-start.6 = (bf16[768,384]{1,0:T(8,128)(2,1)}, bf16[768,384]{1,0:T(8,128)(2,1)}, u32[]{:S(2)}, u32[]{:S(2)}) collective-permute-start(bf16[768,384]{1,0:T(8,128)(2,1)} %collective-permute-done.wi0), channel_id=1, source_target_pairs={{0,4},{2,6},{4,0},{6,2},{8,12},{10,14},{12,8},{14,10},{16,20},{18,... | collective-permute-start | bytes 1769480 | tf_op jit(solution)/shard_map/ppermute | solution.py:1032
  33.3 19.3 %collective-permute-start.7 = (bf16[384,768]{1,0:T(8,128)(2,1)}, bf16[384,768]{1,0:T(8,128)(2,1)}, u32[]{:S(2)}, u32[]{:S(2)}) collective-permute-start(bf16[384,768]{1,0:T(8,128)(2,1)} %collective-permute-done.1.wb0), channel_id=1, source_target_pairs={{0,8},{2,10},{4,12},{6,14},{8,0},{10,2},{12,4},{14,6},{16,24},{18,... | collective-permute-start | bytes 1769480 | tf_op jit(solution)/shard_map/ppermute | solution.py:1032
  34.9 19.2 %collective-permute-start.3 = (bf16[512,768]{1,0:T(8,128)(2,1)}, bf16[512,768]{1,0:T(8,128)(2,1)S(1)}, u32[]{:S(2)}, u32[]{:S(2)}) collective-permute-start(bf16[512,768]{1,0:T(8,128)(2,1)} %get-tuple-element.129), channel_id=1, source_target_pairs={{0,1},{1,0},{2,3},{3,2},{4,5},{5,4},{6,7},{7,6},{8,9},{9,8},{10,11... | collective-permute-start | bytes 2359304 | tf_op jit(solution)/shard_map/ppermute | solution.py:1029
  85.0 5.5 %collective-permute-start.10 = (bf16[2,392,1536]{2,1,0:T(8,128)(2,1)}, bf16[2,392,1536]{2,1,0:T(8,128)(2,1)}, u32[]{:S(2)}, u32[]{:S(2)}) collective-permute-start(bf16[2,392,1536]{2,1,0:T(8,128)(2,1)} %ff_grad_send.2), channel_id=1, source_target_pairs={{0,2},{2,0},{4,6},{6,4},{8,10},{10,8},{12,14},{14,12},{16,18},{18,... | collective-permute-start | bytes 7225352 | tf_op jit(solution)/shard_map/ppermute | solution.py:1032
  90.1 7.1 %collective-permute-start.11 = (bf16[2,392,1536]{2,1,0:T(8,128)(2,1)}, bf16[2,392,1536]{2,1,0:T(8,128)(2,1)}, u32[]{:S(2)}, u32[]{:S(2)}) collective-permute-start(bf16[2,392,1536]{2,1,0:T(8,128)(2,1)} %ff_grad_send.3), channel_id=1, source_target_pairs={{0,2},{2,0},{4,6},{6,4},{8,10},{10,8},{12,14},{14,12},{16,18},{18,... | collective-permute-start | bytes 7225352 | tf_op jit(solution)/shard_map/ppermute | solution.py:1032
  96.1 29.5 %collective-permute-start.12 = (bf16[2,200,1536]{2,1,0:T(8,128)(2,1)}, bf16[2,200,1536]{2,1,0:T(8,128)(2,1)}, u32[]{:S(2)}, u32[]{:S(2)}) collective-permute-start(bf16[2,200,1536]{2,1,0:T(8,128)(2,1)} %get-tuple-element.146), channel_id=1, source_target_pairs={{0,4},{2,6},{4,0},{6,2},{8,12},{10,14},{12,8},{14,10},{16,20},{18,... | collective-permute-start | bytes 3686408 | tf_op jit(solution)/shard_map/ppermute | solution.py:1032
  96.6 26.7 %collective-permute-start.13 = (bf16[512,768]{1,0:T(8,128)(2,1)S(1)}, bf16[512,768]{1,0:T(8,128)(2,1)}, u32[]{:S(2)}, u32[]{:S(2)}) collective-permute-start(bf16[512,768]{1,0:T(8,128)(2,1)S(1)} %copy-done.5), channel_id=1, source_target_pairs={{0,1},{1,0},{2,3},{3,2},{4,5},{5,4},{6,7},{7,6},{8,9},{9,8},{10,11... | collective-permute-start | bytes 2359304 | tf_op jit(solution)/shard_map/ppermute | solution.py:1029
  125.7 28.7 %collective-permute-start.14 = (bf16[2,200,1536]{2,1,0:T(8,128)(2,1)}, bf16[2,200,1536]{2,1,0:T(8,128)(2,1)}, u32[]{:S(2)}, u32[]{:S(2)}) collective-permute-start(bf16[2,200,1536]{2,1,0:T(8,128)(2,1)} %get-tuple-element.179), channel_id=1, source_target_pairs={{0,4},{2,6},{4,0},{6,2},{8,12},{10,14},{12,8},{14,10},{16,20},{18,... | collective-permute-start | bytes 3686408 | tf_op jit(solution)/shard_map/ppermute | solution.py:1032
  129.7 24.2 %collective-permute-start.16 = (bf16[512,768]{1,0:T(8,128)(2,1)S(1)}, bf16[512,768]{1,0:T(8,128)(2,1)}, u32[]{:S(2)}, u32[]{:S(2)}) collective-permute-start(bf16[512,768]{1,0:T(8,128)(2,1)S(1)} %copy-done.6), channel_id=1, source_target_pairs={{0,1},{1,0},{2,3},{3,2},{4,5},{5,4},{6,7},{7,6},{8,9},{9,8},{10,11... | collective-permute-start | bytes 2359304 | tf_op jit(solution)/shard_map/ppermute | solution.py:1029
  130.2 23.7 %collective-permute-start.15 = (bf16[2,104,1536]{2,1,0:T(8,128)(2,1)}, bf16[2,104,1536]{2,1,0:T(8,128)(2,1)}, u32[]{:S(2)}, u32[]{:S(2)}) collective-permute-start(bf16[2,104,1536]{2,1,0:T(8,128)(2,1)} %get-tuple-element.165), channel_id=1, source_target_pairs={{0,8},{2,10},{4,12},{6,14},{8,0},{10,2},{12,4},{14,6},{16,24},{18,... | collective-permute-start | bytes 1916936 | tf_op jit(solution)/shard_map/ppermute | solution.py:1032
  152.3 44.5 %collective-permute-start.21 = (bf16[1024,768]{1,0:T(8,128)(2,1)}, bf16[1024,768]{1,0:T(8,128)(2,1)}, u32[]{:S(2)}, u32[]{:S(2)}) collective-permute-start(bf16[1024,768]{1,0:T(8,128)(2,1)} %get-tuple-element.181.a_ref), channel_id=1, source_target_pairs={{0,1},{1,0},{2,3},{3,2},{4,5},{5,4},{6,7},{7,6},{8,9},{9,8},{10,11... | collective-permute-start | bytes 4718600 | tf_op jit(solution)/shard_map/ppermute | solution.py:1029
  154.4 9.5 %collective-permute-start.19 = (bf16[392,1920]{1,0:T(8,128)(2,1)}, bf16[392,1920]{1,0:T(8,128)(2,1)}, u32[]{:S(2)}, u32[]{:S(2)}) collective-permute-start(bf16[392,1920]{1,0:T(8,128)(2,1)} %get-tuple-element.195), channel_id=1, source_target_pairs={{0,2},{2,0},{4,6},{6,4},{8,10},{10,8},{12,14},{14,12},{16,18},{18,... | collective-permute-start | bytes 4515848 | tf_op jit(solution)/shard_map/ppermute | solution.py:1032
  156.6 35.4 %collective-permute-start.17 = (bf16[2,56,1536]{2,1,0:T(8,128)(2,1)}, bf16[2,56,1536]{2,1,0:T(8,128)(2,1)}, u32[]{:S(2)}, u32[]{:S(2)}) collective-permute-start(bf16[2,56,1536]{2,1,0:T(8,128)(2,1)} %get-tuple-element.189), channel_id=1, source_target_pairs={{0,16},{2,18},{4,20},{6,22},{8,24},{10,26},{12,28},{14,30},{16,0},... | collective-permute-start | bytes 1032200 | tf_op jit(solution)/shard_map/ppermute | solution.py:1032
  162.6 29.3 %collective-permute-start.18 = (bf16[2,96,1536]{2,1,0:T(8,128)(2,1)}, bf16[2,96,1536]{2,1,0:T(8,128)(2,1)}, u32[]{:S(2)}, u32[]{:S(2)}) collective-permute-start(bf16[2,96,1536]{2,1,0:T(8,128)(2,1)} %get-tuple-element.193), channel_id=1, source_target_pairs={{0,8},{2,10},{4,12},{6,14},{8,0},{10,2},{12,4},{14,6},{16,24},{18,... | collective-permute-start | bytes 1769480 | tf_op jit(solution)/shard_map/ppermute | solution.py:1032
  168.1 19.2 %collective-permute-start.20 = (bf16[1,200,1920]{2,1,0:T(8,128)(2,1)}, bf16[1,200,1920]{2,1,0:T(8,128)(2,1)S(1)}, u32[]{:S(2)}, u32[]{:S(2)}) collective-permute-start(bf16[1,200,1920]{2,1,0:T(8,128)(2,1)} %get-tuple-element.199), channel_id=1, source_target_pairs={{0,4},{2,6},{4,0},{6,2},{8,12},{10,14},{12,8},{14,10},{16,20},{18,... | collective-permute-start | bytes 2304008 | tf_op jit(solution)/shard_map/ppermute | solution.py:1032
  191.2 15.4 %collective-permute-start.22 = (bf16[1,104,1920]{2,1,0:T(8,128)(2,1)}, bf16[1,104,1920]{2,1,0:T(8,128)(2,1)}, u32[]{:S(2)}, u32[]{:S(2)}) collective-permute-start(bf16[1,104,1920]{2,1,0:T(8,128)(2,1)} %get-tuple-element.203), channel_id=1, source_target_pairs={{0,8},{2,10},{4,12},{6,14},{8,0},{10,2},{12,4},{14,6},{16,24},{18,... | collective-permute-start | bytes 1198088 | tf_op jit(solution)/shard_map/ppermute | solution.py:1032
  194.1 15.3 %collective-permute-start.23 = (bf16[2,48,1536]{2,1,0:T(8,128)(2,1)}, bf16[2,48,1536]{2,1,0:T(8,128)(2,1)S(1)}, u32[]{:S(2)}, u32[]{:S(2)}) collective-permute-start(bf16[2,48,1536]{2,1,0:T(8,128)(2,1)} %get-tuple-element.209), channel_id=1, source_target_pairs={{0,16},{2,18},{4,20},{6,22},{8,24},{10,26},{12,28},{14,30},{16,0},... | collective-permute-start | bytes 884744 | tf_op jit(solution)/shard_map/ppermute | solution.py:1032
  196.4 13.1 %collective-permute-start.24 = (bf16[2,56,1536]{2,1,0:T(8,128)(2,1)}, bf16[2,56,1536]{2,1,0:T(8,128)(2,1)S(1)}, u32[]{:S(2)}, u32[]{:S(2)}) collective-permute-start(bf16[2,56,1536]{2,1,0:T(8,128)(2,1)} %get-tuple-element.212), channel_id=1, source_target_pairs={{0,1},{1,0},{2,3},{3,2},{4,5},{5,4},{6,7},{7,6},{8,9},{9,8},{10,11... | collective-permute-start | bytes 1032200 | tf_op jit(solution)/shard_map/ppermute | solution.py:1029
  208.6 10.7 %collective-permute-start.25 = (bf16[1,56,1920]{2,1,0:T(8,128)(2,1)}, bf16[1,56,1920]{2,1,0:T(8,128)(2,1)S(1)}, u32[]{:S(2)}, u32[]{:S(2)}) collective-permute-start(bf16[1,56,1920]{2,1,0:T(8,128)(2,1)} %get-tuple-element.217), channel_id=1, source_target_pairs={{0,16},{2,18},{4,20},{6,22},{8,24},{10,26},{12,28},{14,30},{16,0},... | collective-permute-start | bytes 645128 | tf_op jit(solution)/shard_map/ppermute | solution.py:1032
  (12 other events, 59.4 us)
